TPU v7x, 256 devices: a whole 4x4x8 slice. The times are simulated.
256 devices in a mesh: dp: 64 (over z, y, core), mp: 4 (over x).
Axes of the slice: x: 4, y: 4, z: 8, core: 2. Of those that a mesh axis runs over, the one named last changes fastest.
Arguments:
- tokens: bfloat16 [49152, 768], P(('dp', 'mp')), may hold values from -6 to 6
- obs_mask: int32 [768, 64], P(('dp', 'mp')), may hold values 0 or 1
- norm_gains: float32 [5, 768], replicated, may hold values from 0.1 to 1.9
- attn_in: bfloat16 [2, 3, 768, 768], P(None, None, 'dp', 'mp'), may hold values from -0.21875 to 0.21875
- attn_out: bfloat16 [2, 768, 768], P(None, 'mp', 'dp'), may hold values from -0.21875 to 0.21875
- mlp_in: bfloat16 [2, 768, 3072], P(None, 'dp', 'mp'), may hold values from -0.21875 to 0.21875
- mlp_out: bfloat16 [2, 3072, 768], P(None, 'mp', 'dp'), may hold values from -0.109375 to 0.109375
- embodiment: int32 [768, 1], P('dp'), may hold values from 0 to 24; in each aligned block of 12 rows (0 to 11, 12 to 23, ...) no two rows name the same one
- levels: int32 [768, 2], P('dp'), may hold values from 0 to 19
- actions: bfloat16 [768, 2, 56], P('dp'), may hold values from -1 to 1
- noise: bfloat16 [768, 2, 56], P('dp'), may hold values from -5 to 5
- action_dims: int32 [25], replicated, may hold values from 7 to 14
- head_read: bfloat16 [64, 768, 256], P('dp'), may hold values from -0.21875 to 0.21875
- head_act: bfloat16 [64, 56, 256], P('dp'), may hold values from -0.75 to 0.75
- time_table: bfloat16 [64, 20, 256], P('dp'), may hold values from -5 to 5
- block_in: bfloat16 [64, 256, 256], P('dp'), may hold values from -0.375 to 0.375
- block_out: bfloat16 [64, 256, 256], P('dp'), may hold values from -0.375 to 0.375
- head_out: bfloat16 [64, 256, 56], P('dp'), may hold values from -0.375 to 0.375
Outputs:
- readout_grad: bfloat16 [768, 2, 768], P(('dp', 'mp'))
- grad_read: float32 [64, 768, 256], P('dp', 'mp')
- grad_act: float32 [64, 56, 256], P('dp')
- grad_time: float32 [64, 20, 256], P('dp')
- grad_block_in: float32 [64, 256, 256], P('dp')
- grad_block_out: float32 [64, 256, 256], P('dp')
- grad_head_out: float32 [64, 256, 56], P('dp')
Inputs may be any that keep to these rules, and one draw needn't show every extreme that they name: Within each aligned block of 12 samples (those of one dp index) no embodiment appears twice; every embodiment appears in some block.
All inputs are finite; a program needn't handle non-finite values. No bound on the sum of `obs_mask` on one device may be relied on, other than what follows from the above.
Results may differ from a plain program's by a relative error of at most 0.024.
Values may be sent and summed in bfloat16 or wider, within the bound.
No kernel may reach another device: no remote copies, remote signals or barrier semaphores. Data moves between devices by JAX's collectives and lax.ppermute only.
A program may use at most 64 MiB of HBM per device.

v0:
```python
import math

import jax
import jax.numpy as jnp
from jax import lax
from jax.sharding import PartitionSpec as P

D = 768
HDIM = 64
EMB = 25
READ = 2
LEVELS = 20
ADIM_MAX = 14
ACT = 56


norm_eps = 1e-05


def sent_to_all(x, axis):
    copies = jnp.broadcast_to(x, (lax.axis_size(axis), *x.shape))
    return lax.all_to_all(copies, axis, split_axis=0, concat_axis=0, tiled=True)


def in_order(pieces, dim):
    lengths = list(pieces.shape[1:])
    lengths[dim] *= pieces.shape[0]
    return jnp.moveaxis(pieces, 0, dim).reshape(lengths)


def collect(x, axis, dim):
    pieces = sent_to_all(x, axis)
    return in_order(pieces, dim)


def in_blocks(x, dim, peers):
    lengths = x.shape
    pieces = x.reshape(*lengths[:dim], peers, lengths[dim] // peers, *lengths[dim + 1 :])
    return jnp.moveaxis(pieces, dim, 0)


def summed_on_arrival(x, axis, dim):
    pieces = in_blocks(x, dim, lax.axis_size(axis))
    arrived = lax.all_to_all(pieces, axis, split_axis=0, concat_axis=0, tiled=True)
    return arrived.astype(jnp.float32).sum(axis=0)


def gather_turned(arrays, axis, dims):
    turned = [jnp.moveaxis(a, dim, 0) for a, dim in zip(arrays, dims)]
    widths = [t[0].size for t in turned]
    both = jnp.concatenate([t.reshape(-1, w) for t, w in zip(turned, widths)], axis=1)
    whole = lax.all_gather(both, axis, axis=0, tiled=True)
    pieces = jnp.split(whole, [sum(widths[:k]) for k in range(1, len(widths))], axis=1)
    return tuple(
        (
            jnp.moveaxis(b.reshape(-1, *t.shape[1:]), 0, dim)
            for b, t, dim in zip(pieces, turned, dims)
        )
    )


def in_one_piece(arrays, axis, split_dim, concat_dim, along):
    both = jnp.concatenate(arrays, axis=along)
    whole, at, done = (
        lax.all_to_all(both, axis, split_axis=split_dim, concat_axis=concat_dim, tiled=True),
        0,
        [],
    )
    for a in arrays:
        done.append(lax.slice_in_dim(whole, at, at + a.shape[along], axis=along))
        at += a.shape[along]
    return tuple(done)


def of_everyone(x, axis):
    return sent_to_all(x, axis).astype(jnp.float32).sum(axis=0)


def normalize(values, scale_gain):
    center = values - jnp.mean(values, axis=-1, keepdims=True)
    spread = jnp.mean(center * center, axis=-1, keepdims=True)
    return center * lax.rsqrt(spread + norm_eps) * scale_gain


def allowed_keys(observed):
    length = observed.shape[1]
    position = jnp.arange(length)
    visible = (observed == 1) & (position < length - READ)[None, :]
    itself = position[:, None] == position[None, :]
    return visible[:, None, :] | itself[None, :, :]


def attend(queries, key_rows, value_rows, allowed):
    scores = jnp.einsum(
        "sqhd,skhd->shqk", queries, key_rows, preferred_element_type=jnp.float32
    ) * HDIM ** (-0.5)
    weights = jnp.where(allowed[:, None, :, :], jnp.exp(scores), 0.0)
    shares = (weights / jnp.sum(weights, axis=-1, keepdims=True)).astype(jnp.bfloat16)
    context = jnp.einsum("shqk,skhd->sqhd", shares, value_rows, preferred_element_type=jnp.float32)
    return context.astype(jnp.bfloat16)


def plan():
    steps_up = (jnp.arange(LEVELS, dtype=jnp.float32) + 1.0) / LEVELS
    anchor = math.cos(0.008 / 1.008 * math.pi / 2) ** 2
    return jnp.cos((steps_up + 0.008) / 1.008 * (math.pi / 2)) ** 2 / anchor


def noisy_pair(level_ids, clean, noise_draw, table):
    picked = (level_ids[..., None] == jnp.arange(LEVELS)).astype(jnp.float32)
    kept = jnp.sum(picked * table, axis=-1)[..., None]
    mixed = jnp.sqrt(kept) * clean.astype(jnp.float32) + jnp.sqrt(1.0 - kept) * noise_draw.astype(
        jnp.float32
    )
    return mixed.astype(jnp.bfloat16)


def tail(first, target, weight_mask, inner_weight, outer_weight, final_weight):
    active = jax.nn.silu(first).astype(jnp.bfloat16)
    inner = jnp.dot(active, inner_weight, preferred_element_type=jnp.float32)
    second = jax.nn.silu(inner).astype(jnp.bfloat16)
    hidden = first + jnp.dot(second, outer_weight, preferred_element_type=jnp.float32)
    third = jax.nn.silu(hidden).astype(jnp.bfloat16)
    predicted = jnp.dot(third, final_weight, preferred_element_type=jnp.float32)
    differ = predicted - target
    return 0.5 * jnp.sum(weight_mask * differ * differ)


def gather_rows(normed, observed):
    return (collect(normed, "mp", 0), collect(observed, "mp", 0))


def reduce_rows(partial_value):
    return summed_on_arrival(partial_value.astype(jnp.bfloat16), "mp", 0)


def head_grads(first, inner_weight, outer_weight, final_weight, target, weight_mask):

    def head_loss(first_in, inner_in, outer_in, final_in):
        return tail(first_in, target, weight_mask, inner_in, outer_in, final_in)

    loss_value, pullback = jax.vjp(head_loss, first, inner_weight, outer_weight, final_weight)
    return pullback(jnp.ones((), jnp.float32))


def on_device(
    tokens,
    obs_mask,
    norm_gains,
    attn_in,
    attn_out,
    mlp_in,
    mlp_out,
    embodiment,
    levels,
    actions,
    noise,
    action_dims,
    head_read,
    head_act,
    time_table,
    block_in,
    block_out,
    head_out,
):
    group_width = attn_in.shape[3]
    heads_local = group_width // HDIM
    samples_local = obs_mask.shape[0]
    length = obs_mask.shape[1]
    layer_count = attn_in.shape[0]
    residual = tokens.astype(jnp.float32)
    for layer_index in range(layer_count):
        normed = normalize(residual, norm_gains[2 * layer_index]).astype(jnp.bfloat16)
        gathered, mask_group = gather_rows(normed, obs_mask)
        samples_group = mask_group.shape[0]
        qkv_weight, out_weight, up_weight, down_weight = gather_turned(
            (
                attn_in[layer_index],
                attn_out[layer_index],
                mlp_in[layer_index],
                mlp_out[layer_index],
            ),
            "dp",
            (1, 1, 0, 1),
        )
        projected = jnp.einsum(
            "td,jdc->jtc", gathered, qkv_weight, preferred_element_type=jnp.float32
        )
        projected = projected.astype(jnp.bfloat16).reshape(
            3, samples_group, length, heads_local, HDIM
        )
        context = attend(
            projected[0], projected[1], projected[2], allowed_keys(mask_group)
        ).reshape(-1, group_width)
        partial_value = jnp.dot(context, out_weight, preferred_element_type=jnp.float32)
        residual = residual + reduce_rows(partial_value)
        normed = normalize(residual, norm_gains[2 * layer_index + 1]).astype(jnp.bfloat16)
        gathered, mask_group = gather_rows(normed, obs_mask)
        raised = jnp.dot(gathered, up_weight, preferred_element_type=jnp.float32)
        hidden = jax.nn.gelu(raised, approximate=True).astype(jnp.bfloat16)
        partial_value = jnp.dot(hidden, down_weight, preferred_element_type=jnp.float32)
        residual = residual + reduce_rows(partial_value)
    ending = residual.reshape(samples_local, length, D)[:, length - READ :, :]
    readouts = normalize(ending, norm_gains[2 * layer_count]).astype(jnp.bfloat16)
    table = plan()
    heads_dev = head_read.shape[0]
    peers = lax.axis_size("dp")
    slot_count = heads_dev * peers
    my_model = lax.axis_index("mp")
    my_owner = lax.axis_index("dp")
    features = lax.all_to_all(readouts, "mp", split_axis=2, concat_axis=0, tiled=True)
    owners = embodiment[:, 0]
    feature_width = features.shape[2]
    paired = jnp.concatenate([noisy_pair(levels, actions, noise, table), noise], axis=-1)
    send_features = (
        jnp.zeros((slot_count, READ, feature_width), jnp.bfloat16).at[owners].set(features)
    )
    send_paired = jnp.zeros((slot_count, READ, 2 * ACT), jnp.bfloat16).at[owners].set(paired)
    send_levels = jnp.full((slot_count, READ), -1, jnp.int32).at[owners].set(levels)
    got_features, got_paired, got_levels = (
        *in_one_piece((send_features, send_paired), "dp", 0, 0, 2),
        lax.all_to_all(send_levels, "dp", split_axis=0, concat_axis=0, tiled=True),
    )

    def by_head(values):
        trailing = values.shape[2:]
        values = values.reshape((peers, heads_dev, READ) + trailing)
        values = jnp.moveaxis(values, 1, 0)
        return values.reshape((heads_dev, peers * READ) + trailing)

    head_features = by_head(got_features)
    head_paired = by_head(got_paired)
    head_levels = by_head(got_levels)
    head_noisy = head_paired[..., :ACT]
    head_target = head_paired[..., ACT:].astype(jnp.float32)
    head_onehot = (head_levels[..., None] == jnp.arange(LEVELS)).astype(jnp.bfloat16)
    slot_ids = my_owner * heads_dev + jnp.arange(heads_dev)
    dims_here = jnp.sum(
        jnp.where(jnp.arange(EMB)[None, :] == slot_ids[:, None], action_dims[None, :], 0), axis=1
    )
    column = jnp.arange(ACT) % ADIM_MAX
    weight_mask = (head_levels >= 0).astype(jnp.float32)[..., None] * (
        column[None, None, :] < dims_here[:, None, None]
    ).astype(jnp.float32)
    others = jnp.einsum("hna,hac->hnc", head_noisy, head_act, preferred_element_type=jnp.float32)
    others = others + jnp.einsum(
        "hnl,hlc->hnc", head_onehot, time_table, preferred_element_type=jnp.float32
    )
    read_weight = lax.dynamic_slice_in_dim(head_read, my_model * feature_width, feature_width, 1)
    first = (
        of_everyone(
            jnp.einsum(
                "hnd,hdc->hnc", head_features, read_weight, preferred_element_type=jnp.float32
            ).astype(jnp.bfloat16),
            "mp",
        ).astype(jnp.float32)
        + others
    )
    grad_first, grad_inner, grad_outer, grad_final = jax.vmap(head_grads)(
        first,
        block_in.astype(jnp.float32),
        block_out.astype(jnp.float32),
        head_out.astype(jnp.float32),
        head_target,
        weight_mask,
    )
    grad_bf = grad_first.astype(jnp.bfloat16)
    grad_readin = jnp.einsum(
        "hnd,hnc->hdc", head_features, grad_bf, preferred_element_type=jnp.float32
    )
    grad_actin = jnp.einsum("hna,hnc->hac", head_noisy, grad_bf, preferred_element_type=jnp.float32)
    grad_timein = jnp.einsum(
        "hnl,hnc->hlc", head_onehot, grad_bf, preferred_element_type=jnp.float32
    )
    backward = jnp.einsum(
        "hnc,hdc->hnd", grad_bf, read_weight, preferred_element_type=jnp.float32
    ).astype(jnp.bfloat16)
    backward = jnp.moveaxis(backward.reshape(heads_dev, peers, READ, feature_width), 0, 1).reshape(
        peers, heads_dev * READ, feature_width
    )
    arrived = lax.all_to_all(backward, "dp", split_axis=0, concat_axis=0, tiled=True)
    arrived = arrived[owners]
    arrived = lax.all_to_all(arrived, "mp", split_axis=0, concat_axis=2, tiled=True)
    return (arrived, grad_readin, grad_actin, grad_timein, grad_inner, grad_outer, grad_final)


def solution(mesh):
    placed = (
        P(("dp", "mp"), None),
        P(("dp", "mp"), None),
        P(),
        P(None, None, "dp", "mp"),
        P(None, "mp", "dp"),
        P(None, "dp", "mp"),
        P(None, "mp", "dp"),
        P("dp", None),
        P("dp", None),
        P("dp", None, None),
        P("dp", None, None),
        P(),
        P("dp", None, None),
        P("dp", None, None),
        P("dp", None, None),
        P("dp", None, None),
        P("dp", None, None),
        P("dp", None, None),
    )
    return jax.shard_map(
        on_device,
        mesh=mesh,
        in_specs=placed,
        out_specs=(
            P(("dp", "mp"), None, None),
            P("dp", "mp", None),
            P("dp", None, None),
            P("dp", None, None),
            P("dp", None, None),
            P("dp", None, None),
            P("dp", None, None),
        ),
        check_vma=False,
    )
```

profile of v0, /device:TPU:1, one launch (start us, length us, event | category | flops | bytes accessed | tf_op | source)
XLA Modules:
  0.0 352.7 jit_solution(9556182351987897950)
XLA Ops:
  12.4 4.8 %all-to-all-start.2 = ((s32[4,1,192]{2,1,0:T(1,128)}), s32[4,1,192]{2,1,0:T(1,128)S(1)}, u32[]{:S(2)}, u32[]{:S(2)}) async-start(s32[4,1,192]{2,1,0:T(1,128)} %reshape.553), calls=%async_computation.2 | async-start | bytes 8192 | tf_op jit(solution)/shard_map/all_to_all | solution.py:22
  18.8 2.6 all-to-all-done.2
  21.4 1.1 broadcast_in_dim.42
  22.6 3.5 %all-to-all-start.1 = ((bf16[4,192,768]{2,1,0:T(8,128)(2,1)}), bf16[4,192,768]{2,1,0:T(8,128)(2,1)S(1)}, u32[]{:S(2)}, u32[]{:S(2)}) async-start(bf16[4,192,768]{2,1,0:T(8,128)(2,1)} %broadcast_in_dim.42), calls=%async_computation.1 | async-start | bytes 2359296 | tf_op jit(solution)/shard_map/all_to_all | solution.py:22
  27.6 67.6 %all-gather.5.cloned.1.call-done = bf16[64,12,2304]{2,1,0:T(8,128)(2,1)} async-done(((bf16[1,12,2304]{2,1,0:T(8,128)(2,1)}), bf16[64,12,2304]{2,1,0:T(8,128)(2,1)}) %all-gather.5.cloned.1.call-update) | async-done | bytes 3538960 | tf_op jit(solution)/shard_map/all_gather | solution.py:52
  95.2 6.4 %reshape.532 = bf16[768,2304]{1,0:T(8,128)(2,1)} reshape(bf16[64,12,2304]{2,1,0:T(8,128)(2,1)} %all-gather.5.cloned.1.call-done) | data formatting | bytes 7077888
  101.6 1.2 slice-done.1
  102.8 1.3 copy.223
  104.1 2.0 fusion.20
  107.2 1.4 squeeze.47
  108.6 1.5 fusion.19
  110.1 2.1 fusion.22
  113.0 1.8 convolution_convert_fusion.3
  114.8 19.9 %all_to_all.106 = bf16[4,192,768]{2,1,0:T(8,128)(2,1)S(1)} all-to-all(bf16[4,192,768]{2,1,0:T(8,128)(2,1)S(1)} %bitcast.178), channel_id=1, replica_groups=mesh['dp'=64,'mp'=4] {'mp'}, dimensions={0} | all-to-all | bytes 2359296 | tf_op jit(solution)/shard_map/all_to_all | solution.py:44
  135.5 17.4 %all_to_all.107 = bf16[4,192,768]{2,1,0:T(8,128)(2,1)S(1)} all-to-all(bf16[4,192,768]{2,1,0:T(8,128)(2,1)S(1)} %broadcast_in_dim.46), channel_id=1, replica_groups=mesh['dp'=64,'mp'=4] {'mp'}, dimensions={0} | all-to-all | bytes 2359296 | tf_op jit(solution)/shard_map/all_to_all | solution.py:22
  152.8 4.9 %convolution_convert_fusion.2 = bf16[768,768]{1,0:T(8,128)(2,1)} fusion(bf16[768,2304]{1,0:T(8,128)(2,1)} %reshape.532, bf16[768,768]{1,0:T(8,128)(2,1)S(1)} %bitcast.184), kind=kOutput, calls=%fused_computation.28 | convolution fusion | flops 1817837568 | bytes 4718592 | tf_op jit(solution)/shard_map/dot_general | solution.py:201
  157.7 17.6 %all_to_all.108 = bf16[4,192,768]{2,1,0:T(8,128)(2,1)S(1)} all-to-all(bf16[4,192,768]{2,1,0:T(8,128)(2,1)} %bitcast.185), channel_id=1, replica_groups=mesh['dp'=64,'mp'=4] {'mp'}, dimensions={0} | all-to-all | bytes 2359296 | tf_op jit(solution)/shard_map/all_to_all | solution.py:44
  177.1 4.5 %all-to-all-start.6 = ((bf16[4,192,768]{2,1,0:T(8,128)(2,1)}), bf16[4,192,768]{2,1,0:T(8,128)(2,1)}, u32[]{:S(2)}, u32[]{:S(2)}) async-start(bf16[4,192,768]{2,1,0:T(8,128)(2,1)} %broadcast_in_dim.47), calls=%async_computation.6 | async-start | bytes 2359296 | tf_op jit(solution)/shard_map/all_to_all | solution.py:22
  181.7 6.4 %reshape.534 = bf16[768,2304]{1,0:T(8,128)(2,1)} reshape(bf16[64,12,2304]{2,1,0:T(8,128)(2,1)} %all-gather.7.cloned.1.call-done) | data formatting | bytes 7077888
  188.1 1.2 slice-done
  189.9 4.6 %all-to-all-done.6 = bf16[4,192,768]{2,1,0:T(8,128)(2,1)} async-done(((bf16[4,192,768]{2,1,0:T(8,128)(2,1)}), bf16[4,192,768]{2,1,0:T(8,128)(2,1)}, u32[]{:S(2)}, u32[]{:S(2)}) %all-to-all-start.6) | async-done | bytes 1179680 | tf_op jit(solution)/shard_map/all_to_all | solution.py:22
  194.5 2.1 fusion.21
  197.6 1.4 squeeze.54
  199.0 1.5 fusion.17
  200.5 2.3 fusion.23
  203.6 1.8 convolution_convert_fusion.1
  205.4 14.5 %all_to_all.109 = bf16[4,192,768]{2,1,0:T(8,128)(2,1)S(1)} all-to-all(bf16[4,192,768]{2,1,0:T(8,128)(2,1)S(1)} %bitcast.179), channel_id=1, replica_groups=mesh['dp'=64,'mp'=4] {'mp'}, dimensions={0} | all-to-all | bytes 2359296 | tf_op jit(solution)/shard_map/all_to_all | solution.py:44
  220.6 1.1 broadcast_in_dim.48
  221.7 3.7 %all-to-all-start.8 = ((bf16[4,192,768]{2,1,0:T(8,128)(2,1)}), bf16[4,192,768]{2,1,0:T(8,128)(2,1)S(1)}, u32[]{:S(2)}, u32[]{:S(2)}) async-start(bf16[4,192,768]{2,1,0:T(8,128)(2,1)} %broadcast_in_dim.48), calls=%async_computation.8 | async-start | bytes 2359296 | tf_op jit(solution)/shard_map/all_to_all | solution.py:22
  225.5 1.2 scatter_custom_fusion
  226.7 9.6 %all-to-all-done.8 = bf16[4,192,768]{2,1,0:T(8,128)(2,1)S(1)} async-done(((bf16[4,192,768]{2,1,0:T(8,128)(2,1)}), bf16[4,192,768]{2,1,0:T(8,128)(2,1)S(1)}, u32[]{:S(2)}, u32[]{:S(2)}) %all-to-all-start.8) | async-done | bytes 1179680 | tf_op jit(solution)/shard_map/all_to_all | solution.py:22
  236.3 4.8 %convolution_convert_fusion = bf16[768,768]{1,0:T(8,128)(2,1)} fusion(bf16[768,2304]{1,0:T(8,128)(2,1)} %reshape.534, bf16[768,768]{1,0:T(8,128)(2,1)S(1)} %bitcast.183), kind=kOutput, calls=%fused_computation.26 | convolution fusion | flops 1817837568 | bytes 4718592 | tf_op jit(solution)/shard_map/dot_general | solution.py:201
  241.1 3.7 %all-to-all-start.9 = ((bf16[4,192,768]{2,1,0:T(8,128)(2,1)}), bf16[4,192,768]{2,1,0:T(8,128)(2,1)S(1)}, u32[]{:S(2)}, u32[]{:S(2)}) async-start(bf16[4,192,768]{2,1,0:T(8,128)(2,1)} %bitcast.35), calls=%async_computation.9 | async-start | bytes 2359296 | tf_op jit(solution)/shard_map/all_to_all | solution.py:44
  245.8 9.3 %all-to-all-done.9 = bf16[4,192,768]{2,1,0:T(8,128)(2,1)S(1)} async-done(((bf16[4,192,768]{2,1,0:T(8,128)(2,1)}), bf16[4,192,768]{2,1,0:T(8,128)(2,1)S(1)}, u32[]{:S(2)}, u32[]{:S(2)}) %all-to-all-start.9) | async-done | bytes 1179680 | tf_op jit(solution)/shard_map/all_to_all | solution.py:44
  255.2 13.7 %all-to-all-start = ((s32[64,1,2]{2,1,0:T(1,128)}), s32[64,1,2]{2,1,0:T(1,128)S(1)}, u32[]{:S(2)}, u32[]{:S(2)}) async-start(s32[64,1,2]{2,1,0:T(1,128)} %bitcast.62), calls=%async_computation | async-start | bytes 65536 | tf_op jit(solution)/shard_map/all_to_all | solution.py:222
  269.9 1.1 reshape.555
  271.1 7.1 %all-to-all-done = s32[64,1,2]{2,1,0:T(1,128)S(1)} async-done(((s32[64,1,2]{2,1,0:T(1,128)}), s32[64,1,2]{2,1,0:T(1,128)S(1)}, u32[]{:S(2)}, u32[]{:S(2)}) %all-to-all-start) | async-done | bytes 544 | tf_op jit(solution)/shard_map/all_to_all | solution.py:222
  278.2 3.3 all-to-all-start.10
  284.5 1.1 all-to-all-done.10
  288.6 6.2 %all-to-all-start.11 = ((bf16[64,2,304]{2,1,0:T(2,128)(2,1)}), bf16[64,2,304]{2,1,0:T(2,128)(2,1)S(1)}, u32[]{:S(2)}, u32[]{:S(2)}) async-start(bf16[64,2,304]{2,1,0:T(2,128)(2,1)} %pad_maximum_fusion), calls=%async_computation.11 | async-start | bytes 196608 | tf_op jit(solution)/shard_map/all_to_all | solution.py:65
  294.9 10.7 %all-to-all-done.11 = bf16[64,2,304]{2,1,0:T(2,128)(2,1)S(1)} async-done(((bf16[64,2,304]{2,1,0:T(2,128)(2,1)}), bf16[64,2,304]{2,1,0:T(2,128)(2,1)S(1)}, u32[]{:S(2)}, u32[]{:S(2)}) %all-to-all-start.11) | async-done | bytes 77856 | tf_op jit(solution)/shard_map/all_to_all | solution.py:65
  306.6 3.5 %all-to-all-start.12 = ((bf16[4,1,128,256]{3,2,1,0:T(8,128)(2,1)}), bf16[4,1,128,256]{3,2,1,0:T(8,128)(2,1)S(1)}, u32[]{:S(2)}, u32[]{:S(2)}) async-start(bf16[4,1,128,256]{3,2,1,0:T(8,128)(2,1)} %broadcast_in_dim.50), calls=%async_computation.12 | async-start | bytes 524288 | tf_op jit(solution)/shard_map/all_to_all | solution.py:22
  310.6 5.6 %all-to-all-done.12 = bf16[4,1,128,256]{3,2,1,0:T(8,128)(2,1)S(1)} async-done(((bf16[4,1,128,256]{3,2,1,0:T(8,128)(2,1)}), bf16[4,1,128,256]{3,2,1,0:T(8,128)(2,1)S(1)}, u32[]{:S(2)}, u32[]{:S(2)}) %all-to-all-start.12) | async-done | bytes 262176 | tf_op jit(solution)/shard_map/all_to_all | solution.py:22
  320.9 5.6 %all-to-all-start.13 = ((bf16[64,2,192]{2,1,0:T(2,128)(2,1)}), bf16[64,2,192]{2,1,0:T(2,128)(2,1)S(1)}, u32[]{:S(2)}, u32[]{:S(2)}) async-start(bf16[64,2,192]{2,1,0:T(2,128)(2,1)} %reshape_transpose_reshape.12), calls=%async_computation.13 | async-start | bytes 131072 | tf_op jit(solution)/shard_map/all_to_all | solution.py:281
  326.7 9.9 %all-to-all-done.13 = bf16[64,2,192]{2,1,0:T(2,128)(2,1)S(1)} async-done(((bf16[64,2,192]{2,1,0:T(2,128)(2,1)}), bf16[64,2,192]{2,1,0:T(2,128)(2,1)S(1)}, u32[]{:S(2)}, u32[]{:S(2)}) %all-to-all-start.13) | async-done | bytes 49184 | tf_op jit(solution)/shard_map/all_to_all | solution.py:281
  336.6 1.2 gather_fusion
  337.8 3.2 all-to-all-start.14
  344.1 1.1 all-to-all-done.14
  (160 shorter events, 33.8 us)
Async XLA Ops:
  7.2 298.6 %copy-start = (bf16[1,768,256]{2,1,0:T(8,128)(2,1)S(1)}, bf16[1,768,256]{2,1,0:T(8,128)(2,1)}, u32[]{:S(2)}) copy-start(bf16[1,768,256]{2,1,0:T(8,128)(2,1)} %param.30) | copy-start | bytes 1179652
  7.2 4.6 %copy-start.8 = (s32[3,64]{1,0:T(4,128)S(1)}, s32[3,64]{1,0:T(4,128)}, u32[]{:S(2)}) copy-start(s32[3,64]{1,0:T(4,128)} %param.19) | copy-start | bytes 2308
  7.2 10.9 %copy-start.6 = (f32[5,768]{1,0:T(8,128)S(1)}, f32[5,768]{1,0:T(8,128)}, u32[]{:S(2)}) copy-start(f32[5,768]{1,0:T(8,128)} %param.20) | copy-start | bytes 46084
  7.2 11.0 %copy-start.1 = (bf16[192,768]{1,0:T(8,128)(2,1)S(1)}, bf16[192,768]{1,0:T(8,128)(2,1)}, u32[]{:S(2)}) copy-start(bf16[192,768]{1,0:T(8,128)(2,1)} %param.18) | copy-start | bytes 884740
  7.2 88.0 %all-gather.5.cloned.1.call-start = ((), (), s32[]{:S(2)}) async-start(), calls=%async_computation.15 | async-start | bytes 4792320 | tf_op jit(solution)/shard_map/all_gather | solution.py:52
  12.4 9.0 %all-to-all-start.2 = ((s32[4,1,192]{2,1,0:T(1,128)}), s32[4,1,192]{2,1,0:T(1,128)S(1)}, u32[]{:S(2)}, u32[]{:S(2)}) async-start(s32[4,1,192]{2,1,0:T(1,128)} %reshape.553), calls=%async_computation.2 | async-start | bytes 8192 | tf_op jit(solution)/shard_map/all_to_all | solution.py:22
  17.3 164.4 %all-gather.7.cloned.1.call-start = ((), (), s32[]{:S(2)}) async-start(), calls=%async_computation.16 | async-start | bytes 4792320 | tf_op jit(solution)/shard_map/all_gather | solution.py:52
  22.6 81.6 %all-to-all-start.1 = ((bf16[4,192,768]{2,1,0:T(8,128)(2,1)}), bf16[4,192,768]{2,1,0:T(8,128)(2,1)S(1)}, u32[]{:S(2)}, u32[]{:S(2)}) async-start(bf16[4,192,768]{2,1,0:T(8,128)(2,1)} %broadcast_in_dim.42), calls=%async_computation.1 | async-start | bytes 2359296 | tf_op jit(solution)/shard_map/all_to_all | solution.py:22
  101.6 1.2 slice-start.1
  108.6 1.5 copy-start.2
  177.1 17.3 %all-to-all-start.6 = ((bf16[4,192,768]{2,1,0:T(8,128)(2,1)}), bf16[4,192,768]{2,1,0:T(8,128)(2,1)}, u32[]{:S(2)}, u32[]{:S(2)}) async-start(bf16[4,192,768]{2,1,0:T(8,128)(2,1)} %broadcast_in_dim.47), calls=%async_computation.6 | async-start | bytes 2359296 | tf_op jit(solution)/shard_map/all_to_all | solution.py:22
  188.1 1.2 slice-start
  221.7 3.7 %copy-start.9 = (s32[12,2]{0,1:T(2,128)S(1)}, s32[12,2]{0,1:T(2,128)}, u32[]{:S(2)}) copy-start(s32[12,2]{0,1:T(2,128)} %param.26) | copy-start | bytes 292
  221.7 3.8 %copy-start.13 = (s32[12,1]{0,1:T(1,128)S(1)}, s32[12,1]{0,1:T(1,128)}, u32[]{:S(2)}) copy-start(s32[12,1]{0,1:T(1,128)} %param.25) | copy-start | bytes 148
  221.7 14.6 %all-to-all-start.8 = ((bf16[4,192,768]{2,1,0:T(8,128)(2,1)}), bf16[4,192,768]{2,1,0:T(8,128)(2,1)S(1)}, u32[]{:S(2)}, u32[]{:S(2)}) async-start(bf16[4,192,768]{2,1,0:T(8,128)(2,1)} %broadcast_in_dim.48), calls=%async_computation.8 | async-start | bytes 2359296 | tf_op jit(solution)/shard_map/all_to_all | solution.py:22
  241.1 3.7 %copy-start.14 = (s32[25]{0:T(128)S(1)}, s32[25]{0:T(128)}, u32[]{:S(2)}) copy-start(s32[25]{0:T(128)} %param.29) | copy-start | bytes 304
  241.1 4.5 %copy-start.4 = (bf16[12,2,56]{2,1,0:T(2,128)(2,1)S(1)}, bf16[12,2,56]{2,1,0:T(2,128)(2,1)}, u32[]{:S(2)}) copy-start(bf16[12,2,56]{2,1,0:T(2,128)(2,1)} %param.28) | copy-start | bytes 8068
  241.1 4.6 %copy-start.7 = (bf16[12,2,56]{2,1,0:T(2,128)(2,1)S(1)}, bf16[12,2,56]{2,1,0:T(2,128)(2,1)}, u32[]{:S(2)}) copy-start(bf16[12,2,56]{2,1,0:T(2,128)(2,1)} %param.27) | copy-start | bytes 8068
  241.1 14.1 %all-to-all-start.9 = ((bf16[4,192,768]{2,1,0:T(8,128)(2,1)}), bf16[4,192,768]{2,1,0:T(8,128)(2,1)S(1)}, u32[]{:S(2)}, u32[]{:S(2)}) async-start(bf16[4,192,768]{2,1,0:T(8,128)(2,1)} %bitcast.35), calls=%async_computation.9 | async-start | bytes 2359296 | tf_op jit(solution)/shard_map/all_to_all | solution.py:44
  255.2 23.1 %all-to-all-start = ((s32[64,1,2]{2,1,0:T(1,128)}), s32[64,1,2]{2,1,0:T(1,128)S(1)}, u32[]{:S(2)}, u32[]{:S(2)}) async-start(s32[64,1,2]{2,1,0:T(1,128)} %bitcast.62), calls=%async_computation | async-start | bytes 65536 | tf_op jit(solution)/shard_map/all_to_all | solution.py:222
  278.2 7.4 %all-to-all-start.10 = ((bf16[4,2,576]{2,1,0:T(2,128)(2,1)}), bf16[4,2,576]{2,1,0:T(2,128)(2,1)S(1)}, u32[]{:S(2)}, u32[]{:S(2)}) async-start(bf16[4,2,576]{2,1,0:T(2,128)(2,1)} %reshape.555), calls=%async_computation.10 | async-start | bytes 20480 | tf_op jit(solution)/shard_map/all_to_all | solution.py:211
  286.4 24.1 %copy-start.3 = (bf16[1,56,256]{2,1,0:T(8,128)(2,1)S(1)}, bf16[1,56,256]{2,1,0:T(8,128)(2,1)}, u32[]{:S(2)}) copy-start(bf16[1,56,256]{2,1,0:T(8,128)(2,1)} %param.31) | copy-start | bytes 86020
  288.6 27.6 %copy-start.5 = (bf16[1,20,256]{2,1,0:T(8,128)(2,1)S(1)}, bf16[1,20,256]{2,1,0:T(8,128)(2,1)}, u32[]{:S(2)}) copy-start(bf16[1,20,256]{2,1,0:T(8,128)(2,1)} %param.32) | copy-start | bytes 30724
  288.6 16.9 %all-to-all-start.11 = ((bf16[64,2,304]{2,1,0:T(2,128)(2,1)}), bf16[64,2,304]{2,1,0:T(2,128)(2,1)S(1)}, u32[]{:S(2)}, u32[]{:S(2)}) async-start(bf16[64,2,304]{2,1,0:T(2,128)(2,1)} %pad_maximum_fusion), calls=%async_computation.11 | async-start | bytes 196608 | tf_op jit(solution)/shard_map/all_to_all | solution.py:65
  305.6 10.9 %copy-start.11 = (bf16[1,256,256]{2,1,0:T(8,128)(2,1)S(1)}, bf16[1,256,256]{2,1,0:T(8,128)(2,1)}, u32[]{:S(2)}) copy-start(bf16[1,256,256]{2,1,0:T(8,128)(2,1)} %param.33) | copy-start | bytes 393220
  306.6 10.1 %copy-start.10 = (bf16[1,256,256]{2,1,0:T(8,128)(2,1)S(1)}, bf16[1,256,256]{2,1,0:T(8,128)(2,1)}, u32[]{:S(2)}) copy-start(bf16[1,256,256]{2,1,0:T(8,128)(2,1)} %param.34) | copy-start | bytes 393220
  306.6 9.6 %all-to-all-start.12 = ((bf16[4,1,128,256]{3,2,1,0:T(8,128)(2,1)}), bf16[4,1,128,256]{3,2,1,0:T(8,128)(2,1)S(1)}, u32[]{:S(2)}, u32[]{:S(2)}) async-start(bf16[4,1,128,256]{3,2,1,0:T(8,128)(2,1)} %broadcast_in_dim.50), calls=%async_computation.12 | async-start | bytes 524288 | tf_op jit(solution)/shard_map/all_to_all | solution.py:22
  316.3 0.8 copy-start.12
  320.9 15.7 %all-to-all-start.13 = ((bf16[64,2,192]{2,1,0:T(2,128)(2,1)}), bf16[64,2,192]{2,1,0:T(2,128)(2,1)S(1)}, u32[]{:S(2)}, u32[]{:S(2)}) async-start(bf16[64,2,192]{2,1,0:T(2,128)(2,1)} %reshape_transpose_reshape.12), calls=%async_computation.13 | async-start | bytes 131072 | tf_op jit(solution)/shard_map/all_to_all | solution.py:281
  337.8 7.4 %all-to-all-start.14 = ((bf16[12,2,192]{2,1,0:T(2,128)(2,1)}), bf16[12,2,192]{2,1,0:T(2,128)(2,1)S(1)}, u32[]{:S(2)}, u32[]{:S(2)}) async-start(bf16[12,2,192]{2,1,0:T(2,128)(2,1)} %gather_fusion), calls=%async_computation.14 | async-start | bytes 24576 | tf_op jit(solution)/shard_map/all_to_all | solution.py:283
Sparse Core Ops, SparseCore 0:
  11.9 83.2 all-gather.4
  98.5 76.4 all-gather.6
where the time goes:
time: 355 us; the launch traced here: 353 us
  waiting for transfers between devices  129 us (36%)
  blocking collectives  69.4 us (20%)
  starting transfers between devices  55.8 us (16%)
  local copies, waits for them, and re-layouts  46.4 us (13%)
  matrix products  29.7 us (8%)
  between operations  14.8 us (4%)
  other arithmetic  7.36 us (2%)
    all_gather x2, waiting for transfers between devices, gather_turned(): whole = lax.all_gather(both, axis, axis=0, tiled=True)  67.6 us
    all_to_all x3, blocking collectives, summed_on_arrival(): lax.all_to_all(pieces, axis, split_axis=0, concat_axis=0, tiled=True)  52 us
    all_to_all x5, waiting for transfers between devices, sent_to_all(): return lax.all_to_all(copies, axis, split_axis=0, concat_axis=0, tiled=True)  22.4 us
    all_to_all x5, starting transfers between devices, sent_to_all(): return lax.all_to_all(copies, axis, split_axis=0, concat_axis=0, tiled=True)  20.1 us
    unnamed x41, local copies, waits for them, and re-layouts  18.1 us
    all_to_all x1, blocking collectives, sent_to_all(): return lax.all_to_all(copies, axis, split_axis=0, concat_axis=0, tiled=True)  17.4 us
    all_to_all x1, starting transfers between devices, on_device(): lax.all_to_all(send_levels, 'dp', split_axis=0, concat_axis=0, tiled=True)  13.7 us
    all_to_all x1, waiting for transfers between devices, in_one_piece(): lax.all_to_all(both, axis, split_axis=split_dim, concat_axis=concat_dim,...  10.7 us
  transfers between devices with their start and end apart: 13, of which 11 were waited for; matrix products, arithmetic and copies ran while one was open for 14% of the time, Pallas kernels for 0%

commit v1 on v0

v1 whole, which is shorter than its diff:
```python
import math

import jax
import jax.numpy as jnp
from jax import lax
from jax.sharding import Mesh, PartitionSpec as P

D = 768
HDIM = 64
EMB = 25
READ = 2
LEVELS = 20
ADIM_MAX = 14
ACT = 56
SEQ = 64
F32 = jnp.float32
BF16 = jnp.bfloat16
DP = ("z", "y", "c")


norm_eps = 1e-05


def sent_to_all(x, axis):
    copies = jnp.broadcast_to(x, (lax.axis_size(axis), *x.shape))
    return lax.all_to_all(copies, axis, split_axis=0, concat_axis=0, tiled=True)


def gather_rows(x, axis):
    pieces = sent_to_all(x, axis)
    return pieces.reshape(-1, *x.shape[1:])


def summed_on_arrival(x, axis):
    pieces = x.reshape(lax.axis_size(axis), -1, x.shape[1])
    arrived = lax.all_to_all(pieces, axis, split_axis=0, concat_axis=0, tiled=True)
    return arrived.astype(F32).sum(axis=0)


def summed_for_all(x, axis):
    return sent_to_all(x, axis).astype(F32).sum(axis=0)


def gather_turned(arrays, axis, dims):
    turned = [jnp.moveaxis(a, dim, 0) for a, dim in zip(arrays, dims)]
    widths = [t[0].size for t in turned]
    both = jnp.concatenate([t.reshape(-1, w) for t, w in zip(turned, widths)], axis=1)
    whole = lax.all_gather(both, axis, axis=0, tiled=True)
    pieces = jnp.split(whole, [sum(widths[:k]) for k in range(1, len(widths))], axis=1)
    return tuple(
        (
            jnp.moveaxis(b.reshape(-1, *t.shape[1:]), 0, dim)
            for b, t, dim in zip(pieces, turned, dims)
        )
    )


def normalize(values, scale_gain):
    center = values - jnp.mean(values, axis=-1, keepdims=True)
    spread = jnp.mean(center * center, axis=-1, keepdims=True)
    return center * lax.rsqrt(spread + norm_eps) * scale_gain


def mm(a, b):
    return jnp.dot(a, b, preferred_element_type=F32)


def allowed_keys(observed):
    length = observed.shape[1]
    position = jnp.arange(length)
    visible = (observed == 1) & (position < length - READ)[None, :]
    itself = position[:, None] == position[None, :]
    return visible[:, None, :] | itself[None, :, :]


def attend(queries, key_rows, value_rows, allowed):
    scores = jnp.einsum(
        "sqhd,skhd->shqk", queries, key_rows, preferred_element_type=F32
    ) * HDIM ** (-0.5)
    weights = jnp.where(allowed[:, None, :, :], jnp.exp(scores), 0.0)
    shares = (weights / jnp.sum(weights, axis=-1, keepdims=True)).astype(BF16)
    context = jnp.einsum("shqk,skhd->sqhd", shares, value_rows, preferred_element_type=F32)
    return context.astype(BF16)


def plan():
    steps_up = (jnp.arange(LEVELS, dtype=F32) + 1.0) / LEVELS
    anchor = math.cos(0.008 / 1.008 * math.pi / 2) ** 2
    return jnp.cos((steps_up + 0.008) / 1.008 * (math.pi / 2)) ** 2 / anchor


def noisy_pair(level_ids, clean, noise_draw, table):
    picked = (level_ids[..., None] == jnp.arange(LEVELS)).astype(F32)
    kept = jnp.sum(picked * table, axis=-1)[..., None]
    mixed = jnp.sqrt(kept) * clean.astype(F32) + jnp.sqrt(1.0 - kept) * noise_draw.astype(F32)
    return mixed.astype(BF16)


def tail(first, target, weight_mask, inner_weight, outer_weight, final_weight):
    active = jax.nn.silu(first).astype(BF16)
    inner = jnp.dot(active, inner_weight, preferred_element_type=F32)
    second = jax.nn.silu(inner).astype(BF16)
    hidden = first + jnp.dot(second, outer_weight, preferred_element_type=F32)
    third = jax.nn.silu(hidden).astype(BF16)
    predicted = jnp.dot(third, final_weight, preferred_element_type=F32)
    differ = predicted - target
    return 0.5 * jnp.sum(weight_mask * differ * differ)


def head_grads(first, inner_weight, outer_weight, final_weight, target, weight_mask):

    def head_loss(first_in, inner_in, outer_in, final_in):
        return tail(first_in, target, weight_mask, inner_in, outer_in, final_in)

    loss_value, pullback = jax.vjp(head_loss, first, inner_weight, outer_weight, final_weight)
    return pullback(jnp.ones((), F32))


def on_device(
    tokens,
    obs_mask,
    norm_gains,
    attn_in,
    attn_out,
    mlp_in,
    mlp_out,
    embodiment,
    levels,
    actions,
    noise,
    action_dims,
    head_read,
    head_act,
    time_table,
    block_in,
    block_out,
    head_out,
):
    width = attn_in.shape[3]
    heads = width // HDIM
    peers = lax.axis_size(DP)
    my_model = lax.axis_index("mp")
    my_owner = lax.axis_index(DP)

    owners = embodiment[:, 0]
    place = (jnp.arange(peers)[:, None] == owners[None, :]).astype(BF16)
    noisy = noisy_pair(levels, actions, noise, plan())
    marks = (levels + 1).astype(BF16)[..., None]
    early = jnp.concatenate([noisy, noise, marks, jnp.zeros((*levels.shape, 15), BF16)], axis=-1)
    sent = jnp.einsum("es,srf->erf", place, early, preferred_element_type=F32).astype(BF16)
    got = lax.all_to_all(sent, DP, split_axis=0, concat_axis=0, tiled=True)
    got = got.reshape(peers * READ, 128)

    def weights_of(layer):
        return gather_turned(
            (attn_in[layer], attn_out[layer], mlp_in[layer], mlp_out[layer]), DP, (1, 1, 0, 1)
        )

    residual = tokens.astype(F32)
    normed = normalize(residual, norm_gains[0]).astype(BF16)
    gathered = gather_rows(normed, "mp")
    mask_group = gather_rows(obs_mask, "mp")
    samples = mask_group.shape[0]
    allowed = allowed_keys(mask_group)
    qkv_weight, out_weight, up_weight, down_weight = weights_of(0)
    projected = jnp.einsum("td,jdc->jtc", gathered, qkv_weight, preferred_element_type=F32)
    projected = projected.astype(BF16).reshape(3, samples, SEQ, heads, HDIM)
    context = attend(projected[0], projected[1], projected[2], allowed).reshape(-1, width)
    residual = residual + summed_on_arrival(mm(context, out_weight).astype(BF16), "mp")
    normed = normalize(residual, norm_gains[1]).astype(BF16)
    gathered = gather_rows(normed, "mp")
    hidden = jax.nn.gelu(mm(gathered, up_weight), approximate=True).astype(BF16)
    residual = residual + summed_on_arrival(mm(hidden, down_weight).astype(BF16), "mp")

    whole = gather_rows(residual.astype(BF16), "mp").astype(F32)
    qkv_weight, out_weight, up_weight, down_weight = weights_of(1)
    normed = normalize(whole, norm_gains[2]).astype(BF16)
    last = slice(SEQ - READ, SEQ)
    ending = whole.reshape(samples, SEQ, D)[:, last].reshape(-1, D)
    normed_end = normed.reshape(samples, SEQ, D)[:, last].reshape(-1, D)
    queries = mm(normed_end, qkv_weight[0]).astype(BF16).reshape(samples, READ, heads, HDIM)
    key_rows = mm(normed, qkv_weight[1]).astype(BF16).reshape(samples, SEQ, heads, HDIM)
    value_rows = mm(normed, qkv_weight[2]).astype(BF16).reshape(samples, SEQ, heads, HDIM)
    context = attend(queries, key_rows, value_rows, allowed[:, last]).reshape(-1, width)
    ending = ending + summed_for_all(mm(context, out_weight).astype(BF16), "mp")
    normed = normalize(ending, norm_gains[3]).astype(BF16)
    hidden = jax.nn.gelu(mm(normed, up_weight), approximate=True).astype(BF16)
    ending = ending + summed_for_all(mm(hidden, down_weight).astype(BF16), "mp")
    readouts = normalize(ending, norm_gains[4]).astype(BF16).reshape(samples, READ * D)

    send = mm(place, readouts).astype(BF16)
    features = lax.all_to_all(send, DP, split_axis=0, concat_axis=0, tiled=True)
    features = features.reshape(peers * READ, D)
    head_noisy = got[:, :ACT]
    head_target = got[:, ACT : 2 * ACT].astype(F32)
    head_level = got[:, 2 * ACT].astype(jnp.int32) - 1
    onehot = (head_level[:, None] == jnp.arange(LEVELS)).astype(BF16)
    dims_here = jnp.sum(jnp.where(jnp.arange(EMB) == my_owner, action_dims, 0))
    column = jnp.arange(ACT) % ADIM_MAX
    weight_mask = (head_level >= 0).astype(F32)[:, None] * (column < dims_here).astype(F32)[None, :]
    others = mm(head_noisy, head_act[0]) + mm(onehot, time_table[0])
    first = mm(features, head_read[0]) + others
    grad_first, grad_inner, grad_outer, grad_final = head_grads(
        first,
        block_in[0].astype(F32),
        block_out[0].astype(F32),
        head_out[0].astype(F32),
        head_target,
        weight_mask,
    )
    grad_bf = grad_first.astype(BF16)
    backward = jnp.einsum("nc,dc->nd", grad_bf, head_read[0], preferred_element_type=F32)
    backward = backward.astype(BF16).reshape(peers, READ * D)
    arrived = lax.all_to_all(backward, DP, split_axis=0, concat_axis=0, tiled=True)
    mine = samples // 4
    own_place = lax.dynamic_slice_in_dim(place, my_model * mine, mine, 1)
    arrived = jnp.einsum("es,ef->sf", own_place, arrived, preferred_element_type=F32)
    arrived = arrived.astype(BF16).reshape(mine, READ, D)
    part = lax.dynamic_slice_in_dim(features, my_model * width, width, 1)
    grad_read = jnp.einsum("nd,nc->dc", part, grad_bf, preferred_element_type=F32)
    grad_act = jnp.einsum("na,nc->ac", head_noisy, grad_bf, preferred_element_type=F32)
    grad_time = jnp.einsum("nl,nc->lc", onehot, grad_bf, preferred_element_type=F32)
    return (
        arrived,
        grad_read[None],
        grad_act[None],
        grad_time[None],
        grad_inner[None],
        grad_outer[None],
        grad_final[None],
    )


def solution(mesh):
    fine = Mesh(mesh.devices.reshape(8, 4, 2, 4), ("z", "y", "c", "mp"))
    both = (*DP, "mp")
    placed = (
        P(both, None),
        P(both, None),
        P(),
        P(None, None, DP, "mp"),
        P(None, "mp", DP),
        P(None, DP, "mp"),
        P(None, "mp", DP),
        P(DP, None),
        P(DP, None),
        P(DP, None, None),
        P(DP, None, None),
        P(),
        P(DP, None, None),
        P(DP, None, None),
        P(DP, None, None),
        P(DP, None, None),
        P(DP, None, None),
        P(DP, None, None),
    )
    return jax.shard_map(
        on_device,
        mesh=fine,
        in_specs=placed,
        out_specs=(
            P(both, None, None),
            P(DP, "mp", None),
            P(DP, None, None),
            P(DP, None, None),
            P(DP, None, None),
            P(DP, None, None),
            P(DP, None, None),
        ),
        check_vma=False,
    )
```

time: 355 us -> 304 us (0.86)
  blocking collectives: 69.4 us -> 37.2 us
  waiting for transfers between devices: 129 us -> 118 us
  starting transfers between devices: 55.8 us -> 45.9 us
  other arithmetic: 7.36 us -> 13.7 us
  local copies, waits for them, and re-layouts: 46.4 us -> 42.7 us
    all_to_all x3 -> x1, blocking collectives: 52 us -> 19.9 us  [summed_on_arrival(): lax.all_to_all(pieces, axis, split_axis=0, concat_axis=0, tiled=True)]
    all_to_all x5, waiting for transfers between devices: 22.4 us -> 12.9 us  [sent_to_all(): return lax.all_to_all(copies, axis, split_axis=0, concat_axis=0, tiled=True)]
    all_to_all x5 -> x3, starting transfers between devices: 32 us -> 23.3 us  [the longest x1 11.9 us: on_device(): got = lax.all_to_all(sent, DP, split_axis=0, concat_axis=0, tiled=True)]
    all_to_all x5 -> x3, waiting for transfers between devices: 29.9 us -> 23.7 us  [the longest x1 11.2 us: on_device(): features = lax.all_to_all(send, DP, split_axis=0, concat_axis=0, tiled=True)]
    reshape x2 -> x9, local copies, waits for them, and re-layouts: 0.85 us -> 5.22 us  [the longest x1 2.34 us: on_device(): mm(normed, qkv_weight[1]).astype(BF16).reshape(samples, SEQ, heads, HDIM)]
    all_to_all x1, waiting for transfers between devices: 9.34 us -> 13.6 us  [summed_on_arrival(): lax.all_to_all(pieces, axis, split_axis=0, concat_axis=0, tiled=True)]
    dot_general x24 -> x29, matrix products: 25.4 us -> 27.3 us  [the longest x11 14 us: mm(): return jnp.dot(a, b, preferred_element_type=F32)]
    unnamed x41 -> x50, local copies, waits for them, and re-layouts: 18.1 us -> 18.1 us
  transfers between devices with their start and end apart: 13 -> 11, of which waited for: 11 -> 9; matrix products, arithmetic and copies ran while one was open for 14% -> 17% of each run, Pallas kernels for 0% -> 0%
where the time goes in v1:
time: 304 us; the launch traced here: 302 us
  waiting for transfers between devices  118 us (39%)
  starting transfers between devices  45.9 us (15%)
  local copies, waits for them, and re-layouts  42.7 us (14%)
  blocking collectives  37.2 us (12%)
  matrix products  29.9 us (10%)
  between operations  14.9 us (5%)
  other arithmetic  13.7 us (5%)
    all_gather x2, waiting for transfers between devices, gather_turned(): whole = lax.all_gather(both, axis, axis=0, tiled=True)  67.6 us
    all_to_all x1, blocking collectives, summed_on_arrival(): lax.all_to_all(pieces, axis, split_axis=0, concat_axis=0, tiled=True)  19.9 us
    all_to_all x5, starting transfers between devices, sent_to_all(): return lax.all_to_all(copies, axis, split_axis=0, concat_axis=0, tiled=True)  18.9 us
    unnamed x50, local copies, waits for them, and re-layouts  18.1 us
    all_to_all x1, blocking collectives, sent_to_all(): return lax.all_to_all(copies, axis, split_axis=0, concat_axis=0, tiled=True)  17.3 us
    dot_general x11, matrix products, mm(): return jnp.dot(a, b, preferred_element_type=F32)  14 us
    all_to_all x1, waiting for transfers between devices, summed_on_arrival(): lax.all_to_all(pieces, axis, split_axis=0, concat_axis=0, tiled=True)  13.6 us
    all_to_all x5, waiting for transfers between devices, sent_to_all(): return lax.all_to_all(copies, axis, split_axis=0, concat_axis=0, tiled=True)  12.9 us
  transfers between devices with their start and end apart: 11, of which 9 were waited for; matrix products, arithmetic and copies ran while one was open for 17% of the time, Pallas kernels for 0%

profile of v1, /device:TPU:1, one launch (start us, length us, event | category | flops | bytes accessed | tf_op | source)
XLA Modules:
  0.0 302.3 jit_solution(15710188673894022588)
XLA Ops:
  12.4 4.8 %all-to-all-start.2 = ((s32[4,1,192]{2,1,0:T(1,128)}), s32[4,1,192]{2,1,0:T(1,128)S(1)}, u32[]{:S(2)}, u32[]{:S(2)}) async-start(s32[4,1,192]{2,1,0:T(1,128)} %reshape.374), calls=%async_computation.2 | async-start | bytes 8192 | tf_op jit(solution)/shard_map/all_to_all | solution.py:26
  18.8 2.6 all-to-all-done.2
  21.4 1.1 broadcast_in_dim.107
  22.5 3.5 %all-to-all-start.1 = ((bf16[4,192,768]{2,1,0:T(8,128)(2,1)}), bf16[4,192,768]{2,1,0:T(8,128)(2,1)S(1)}, u32[]{:S(2)}, u32[]{:S(2)}) async-start(bf16[4,192,768]{2,1,0:T(8,128)(2,1)} %broadcast_in_dim.107), calls=%async_computation.1 | async-start | bytes 2359296 | tf_op jit(solution)/shard_map/all_to_all | solution.py:26
  27.6 67.6 %all-gather.5.cloned.1.call-done = bf16[64,12,2304]{2,1,0:T(8,128)(2,1)} async-done(((bf16[1,12,2304]{2,1,0:T(8,128)(2,1)}), bf16[64,12,2304]{2,1,0:T(8,128)(2,1)}) %all-gather.5.cloned.1.call-update) | async-done | bytes 3538960 | tf_op jit(solution)/shard_map/all_gather | solution.py:48
  95.2 6.4 %reshape.361 = bf16[768,2304]{1,0:T(8,128)(2,1)} reshape(bf16[64,12,2304]{2,1,0:T(8,128)(2,1)} %all-gather.5.cloned.1.call-done) | data formatting | bytes 7077888
  101.6 1.2 slice-done.1
  102.8 1.3 copy.215
  104.1 2.1 fusion.11
  107.2 1.4 squeeze.67
  108.5 2.6 fusion.10
  111.2 2.1 fusion.12
  114.2 1.8 convolution_convert_fusion.3
  115.9 19.9 %all_to_all.67 = bf16[4,192,768]{2,1,0:T(8,128)(2,1)S(1)} all-to-all(bf16[4,192,768]{2,1,0:T(8,128)(2,1)S(1)} %bitcast.164), channel_id=1, replica_groups=mesh['z'=8,'y'=4,'c'=2,'mp'=4] {'mp'}, dimensions={0} | all-to-all | bytes 2359296 | tf_op jit(solution)/shard_map/all_to_all | solution.py:36
  136.6 17.3 %all_to_all.68 = bf16[4,192,768]{2,1,0:T(8,128)(2,1)S(1)} all-to-all(bf16[4,192,768]{2,1,0:T(8,128)(2,1)S(1)} %broadcast_in_dim.111), channel_id=1, replica_groups=mesh['z'=8,'y'=4,'c'=2,'mp'=4] {'mp'}, dimensions={0} | all-to-all | bytes 2359296 | tf_op jit(solution)/shard_map/all_to_all | solution.py:26
  153.9 4.9 %convolution_convert_fusion.2 = bf16[768,768]{1,0:T(8,128)(2,1)} fusion(bf16[768,2304]{1,0:T(8,128)(2,1)} %reshape.361, bf16[768,768]{1,0:T(8,128)(2,1)S(1)} %bitcast.177), kind=kOutput, calls=%fused_computation.17 | convolution fusion | flops 1817837568 | bytes 4718592 | tf_op jit(solution)/shard_map/dot_general | solution.py:65
  158.8 3.7 %all-to-all-start.5 = ((bf16[4,192,768]{2,1,0:T(8,128)(2,1)}), bf16[4,192,768]{2,1,0:T(8,128)(2,1)S(1)}, u32[]{:S(2)}, u32[]{:S(2)}) async-start(bf16[4,192,768]{2,1,0:T(8,128)(2,1)} %bitcast.174), calls=%async_computation.5 | async-start | bytes 2359296 | tf_op jit(solution)/shard_map/all_to_all | solution.py:36
  162.9 13.6 %all-to-all-done.5 = bf16[4,192,768]{2,1,0:T(8,128)(2,1)S(1)} async-done(((bf16[4,192,768]{2,1,0:T(8,128)(2,1)}), bf16[4,192,768]{2,1,0:T(8,128)(2,1)S(1)}, u32[]{:S(2)}, u32[]{:S(2)}) %all-to-all-start.5) | async-done | bytes 1179680 | tf_op jit(solution)/shard_map/all_to_all | solution.py:36
  176.7 1.2 broadcast_in_dim.112
  177.9 3.9 %all-to-all-start.6 = ((bf16[4,192,768]{2,1,0:T(8,128)(2,1)}), bf16[4,192,768]{2,1,0:T(8,128)(2,1)S(1)}, u32[]{:S(2)}, u32[]{:S(2)}) async-start(bf16[4,192,768]{2,1,0:T(8,128)(2,1)} %broadcast_in_dim.112), calls=%async_computation.6 | async-start | bytes 2359296 | tf_op jit(solution)/shard_map/all_to_all | solution.py:26
  184.7 6.4 %reshape.363 = bf16[768,2304]{1,0:T(8,128)(2,1)} reshape(bf16[64,12,2304]{2,1,0:T(8,128)(2,1)} %all-gather.7.cloned.1.call-done) | data formatting | bytes 7077888
  191.2 1.2 slice-done
  193.0 1.5 all-to-all-done.6
  195.8 1.3 convolution_convert_fusion.6
  197.1 1.3 convolution_convert_fusion.7
  198.5 1.4 reshape.350
  200.0 2.3 reshape.353
  202.5 1.4 copy-done.2
  204.4 1.4 fusion.36
  206.4 1.4 convolution_convert_fusion.12
  208.5 3.3 %all-to-all-start.7 = ((bf16[4,24,768]{2,1,0:T(8,128)(2,1)}), bf16[4,24,768]{2,1,0:T(8,128)(2,1)S(1)}, u32[]{:S(2)}, u32[]{:S(2)}) async-start(bf16[4,24,768]{2,1,0:T(8,128)(2,1)} %broadcast_in_dim.115), calls=%async_computation.7 | async-start | bytes 294912 | tf_op jit(solution)/shard_map/all_to_all | solution.py:26
  212.6 4.1 %all-to-all-done.7 = bf16[4,24,768]{2,1,0:T(8,128)(2,1)S(1)} async-done(((bf16[4,24,768]{2,1,0:T(8,128)(2,1)}), bf16[4,24,768]{2,1,0:T(8,128)(2,1)S(1)}, u32[]{:S(2)}, u32[]{:S(2)}) %all-to-all-start.7) | async-done | bytes 147488 | tf_op jit(solution)/shard_map/all_to_all | solution.py:26
  216.7 11.9 %all-to-all-start = ((bf16[64,2,128]{2,1,0:T(2,128)(2,1)}), bf16[64,2,128]{2,1,0:T(2,128)(2,1)S(1)}, u32[]{:S(2)}, u32[]{:S(2)}) async-start(bf16[64,2,128]{2,1,0:T(2,128)(2,1)} %copy.209), calls=%async_computation | async-start | bytes 65536 | tf_op jit(solution)/shard_map/all_to_all | solution.py:151
  228.6 1.1 fusion.146
  229.8 1.2 multiply_reduce_fusion.3
  231.1 2.4 fusion.32
  233.4 4.5 %all-to-all-done = bf16[64,2,128]{2,1,0:T(2,128)(2,1)S(1)} async-done(((bf16[64,2,128]{2,1,0:T(2,128)(2,1)}), bf16[64,2,128]{2,1,0:T(2,128)(2,1)S(1)}, u32[]{:S(2)}, u32[]{:S(2)}) %all-to-all-start) | async-done | bytes 32800 | tf_op jit(solution)/shard_map/all_to_all | solution.py:151
  238.6 3.3 %all-to-all-start.8 = ((bf16[4,24,768]{2,1,0:T(8,128)(2,1)}), bf16[4,24,768]{2,1,0:T(8,128)(2,1)S(1)}, u32[]{:S(2)}, u32[]{:S(2)}) async-start(bf16[4,24,768]{2,1,0:T(8,128)(2,1)} %broadcast_in_dim.116), calls=%async_computation.8 | async-start | bytes 294912 | tf_op jit(solution)/shard_map/all_to_all | solution.py:26
  242.2 4.6 %all-to-all-done.8 = bf16[4,24,768]{2,1,0:T(8,128)(2,1)S(1)} async-done(((bf16[4,24,768]{2,1,0:T(8,128)(2,1)}), bf16[4,24,768]{2,1,0:T(8,128)(2,1)S(1)}, u32[]{:S(2)}, u32[]{:S(2)}) %all-to-all-start.8) | async-done | bytes 147488 | tf_op jit(solution)/shard_map/all_to_all | solution.py:26
  246.9 1.1 fusion.147
  250.8 7.0 %all-to-all-start.9 = ((bf16[64,2,768]{2,1,0:T(2,128)(2,1)}), bf16[64,2,768]{2,1,0:T(2,128)(2,1)S(1)}, u32[]{:S(2)}, u32[]{:S(2)}) async-start(bf16[64,2,768]{2,1,0:T(2,128)(2,1)} %reshape.376), calls=%async_computation.9 | async-start | bytes 393216 | tf_op jit(solution)/shard_map/all_to_all | solution.py:192
  258.7 11.2 %all-to-all-done.9 = bf16[64,2,768]{2,1,0:T(2,128)(2,1)S(1)} async-done(((bf16[64,2,768]{2,1,0:T(2,128)(2,1)}), bf16[64,2,768]{2,1,0:T(2,128)(2,1)S(1)}, u32[]{:S(2)}, u32[]{:S(2)}) %all-to-all-start.9) | async-done | bytes 196640 | tf_op jit(solution)/shard_map/all_to_all | solution.py:192
  270.0 1.1 reduce.12
  273.6 1.0 convolution_bitcast_fusion.2
  274.7 1.8 reduce.23
  277.2 4.5 %all-to-all-start.10 = ((bf16[64,2,768]{2,1,0:T(2,128)(2,1)}), bf16[64,2,768]{2,1,0:T(2,128)(2,1)S(1)}, u32[]{:S(2)}, u32[]{:S(2)}) async-start(bf16[64,2,768]{2,1,0:T(2,128)(2,1)} %reshape.378), calls=%async_computation.10 | async-start | bytes 393216 | tf_op jit(solution)/shard_map/all_to_all | solution.py:214
  283.8 0.9 convolution_bitcast_fusion.1
  285.7 8.1 %all-to-all-done.10 = bf16[64,2,768]{2,1,0:T(2,128)(2,1)S(1)} async-done(((bf16[64,2,768]{2,1,0:T(2,128)(2,1)}), bf16[64,2,768]{2,1,0:T(2,128)(2,1)S(1)}, u32[]{:S(2)}, u32[]{:S(2)}) %all-to-all-start.10) | async-done | bytes 196640 | tf_op jit(solution)/shard_map/all_to_all | solution.py:214
  (177 shorter events, 31.7 us)
Async XLA Ops:
  7.2 264.1 %copy-start = (bf16[1,768,256]{2,1,0:T(8,128)(2,1)S(1)}, bf16[1,768,256]{2,1,0:T(8,128)(2,1)}, u32[]{:S(2)}) copy-start(bf16[1,768,256]{2,1,0:T(8,128)(2,1)} %param.30) | copy-start | bytes 1179652
  7.2 4.6 %copy-start.10 = (s32[3,64]{1,0:T(4,128)S(1)}, s32[3,64]{1,0:T(4,128)}, u32[]{:S(2)}) copy-start(s32[3,64]{1,0:T(4,128)} %param.19) | copy-start | bytes 2308
  7.2 10.9 %copy-start.1 = (bf16[192,768]{1,0:T(8,128)(2,1)S(1)}, bf16[192,768]{1,0:T(8,128)(2,1)}, u32[]{:S(2)}) copy-start(bf16[192,768]{1,0:T(8,128)(2,1)} %param.18) | copy-start | bytes 884740
  7.2 11.3 %copy-start.6 = (f32[5,768]{1,0:T(8,128)S(1)}, f32[5,768]{1,0:T(8,128)}, u32[]{:S(2)}) copy-start(f32[5,768]{1,0:T(8,128)} %param.20) | copy-start | bytes 46084
  7.2 88.0 %all-gather.5.cloned.1.call-start = ((), (), s32[]{:S(2)}) async-start(), calls=%async_computation.11 | async-start | bytes 4792320 | tf_op jit(solution)/shard_map/all_gather | solution.py:48
  12.4 9.0 %all-to-all-start.2 = ((s32[4,1,192]{2,1,0:T(1,128)}), s32[4,1,192]{2,1,0:T(1,128)S(1)}, u32[]{:S(2)}, u32[]{:S(2)}) async-start(s32[4,1,192]{2,1,0:T(1,128)} %reshape.374), calls=%async_computation.2 | async-start | bytes 8192 | tf_op jit(solution)/shard_map/all_to_all | solution.py:26
  17.3 167.5 %all-gather.7.cloned.1.call-start = ((), (), s32[]{:S(2)}) async-start(), calls=%async_computation.12 | async-start | bytes 4792320 | tf_op jit(solution)/shard_map/all_gather | solution.py:48
  22.5 81.6 %all-to-all-start.1 = ((bf16[4,192,768]{2,1,0:T(8,128)(2,1)}), bf16[4,192,768]{2,1,0:T(8,128)(2,1)S(1)}, u32[]{:S(2)}, u32[]{:S(2)}) async-start(bf16[4,192,768]{2,1,0:T(8,128)(2,1)} %broadcast_in_dim.107), calls=%async_computation.1 | async-start | bytes 2359296 | tf_op jit(solution)/shard_map/all_to_all | solution.py:26
  101.6 1.2 slice-start.1
  158.8 3.7 %copy-start.11 = (s32[12,2]{0,1:T(2,128)S(1)}, s32[12,2]{0,1:T(2,128)}, u32[]{:S(2)}) copy-start(s32[12,2]{0,1:T(2,128)} %param.26) | copy-start | bytes 292
  158.8 17.7 %all-to-all-start.5 = ((bf16[4,192,768]{2,1,0:T(8,128)(2,1)}), bf16[4,192,768]{2,1,0:T(8,128)(2,1)S(1)}, u32[]{:S(2)}, u32[]{:S(2)}) async-start(bf16[4,192,768]{2,1,0:T(8,128)(2,1)} %bitcast.174), calls=%async_computation.5 | async-start | bytes 2359296 | tf_op jit(solution)/shard_map/all_to_all | solution.py:36
  177.9 4.0 %copy-start.4 = (bf16[12,2,56]{2,1,0:T(2,128)(2,1)S(1)}, bf16[12,2,56]{2,1,0:T(2,128)(2,1)}, u32[]{:S(2)}) copy-start(bf16[12,2,56]{2,1,0:T(2,128)(2,1)} %param.28) | copy-start | bytes 8068
  177.9 4.1 %copy-start.7 = (bf16[12,2,56]{2,1,0:T(2,128)(2,1)S(1)}, bf16[12,2,56]{2,1,0:T(2,128)(2,1)}, u32[]{:S(2)}) copy-start(bf16[12,2,56]{2,1,0:T(2,128)(2,1)} %param.27) | copy-start | bytes 8068
  177.9 4.2 %copy-start.8 = (s32[12,1]{0,1:T(1,128)S(1)}, s32[12,1]{0,1:T(1,128)}, u32[]{:S(2)}) copy-start(s32[12,1]{0,1:T(1,128)} %param.25) | copy-start | bytes 148
  177.9 5.1 %copy-start.15 = (s32[25]{0:T(128)S(1)}, s32[25]{0:T(128)}, u32[]{:S(2)}) copy-start(s32[25]{0:T(128)} %param.29) | copy-start | bytes 304
  177.9 16.5 %all-to-all-start.6 = ((bf16[4,192,768]{2,1,0:T(8,128)(2,1)}), bf16[4,192,768]{2,1,0:T(8,128)(2,1)S(1)}, u32[]{:S(2)}, u32[]{:S(2)}) async-start(bf16[4,192,768]{2,1,0:T(8,128)(2,1)} %broadcast_in_dim.112), calls=%async_computation.6 | async-start | bytes 2359296 | tf_op jit(solution)/shard_map/all_to_all | solution.py:26
  191.2 1.2 slice-start
  202.5 1.4 copy-start.2
  208.5 8.2 %all-to-all-start.7 = ((bf16[4,24,768]{2,1,0:T(8,128)(2,1)}), bf16[4,24,768]{2,1,0:T(8,128)(2,1)S(1)}, u32[]{:S(2)}, u32[]{:S(2)}) async-start(bf16[4,24,768]{2,1,0:T(8,128)(2,1)} %broadcast_in_dim.115), calls=%async_computation.7 | async-start | bytes 294912 | tf_op jit(solution)/shard_map/all_to_all | solution.py:26
  216.7 21.2 %all-to-all-start = ((bf16[64,2,128]{2,1,0:T(2,128)(2,1)}), bf16[64,2,128]{2,1,0:T(2,128)(2,1)S(1)}, u32[]{:S(2)}, u32[]{:S(2)}) async-start(bf16[64,2,128]{2,1,0:T(2,128)(2,1)} %copy.209), calls=%async_computation | async-start | bytes 65536 | tf_op jit(solution)/shard_map/all_to_all | solution.py:151
  231.1 10.8 %copy-start.3 = (bf16[1,56,256]{2,1,0:T(8,128)(2,1)S(1)}, bf16[1,56,256]{2,1,0:T(8,128)(2,1)}, u32[]{:S(2)}) copy-start(bf16[1,56,256]{2,1,0:T(8,128)(2,1)} %param.31) | copy-start | bytes 86020
  238.6 8.2 %all-to-all-start.8 = ((bf16[4,24,768]{2,1,0:T(8,128)(2,1)}), bf16[4,24,768]{2,1,0:T(8,128)(2,1)S(1)}, u32[]{:S(2)}, u32[]{:S(2)}) async-start(bf16[4,24,768]{2,1,0:T(8,128)(2,1)} %broadcast_in_dim.116), calls=%async_computation.8 | async-start | bytes 294912 | tf_op jit(solution)/shard_map/all_to_all | solution.py:26
  242.1 6.5 %copy-start.9 = (s32[12,1]{0,1:T(1,128)S(1)}, s32[12,1]{0,1:T(1,128)}, u32[]{:S(2)}) copy-start(s32[12,1]{0,1:T(1,128)} %param.25) | copy-start | bytes 148
  248.5 10.0 %copy-start.5 = (bf16[1,20,256]{2,1,0:T(8,128)(2,1)S(1)}, bf16[1,20,256]{2,1,0:T(8,128)(2,1)}, u32[]{:S(2)}) copy-start(bf16[1,20,256]{2,1,0:T(8,128)(2,1)} %param.32) | copy-start | bytes 30724
  250.8 19.0 %all-to-all-start.9 = ((bf16[64,2,768]{2,1,0:T(2,128)(2,1)}), bf16[64,2,768]{2,1,0:T(2,128)(2,1)S(1)}, u32[]{:S(2)}, u32[]{:S(2)}) async-start(bf16[64,2,768]{2,1,0:T(2,128)(2,1)} %reshape.376), calls=%async_computation.9 | async-start | bytes 393216 | tf_op jit(solution)/shard_map/all_to_all | solution.py:192
  258.7 12.8 %copy-start.13 = (bf16[1,256,256]{2,1,0:T(8,128)(2,1)S(1)}, bf16[1,256,256]{2,1,0:T(8,128)(2,1)}, u32[]{:S(2)}) copy-start(bf16[1,256,256]{2,1,0:T(8,128)(2,1)} %param.33) | copy-start | bytes 393220
  270.0 1.7 copy-start.12
  271.5 0.8 copy-start.14
  277.2 16.6 %all-to-all-start.10 = ((bf16[64,2,768]{2,1,0:T(2,128)(2,1)}), bf16[64,2,768]{2,1,0:T(2,128)(2,1)S(1)}, u32[]{:S(2)}, u32[]{:S(2)}) async-start(bf16[64,2,768]{2,1,0:T(2,128)(2,1)} %reshape.378), calls=%async_computation.10 | async-start | bytes 393216 | tf_op jit(solution)/shard_map/all_to_all | solution.py:214
Sparse Core Ops, SparseCore 0:
  11.9 83.2 all-gather.4
  98.5 76.5 all-gather.6

commit v2 on v1

--- a/solution.py
+++ b/solution.py
@@ -41,20 +41,6 @@
     return sent_to_all(x, axis).astype(F32).sum(axis=0)
 
 
-def gather_turned(arrays, axis, dims):
-    turned = [jnp.moveaxis(a, dim, 0) for a, dim in zip(arrays, dims)]
-    widths = [t[0].size for t in turned]
-    both = jnp.concatenate([t.reshape(-1, w) for t, w in zip(turned, widths)], axis=1)
-    whole = lax.all_gather(both, axis, axis=0, tiled=True)
-    pieces = jnp.split(whole, [sum(widths[:k]) for k in range(1, len(widths))], axis=1)
-    return tuple(
-        (
-            jnp.moveaxis(b.reshape(-1, *t.shape[1:]), 0, dim)
-            for b, t, dim in zip(pieces, turned, dims)
-        )
-    )
-
-
 def normalize(values, scale_gain):
     center = values - jnp.mean(values, axis=-1, keepdims=True)
     spread = jnp.mean(center * center, axis=-1, keepdims=True)
@@ -63,6 +49,10 @@
 
 def mm(a, b):
     return jnp.dot(a, b, preferred_element_type=F32)
+
+
+def mm_t(a, b):
+    return jnp.einsum("tk,dk->td", a, b, preferred_element_type=F32)
 
 
 def allowed_keys(observed):
@@ -142,50 +132,99 @@
     my_model = lax.axis_index("mp")
     my_owner = lax.axis_index(DP)
 
+    own_z = lax.axis_index("z")
+
+    full = jnp.concatenate(
+        [
+            jnp.moveaxis(attn_in[1], 0, 1).reshape(12, -1),
+            attn_out[1].T,
+            mlp_in[0],
+            mlp_out[0].T,
+        ],
+        axis=1,
+    )
+    groups = full.shape[1] // width
+    full = sent_to_all(full, "mp").reshape(2, 2, 12, groups, width)
+    full = full.transpose(0, 2, 3, 1, 4).reshape(2, 12, -1)
+    share = jnp.stack([mlp_in[1], mlp_out[1].T], axis=1).reshape(12, 2, 2, -1)
+    share = share.transpose(2, 0, 1, 3).reshape(2, 12, -1)
+    halves = jnp.concatenate([full, share], axis=2)
+    halves = lax.all_to_all(halves, "c", split_axis=0, concat_axis=0, tiled=True)
+    piece = halves.reshape(24, -1)
+
     owners = embodiment[:, 0]
     place = (jnp.arange(peers)[:, None] == owners[None, :]).astype(BF16)
     noisy = noisy_pair(levels, actions, noise, plan())
     marks = (levels + 1).astype(BF16)[..., None]
     early = jnp.concatenate([noisy, noise, marks, jnp.zeros((*levels.shape, 15), BF16)], axis=-1)
     sent = jnp.einsum("es,srf->erf", place, early, preferred_element_type=F32).astype(BF16)
-    got = lax.all_to_all(sent, DP, split_axis=0, concat_axis=0, tiled=True)
-    got = got.reshape(peers * READ, 128)
-
-    def weights_of(layer):
-        return gather_turned(
-            (attn_in[layer], attn_out[layer], mlp_in[layer], mlp_out[layer]), DP, (1, 1, 0, 1)
-        )
-
     residual = tokens.astype(F32)
     normed = normalize(residual, norm_gains[0]).astype(BF16)
+    first_piece = jnp.concatenate(
+        [jnp.moveaxis(attn_in[0], 0, 1).reshape(12, -1), attn_out[0].T], axis=1
+    )
+    piece, sent, normed, first_piece, obs_mask = lax.optimization_barrier(
+        (piece, sent, normed, first_piece, obs_mask)
+    )
+    gathered_weights = lax.all_gather(piece, ("c", "z", "y"), axis=0, tiled=True)
+
+    for step in (1, 2, 4):
+        other = lax.ppermute(first_piece, "z", [(k, k ^ step) for k in range(8)])
+        upper = (own_z // step) % 2 == 1
+        low = jnp.where(upper, other, first_piece)
+        high = jnp.where(upper, first_piece, other)
+        first_piece = jnp.concatenate([low, high], axis=0)
+    first_weight = sent_to_all(first_piece, ("y", "c")).reshape(8, 8, 12, -1)
+    first_weight = jnp.moveaxis(first_weight, 0, 1).reshape(D, -1)
     gathered = gather_rows(normed, "mp")
     mask_group = gather_rows(obs_mask, "mp")
+    got = lax.all_to_all(sent, DP, split_axis=0, concat_axis=0, tiled=True)
+    gathered, mask_group, got, first_weight = lax.optimization_barrier(
+        (gathered, mask_group, got, first_weight)
+    )
+    got = got.reshape(peers * READ, 128)
     samples = mask_group.shape[0]
-    allowed = allowed_keys(mask_group)
-    qkv_weight, out_weight, up_weight, down_weight = weights_of(0)
-    projected = jnp.einsum("td,jdc->jtc", gathered, qkv_weight, preferred_element_type=F32)
-    projected = projected.astype(BF16).reshape(3, samples, SEQ, heads, HDIM)
-    context = attend(projected[0], projected[1], projected[2], allowed).reshape(-1, width)
-    residual = residual + summed_on_arrival(mm(context, out_weight).astype(BF16), "mp")
+    projected = mm(gathered, first_weight[:, : 3 * width]).astype(BF16)
+    projected = jnp.moveaxis(projected.reshape(-1, 3, width), 1, 0)
+    projected = projected.reshape(3, samples, SEQ, heads, HDIM)
+    context = attend(projected[0], projected[1], projected[2], allowed_keys(mask_group))
+    partial_value = mm_t(context.reshape(-1, width), first_weight[:, 3 * width :])
+    residual = residual + summed_on_arrival(partial_value.astype(BF16), "mp")
+
+    residual, gathered_weights = lax.optimization_barrier((residual, gathered_weights))
+    sides = gathered_weights.reshape(2, D, -1)
+
+    def weight(side, start, columns):
+        return sides[side, :, start : start + columns]
+
     normed = normalize(residual, norm_gains[1]).astype(BF16)
-    gathered = gather_rows(normed, "mp")
-    hidden = jax.nn.gelu(mm(gathered, up_weight), approximate=True).astype(BF16)
-    residual = residual + summed_on_arrival(mm(hidden, down_weight).astype(BF16), "mp")
-
-    whole = gather_rows(residual.astype(BF16), "mp").astype(F32)
-    qkv_weight, out_weight, up_weight, down_weight = weights_of(1)
-    normed = normalize(whole, norm_gains[2]).astype(BF16)
+    for side in range(2):
+        hidden = jax.nn.gelu(mm(normed, weight(side, 1536, 1536)), approximate=True).astype(BF16)
+        residual = residual + mm_t(hidden, weight(side, 3072, 1536))
+    own_samples = obs_mask.shape[0]
+    normed = normalize(residual, norm_gains[2]).astype(BF16)
     last = slice(SEQ - READ, SEQ)
-    ending = whole.reshape(samples, SEQ, D)[:, last].reshape(-1, D)
-    normed_end = normed.reshape(samples, SEQ, D)[:, last].reshape(-1, D)
-    queries = mm(normed_end, qkv_weight[0]).astype(BF16).reshape(samples, READ, heads, HDIM)
-    key_rows = mm(normed, qkv_weight[1]).astype(BF16).reshape(samples, SEQ, heads, HDIM)
-    value_rows = mm(normed, qkv_weight[2]).astype(BF16).reshape(samples, SEQ, heads, HDIM)
-    context = attend(queries, key_rows, value_rows, allowed[:, last]).reshape(-1, width)
-    ending = ending + summed_for_all(mm(context, out_weight).astype(BF16), "mp")
+    ending = residual.reshape(own_samples, SEQ, D)[:, last].reshape(-1, D)
+    normed_end = normed.reshape(own_samples, SEQ, D)[:, last].reshape(-1, D)
+    allowed = allowed_keys(obs_mask)[:, last]
+    for side in range(2):
+        queries = mm(normed_end, weight(side, 0, 384)).astype(BF16)
+        key_rows = mm(normed, weight(side, 384, 384)).astype(BF16)
+        value_rows = mm(normed, weight(side, 768, 384)).astype(BF16)
+        context = attend(
+            queries.reshape(own_samples, READ, -1, HDIM),
+            key_rows.reshape(own_samples, SEQ, -1, HDIM),
+            value_rows.reshape(own_samples, SEQ, -1, HDIM),
+            allowed,
+        ).reshape(own_samples * READ, -1)
+        ending = ending + mm_t(context, weight(side, 1152, 384))
+    ending = gather_rows(ending.astype(BF16), "mp").astype(F32)
     normed = normalize(ending, norm_gains[3]).astype(BF16)
-    hidden = jax.nn.gelu(mm(normed, up_weight), approximate=True).astype(BF16)
-    ending = ending + summed_for_all(mm(hidden, down_weight).astype(BF16), "mp")
+    partial_value = 0.0
+    for side in range(2):
+        hidden = jax.nn.gelu(mm(normed, weight(side, 4608, 384)), approximate=True).astype(BF16)
+        partial_value = partial_value + mm_t(hidden, weight(side, 4992, 384))
+    ending = ending + summed_for_all(partial_value.astype(BF16), "mp")
     readouts = normalize(ending, norm_gains[4]).astype(BF16).reshape(samples, READ * D)
 
     send = mm(place, readouts).astype(BF16)

time: 304 us -> 253 us (0.83)
  waiting for transfers between devices: 118 us -> 72.8 us
  local copies, waits for them, and re-layouts: 42.7 us -> 25.1 us
  starting transfers between devices: 45.9 us -> 56.9 us
  matrix products: 29.9 us -> 40.2 us
  blocking collectives: 37.2 us -> 32.3 us
  other arithmetic: 13.7 us -> 9.35 us
    all_gather x2 -> x1, waiting for transfers between devices: 67.6 us -> 0.02 us  [on_device(): lax.all_gather(piece, ('c', 'z', 'y'), axis=0, tiled=True)]
    all_to_all x5, waiting for transfers between devices: 12.9 us -> 28.2 us  [sent_to_all(): return lax.all_to_all(copies, axis, split_axis=0, concat_axis=0, tiled=True)]
    unnamed x50, local copies, waits for them, and re-layouts: 18.1 us -> 3.93 us
    dot_general x1 -> x7, matrix products: 2.05 us -> 15.7 us  [mm_t(): return jnp.einsum('tk,dk->td', a, b, preferred_element_type=F32)]
    all_to_all x1, blocking collectives: 19.9 us -> 6.55 us  [on_device(): lax.all_to_all(halves, 'c', split_axis=0, concat_axis=0, tiled=True)]
    ppermute x0 -> x3, starting transfers between devices: none -> 9.82 us  [on_device(): other = lax.ppermute(first_piece, 'z', [(k, k ^ step) for k in range(8)])]
    all_to_all x1, blocking collectives: 17.3 us -> 25.8 us  [sent_to_all(): return lax.all_to_all(copies, axis, split_axis=0, concat_axis=0, tiled=True)]
    all_to_all x1, waiting for transfers between devices: 4.45 us -> 9.31 us  [on_device(): got = lax.all_to_all(sent, DP, split_axis=0, concat_axis=0, tiled=True)]
  transfers between devices with their start and end apart: 11 -> 13, of which waited for: 9 -> 11; matrix products, arithmetic and copies ran while one was open for 17% -> 12% of each run, Pallas kernels for 0% -> 0%
where the time goes in v2:
time: 253 us; the launch traced here: 252 us
  waiting for transfers between devices  72.8 us (29%)
  starting transfers between devices  56.9 us (22%)
  matrix products  40.2 us (16%)
  blocking collectives  32.3 us (13%)
  local copies, waits for them, and re-layouts  25.1 us (10%)
  between operations  15 us (6%)
  other arithmetic  9.35 us (4%)
    all_to_all x5, waiting for transfers between devices, sent_to_all(): return lax.all_to_all(copies, axis, split_axis=0, concat_axis=0, tiled=True)  28.2 us
    all_to_all x1, blocking collectives, sent_to_all(): return lax.all_to_all(copies, axis, split_axis=0, concat_axis=0, tiled=True)  25.8 us
    all_to_all x5, starting transfers between devices, sent_to_all(): return lax.all_to_all(copies, axis, split_axis=0, concat_axis=0, tiled=True)  19.2 us
    dot_general x7, matrix products, mm_t(): return jnp.einsum('tk,dk->td', a, b, preferred_element_type=F32)  15.7 us
    all_to_all x1, waiting for transfers between devices, summed_on_arrival(): lax.all_to_all(pieces, axis, split_axis=0, concat_axis=0, tiled=True)  13.5 us
    all_to_all x1, waiting for transfers between devices, on_device(): features = lax.all_to_all(send, DP, split_axis=0, concat_axis=0, tiled=True)  11.5 us
    dot_general x11, matrix products, mm(): return jnp.dot(a, b, preferred_element_type=F32)  11.1 us
    all_to_all x1, starting transfers between devices, on_device(): got = lax.all_to_all(sent, DP, split_axis=0, concat_axis=0, tiled=True)  10.5 us
  transfers between devices with their start and end apart: 13, of which 11 were waited for; matrix products, arithmetic and copies ran while one was open for 12% of the time, Pallas kernels for 0%

profile of v2, /device:TPU:1, one launch (start us, length us, event | category | flops | bytes accessed | tf_op | source)
XLA Modules:
  0.0 251.7 jit_solution(8811840583016413337)
XLA Ops:
  11.8 4.8 %all-to-all-start = ((bf16[4,12,2304]{2,1,0:T(8,128)(2,1)}), bf16[4,12,2304]{2,1,0:T(8,128)(2,1)S(1)}, u32[]{:S(2)}, u32[]{:S(2)}) async-start(bf16[4,12,2304]{2,1,0:T(8,128)(2,1)} %broadcast_in_dim.64), calls=%async_computation | async-start | bytes 589824 | tf_op jit(solution)/shard_map/all_to_all | solution.py:26
  18.7 3.7 %all-to-all-done = bf16[4,12,2304]{2,1,0:T(8,128)(2,1)S(1)} async-done(((bf16[4,12,2304]{2,1,0:T(8,128)(2,1)}), bf16[4,12,2304]{2,1,0:T(8,128)(2,1)S(1)}, u32[]{:S(2)}, u32[]{:S(2)}) %all-to-all-start) | async-done | bytes 221216 | tf_op jit(solution)/shard_map/all_to_all | solution.py:26
  23.7 6.6 %all_to_all.67 = bf16[2,12,5376]{2,1,0:T(8,128)(2,1)S(1)} all-to-all(bf16[2,12,5376]{2,1,0:T(8,128)(2,1)S(1)} %copy.239), channel_id=1, replica_groups=mesh['z'=8,'y'=4,'c'=2,'mp'=4] {'c'}, dimensions={0} | all-to-all | bytes 516096 | tf_op jit(solution)/shard_map/all_to_all | solution.py:152
  31.1 1.1 collective-permute-start
  32.1 1.7 collective-permute-done
  33.9 2.6 %collective-permute-start.1 = (bf16[24,768]{1,0:T(8,128)(2,1)S(1)}, bf16[24,768]{1,0:T(8,128)(2,1)S(1)}, u32[]{:S(2)}, u32[]{:S(2)}) collective-permute-start(bf16[24,768]{1,0:T(8,128)(2,1)S(1)} %pad_maximum_fusion.3), channel_id=1, source_target_pairs={{0,64},{32,96},{64,0},{96,32},{128,192},{160,224},{192,128},{224,1... | collective-permute-start | bytes 110600 | tf_op jit(solution)/shard_map/ppermute | solution.py:172
  36.5 1.3 collective-permute-done.1
  37.9 6.2 %collective-permute-start.2 = (bf16[48,768]{1,0:T(8,128)(2,1)S(1)}, bf16[48,768]{1,0:T(8,128)(2,1)S(1)}, u32[]{:S(2)}, u32[]{:S(2)}) collective-permute-start(bf16[48,768]{1,0:T(8,128)(2,1)S(1)} %pad_maximum_fusion.2), channel_id=1, source_target_pairs={{0,128},{32,160},{64,192},{96,224},{128,0},{160,32},{192,64},{224,... | collective-permute-start | bytes 221192 | tf_op jit(solution)/shard_map/ppermute | solution.py:172
  44.7 3.2 %all-to-all-start.3 = ((s32[4,1,192]{2,1,0:T(1,128)}), s32[4,1,192]{2,1,0:T(1,128)S(1)}, u32[]{:S(2)}, u32[]{:S(2)}) async-start(s32[4,1,192]{2,1,0:T(1,128)} %reshape.355), calls=%async_computation.3 | async-start | bytes 8192 | tf_op jit(solution)/shard_map/all_to_all | solution.py:26
  48.7 3.4 %all-to-all-done.3 = s32[4,1,192]{2,1,0:T(1,128)S(1)} async-done(((s32[4,1,192]{2,1,0:T(1,128)}), s32[4,1,192]{2,1,0:T(1,128)S(1)}, u32[]{:S(2)}, u32[]{:S(2)}) %all-to-all-start.3) | async-done | bytes 3104 | tf_op jit(solution)/shard_map/all_to_all | solution.py:26
  52.1 10.5 %all-to-all-start.4 = ((bf16[64,2,128]{2,1,0:T(2,128)(2,1)}), bf16[64,2,128]{2,1,0:T(2,128)(2,1)S(1)}, u32[]{:S(2)}, u32[]{:S(2)}) async-start(bf16[64,2,128]{2,1,0:T(2,128)(2,1)} %copy.250), calls=%async_computation.4 | async-start | bytes 65536 | tf_op jit(solution)/shard_map/all_to_all | solution.py:181
  62.6 9.3 %all-to-all-done.4 = bf16[64,2,128]{2,1,0:T(2,128)(2,1)S(1)} async-done(((bf16[64,2,128]{2,1,0:T(2,128)(2,1)}), bf16[64,2,128]{2,1,0:T(2,128)(2,1)S(1)}, u32[]{:S(2)}, u32[]{:S(2)}) %all-to-all-start.4) | async-done | bytes 32800 | tf_op jit(solution)/shard_map/all_to_all | solution.py:181
  72.0 25.8 %all_to_all.68 = bf16[8,96,768]{2,1,0:T(8,128)(2,1)S(1)} all-to-all(bf16[8,96,768]{2,1,0:T(8,128)(2,1)S(1)} %broadcast_in_dim.120), channel_id=1, replica_groups=mesh['z'=8,'y'=4,'c'=2,'mp'=4] {'y','c'}, dimensions={0} | all-to-all | bytes 2359296 | tf_op jit(solution)/shard_map/all_to_all | solution.py:26
  97.8 1.2 broadcast_in_dim.67
  98.9 4.5 %all-to-all-start.2 = ((bf16[4,192,768]{2,1,0:T(8,128)(2,1)}), bf16[4,192,768]{2,1,0:T(8,128)(2,1)}, u32[]{:S(2)}, u32[]{:S(2)}) async-start(bf16[4,192,768]{2,1,0:T(8,128)(2,1)} %broadcast_in_dim.67), calls=%async_computation.2 | async-start | bytes 2359296 | tf_op jit(solution)/shard_map/all_to_all | solution.py:26
  106.0 12.7 %all-to-all-done.2 = bf16[4,192,768]{2,1,0:T(8,128)(2,1)} async-done(((bf16[4,192,768]{2,1,0:T(8,128)(2,1)}), bf16[4,192,768]{2,1,0:T(8,128)(2,1)}, u32[]{:S(2)}, u32[]{:S(2)}) %all-to-all-start.2) | async-done | bytes 1179680 | tf_op jit(solution)/shard_map/all_to_all | solution.py:26
  118.7 2.2 convolution_convert_fusion.3
  121.0 1.4 squeeze.107
  122.4 1.4 squeeze.106
  123.7 1.3 squeeze.105
  125.3 2.8 %fusion.6 = f32[12,3,64,64]{2,3,1,0:T(8,128)} fusion(bf16[12,64,3,64]{1,0,3,2:T(8,128)(2,1)S(1)} %copy-done.2, bf16[12,64,3,64]{1,0,3,2:T(8,128)(2,1)} %squeeze.106, pred[12,64,64]{1,2,0:T(8,128)(4,1)S(1)} %broadcast_or_fusion), kind=kOutput, calls=%fused_computation.18 | convolution fusion | flops 19169280 | bytes 1228800 | tf_op jit(solution)/shard_map/sqhd,skhd->shqk/dot_general | solution.py:67
  128.1 3.0 %fusion.9 = bf16[12,64,3,64]{1,3,2,0:T(8,128)(2,1)} fusion(f32[12,3,64,64]{2,3,1,0:T(8,128)} %fusion.6, bf16[12,64,3,64]{1,0,3,2:T(8,128)(2,1)S(1)} %copy-done.3), kind=kOutput, calls=%fused_computation.22 | convolution fusion | flops 19319104 | bytes 1179648 | tf_op jit(solution)/shard_map/shqk,skhd->sqhd/dot_general | solution.py:72
  131.1 1.5 copy.257
  133.0 1.7 convolution_convert_fusion.2
  134.7 3.9 %all-to-all-start.6 = ((bf16[4,192,768]{2,1,0:T(8,128)(2,1)}), bf16[4,192,768]{2,1,0:T(8,128)(2,1)S(1)}, u32[]{:S(2)}, u32[]{:S(2)}) async-start(bf16[4,192,768]{2,1,0:T(8,128)(2,1)} %bitcast.26), calls=%async_computation.6 | async-start | bytes 2359296 | tf_op jit(solution)/shard_map/all_to_all | solution.py:36
  139.5 13.5 %all-to-all-done.6 = bf16[4,192,768]{2,1,0:T(8,128)(2,1)S(1)} async-done(((bf16[4,192,768]{2,1,0:T(8,128)(2,1)}), bf16[4,192,768]{2,1,0:T(8,128)(2,1)S(1)}, u32[]{:S(2)}, u32[]{:S(2)}) %all-to-all-start.6) | async-done | bytes 1179680 | tf_op jit(solution)/shard_map/all_to_all | solution.py:36
  153.7 3.8 %fusion.7 = f32[192,768]{1,0:T(8,128)S(1)} fusion(f32[192,768]{1,0:T(8,128)S(1)} %convert_add_fusion, bf16[2,768,5376]{2,1,0:T(8,128)(2,1)} %bitcast.248, f32[768]{0:T(1024)S(1)} %get-tuple-element.80, f32[192]{0:T(256)S(1)} %add_rsqrt_fusion.3, f32[192]{0:T(256)S(1)} %broadcast_multiply_fusion.3), kind=kOutput, calls=%fused_computation.20 | convolution fusion | flops 909361152 | bytes 6494208 | tf_op jit(solution)/shard_map/tk,dk->td/dot_general | solution.py:55
  157.5 3.9 %fusion.187 = (f32[192]{0:T(256)S(1)}, f32[192,768]{1,0:T(8,128)S(1)}) fusion(f32[192,768]{1,0:T(8,128)S(1)} %fusion.7, bf16[2,768,5376]{2,1,0:T(8,128)(2,1)} %bitcast.249, f32[192,768]{1,0:T(8,128)S(1)} %convert_add_fusion, f32[768]{0:T(1024)S(1)} %get-tuple-element.80, f32[192]{0:T(256)S(1)} %add_rsqrt_fusion.3, f32[192]{0:T(256)S(1)} %broadcast_multiply_fusion.3), kind=kOutput, calls=%fused_computation.308 | convolution fusion | flops 909508416 | bytes 6493440 | tf_op jit(solution)/shard_map/tk,dk->td/dot_general | solution.py:55
  161.8 1.4 convolution_convert_fusion.9
  163.2 1.4 convolution_convert_fusion.8
  164.6 1.4 convolution_convert_fusion.7
  166.0 1.4 convolution_convert_fusion.6
  167.4 1.2 convolution_convert_fusion.17
  168.7 1.3 convolution_convert_fusion.16
  172.4 1.3 convolution_add_fusion.5
  173.7 1.3 fusion.30
  175.7 3.3 %all-to-all-start.7 = ((bf16[4,6,768]{2,1,0:T(8,128)(2,1)}), bf16[4,6,768]{2,1,0:T(8,128)(2,1)S(1)}, u32[]{:S(2)}, u32[]{:S(2)}) async-start(bf16[4,6,768]{2,1,0:T(8,128)(2,1)} %broadcast_in_dim.126), calls=%async_computation.7 | async-start | bytes 98304 | tf_op jit(solution)/shard_map/all_to_all | solution.py:26
  179.7 3.7 %all-to-all-done.7 = bf16[4,6,768]{2,1,0:T(8,128)(2,1)S(1)} async-done(((bf16[4,6,768]{2,1,0:T(8,128)(2,1)}), bf16[4,6,768]{2,1,0:T(8,128)(2,1)S(1)}, u32[]{:S(2)}, u32[]{:S(2)}) %all-to-all-start.7) | async-done | bytes 36896 | tf_op jit(solution)/shard_map/all_to_all | solution.py:26
  183.8 1.8 fusion.44
  185.5 1.8 fusion.29
  188.1 3.3 %all-to-all-start.8 = ((bf16[4,24,768]{2,1,0:T(8,128)(2,1)}), bf16[4,24,768]{2,1,0:T(8,128)(2,1)S(1)}, u32[]{:S(2)}, u32[]{:S(2)}) async-start(bf16[4,24,768]{2,1,0:T(8,128)(2,1)} %broadcast_in_dim.127), calls=%async_computation.8 | async-start | bytes 294912 | tf_op jit(solution)/shard_map/all_to_all | solution.py:26
  191.6 4.7 %all-to-all-done.8 = bf16[4,24,768]{2,1,0:T(8,128)(2,1)S(1)} async-done(((bf16[4,24,768]{2,1,0:T(8,128)(2,1)}), bf16[4,24,768]{2,1,0:T(8,128)(2,1)S(1)}, u32[]{:S(2)}, u32[]{:S(2)}) %all-to-all-start.8) | async-done | bytes 147488 | tf_op jit(solution)/shard_map/all_to_all | solution.py:26
  199.4 9.1 %all-to-all-start.9 = ((bf16[64,2,768]{2,1,0:T(2,128)(2,1)}), bf16[64,2,768]{2,1,0:T(2,128)(2,1)S(1)}, u32[]{:S(2)}, u32[]{:S(2)}) async-start(bf16[64,2,768]{2,1,0:T(2,128)(2,1)} %reshape.357), calls=%async_computation.9 | async-start | bytes 393216 | tf_op jit(solution)/shard_map/all_to_all | solution.py:231
  209.3 11.5 %all-to-all-done.9 = bf16[64,2,768]{2,1,0:T(2,128)(2,1)S(1)} async-done(((bf16[64,2,768]{2,1,0:T(2,128)(2,1)}), bf16[64,2,768]{2,1,0:T(2,128)(2,1)S(1)}, u32[]{:S(2)}, u32[]{:S(2)}) %all-to-all-start.9) | async-done | bytes 196640 | tf_op jit(solution)/shard_map/all_to_all | solution.py:231
  221.0 1.2 reduce.11
  224.7 1.8 reduce.23
  227.2 4.4 %all-to-all-start.10 = ((bf16[64,2,768]{2,1,0:T(2,128)(2,1)}), bf16[64,2,768]{2,1,0:T(2,128)(2,1)S(1)}, u32[]{:S(2)}, u32[]{:S(2)}) async-start(bf16[64,2,768]{2,1,0:T(2,128)(2,1)} %reshape.359), calls=%async_computation.10 | async-start | bytes 393216 | tf_op jit(solution)/shard_map/all_to_all | solution.py:253
  236.7 7.2 %all-to-all-done.10 = bf16[64,2,768]{2,1,0:T(2,128)(2,1)S(1)} async-done(((bf16[64,2,768]{2,1,0:T(2,128)(2,1)}), bf16[64,2,768]{2,1,0:T(2,128)(2,1)S(1)}, u32[]{:S(2)}, u32[]{:S(2)}) %all-to-all-start.10) | async-done | bytes 196640 | tf_op jit(solution)/shard_map/all_to_all | solution.py:253
  (197 shorter events, 33.3 us)
Async XLA Ops:
  7.2 215.1 %copy-start = (bf16[1,768,256]{2,1,0:T(8,128)(2,1)S(1)}, bf16[1,768,256]{2,1,0:T(8,128)(2,1)}, u32[]{:S(2)}) copy-start(bf16[1,768,256]{2,1,0:T(8,128)(2,1)} %param.30) | copy-start | bytes 1179652
  7.2 9.6 %copy-start.11 = (s32[12,2]{0,1:T(2,128)S(1)}, s32[12,2]{0,1:T(2,128)}, u32[]{:S(2)}) copy-start(s32[12,2]{0,1:T(2,128)} %param.26) | copy-start | bytes 292
  7.2 9.8 %copy-start.5 = (bf16[12,2,56]{2,1,0:T(2,128)(2,1)S(1)}, bf16[12,2,56]{2,1,0:T(2,128)(2,1)}, u32[]{:S(2)}) copy-start(bf16[12,2,56]{2,1,0:T(2,128)(2,1)} %param.28) | copy-start | bytes 8068
  7.2 10.1 %copy-start.7 = (f32[5,768]{1,0:T(8,128)S(1)}, f32[5,768]{1,0:T(8,128)}, u32[]{:S(2)}) copy-start(f32[5,768]{1,0:T(8,128)} %param.20) | copy-start | bytes 46084
  7.2 10.1 %copy-start.1 = (bf16[192,768]{1,0:T(8,128)(2,1)S(1)}, bf16[192,768]{1,0:T(8,128)(2,1)}, u32[]{:S(2)}) copy-start(bf16[192,768]{1,0:T(8,128)(2,1)} %param.18) | copy-start | bytes 884740
  11.1 6.9 %copy-start.9 = (bf16[12,2,56]{2,1,0:T(2,128)(2,1)S(1)}, bf16[12,2,56]{2,1,0:T(2,128)(2,1)}, u32[]{:S(2)}) copy-start(bf16[12,2,56]{2,1,0:T(2,128)(2,1)} %param.27) | copy-start | bytes 8068
  11.1 7.0 %copy-start.10 = (s32[12,1]{0,1:T(1,128)S(1)}, s32[12,1]{0,1:T(1,128)}, u32[]{:S(2)}) copy-start(s32[12,1]{0,1:T(1,128)} %param.25) | copy-start | bytes 148
  11.8 10.5 %all-to-all-start = ((bf16[4,12,2304]{2,1,0:T(8,128)(2,1)}), bf16[4,12,2304]{2,1,0:T(8,128)(2,1)S(1)}, u32[]{:S(2)}, u32[]{:S(2)}) async-start(bf16[4,12,2304]{2,1,0:T(8,128)(2,1)} %broadcast_in_dim.64), calls=%async_computation | async-start | bytes 589824 | tf_op jit(solution)/shard_map/all_to_all | solution.py:26
  16.7 136.7 %all-gather.2.cloned.1.call-start = ((), (), s32[]{:S(2)}) async-start(), calls=%async_computation.11 | async-start | bytes 16773120 | tf_op jit(solution)/shard_map/all_gather | solution.py:169
  23.7 20.3 %copy-start.8 = (s32[3,64]{1,0:T(4,128)S(1)}, s32[3,64]{1,0:T(4,128)}, u32[]{:S(2)}) copy-start(s32[3,64]{1,0:T(4,128)} %param.19) | copy-start | bytes 2308
  31.1 2.8 %collective-permute-start = (bf16[12,768]{1,0:T(8,128)(2,1)S(1)}, bf16[12,768]{1,0:T(8,128)(2,1)S(1)}, u32[]{:S(2)}, u32[]{:S(2)}) collective-permute-start(bf16[12,768]{1,0:T(8,128)(2,1)S(1)} %pad_maximum_fusion.4), channel_id=1, source_target_pairs={{0,32},{32,0},{64,96},{96,64},{128,160},{160,128},{192,224},{224,1... | collective-permute-start | bytes 55304 | tf_op jit(solution)/shard_map/ppermute | solution.py:172
  33.9 3.9 %collective-permute-start.1 = (bf16[24,768]{1,0:T(8,128)(2,1)S(1)}, bf16[24,768]{1,0:T(8,128)(2,1)S(1)}, u32[]{:S(2)}, u32[]{:S(2)}) collective-permute-start(bf16[24,768]{1,0:T(8,128)(2,1)S(1)} %pad_maximum_fusion.3), channel_id=1, source_target_pairs={{0,64},{32,96},{64,0},{96,32},{128,192},{160,224},{192,128},{224,1... | collective-permute-start | bytes 110600 | tf_op jit(solution)/shard_map/ppermute | solution.py:172
  37.9 10.8 %collective-permute-start.2 = (bf16[48,768]{1,0:T(8,128)(2,1)S(1)}, bf16[48,768]{1,0:T(8,128)(2,1)S(1)}, u32[]{:S(2)}, u32[]{:S(2)}) collective-permute-start(bf16[48,768]{1,0:T(8,128)(2,1)S(1)} %pad_maximum_fusion.2), channel_id=1, source_target_pairs={{0,128},{32,160},{64,192},{96,224},{128,0},{160,32},{192,64},{224,... | collective-permute-start | bytes 221192 | tf_op jit(solution)/shard_map/ppermute | solution.py:172
  44.7 7.4 %all-to-all-start.3 = ((s32[4,1,192]{2,1,0:T(1,128)}), s32[4,1,192]{2,1,0:T(1,128)S(1)}, u32[]{:S(2)}, u32[]{:S(2)}) async-start(s32[4,1,192]{2,1,0:T(1,128)} %reshape.355), calls=%async_computation.3 | async-start | bytes 8192 | tf_op jit(solution)/shard_map/all_to_all | solution.py:26
  52.1 19.8 %all-to-all-start.4 = ((bf16[64,2,128]{2,1,0:T(2,128)(2,1)}), bf16[64,2,128]{2,1,0:T(2,128)(2,1)S(1)}, u32[]{:S(2)}, u32[]{:S(2)}) async-start(bf16[64,2,128]{2,1,0:T(2,128)(2,1)} %copy.250), calls=%async_computation.4 | async-start | bytes 65536 | tf_op jit(solution)/shard_map/all_to_all | solution.py:181
  98.9 19.8 %all-to-all-start.2 = ((bf16[4,192,768]{2,1,0:T(8,128)(2,1)}), bf16[4,192,768]{2,1,0:T(8,128)(2,1)}, u32[]{:S(2)}, u32[]{:S(2)}) async-start(bf16[4,192,768]{2,1,0:T(8,128)(2,1)} %broadcast_in_dim.67), calls=%async_computation.2 | async-start | bytes 2359296 | tf_op jit(solution)/shard_map/all_to_all | solution.py:26
  122.4 2.9 %copy-start.2 = (bf16[12,64,3,64]{1,0,3,2:T(8,128)(2,1)S(1)}, bf16[12,64,3,64]{1,0,3,2:T(8,128)(2,1)}, u32[]{:S(2)}) copy-start(bf16[12,64,3,64]{1,0,3,2:T(8,128)(2,1)} %squeeze.107) | copy-start | bytes 884740
  125.3 2.9 %copy-start.3 = (bf16[12,64,3,64]{1,0,3,2:T(8,128)(2,1)S(1)}, bf16[12,64,3,64]{1,0,3,2:T(8,128)(2,1)}, u32[]{:S(2)}) copy-start(bf16[12,64,3,64]{1,0,3,2:T(8,128)(2,1)} %squeeze.105) | copy-start | bytes 884740
  134.7 4.1 %copy-start.15 = (s32[25]{0:T(128)S(1)}, s32[25]{0:T(128)}, u32[]{:S(2)}) copy-start(s32[25]{0:T(128)} %param.29) | copy-start | bytes 304
  134.7 18.3 %all-to-all-start.6 = ((bf16[4,192,768]{2,1,0:T(8,128)(2,1)}), bf16[4,192,768]{2,1,0:T(8,128)(2,1)S(1)}, u32[]{:S(2)}, u32[]{:S(2)}) async-start(bf16[4,192,768]{2,1,0:T(8,128)(2,1)} %bitcast.26), calls=%async_computation.6 | async-start | bytes 2359296 | tf_op jit(solution)/shard_map/all_to_all | solution.py:36
  175.7 7.6 %all-to-all-start.7 = ((bf16[4,6,768]{2,1,0:T(8,128)(2,1)}), bf16[4,6,768]{2,1,0:T(8,128)(2,1)S(1)}, u32[]{:S(2)}, u32[]{:S(2)}) async-start(bf16[4,6,768]{2,1,0:T(8,128)(2,1)} %broadcast_in_dim.126), calls=%async_computation.7 | async-start | bytes 98304 | tf_op jit(solution)/shard_map/all_to_all | solution.py:26
  185.5 5.9 %copy-start.4 = (bf16[1,56,256]{2,1,0:T(8,128)(2,1)S(1)}, bf16[1,56,256]{2,1,0:T(8,128)(2,1)}, u32[]{:S(2)}) copy-start(bf16[1,56,256]{2,1,0:T(8,128)(2,1)} %param.31) | copy-start | bytes 86020
  188.1 8.2 %all-to-all-start.8 = ((bf16[4,24,768]{2,1,0:T(8,128)(2,1)}), bf16[4,24,768]{2,1,0:T(8,128)(2,1)S(1)}, u32[]{:S(2)}, u32[]{:S(2)}) async-start(bf16[4,24,768]{2,1,0:T(8,128)(2,1)} %broadcast_in_dim.127), calls=%async_computation.8 | async-start | bytes 294912 | tf_op jit(solution)/shard_map/all_to_all | solution.py:26
  197.1 12.1 %copy-start.6 = (bf16[1,20,256]{2,1,0:T(8,128)(2,1)S(1)}, bf16[1,20,256]{2,1,0:T(8,128)(2,1)}, u32[]{:S(2)}) copy-start(bf16[1,20,256]{2,1,0:T(8,128)(2,1)} %param.32) | copy-start | bytes 30724
  199.4 21.4 %all-to-all-start.9 = ((bf16[64,2,768]{2,1,0:T(2,128)(2,1)}), bf16[64,2,768]{2,1,0:T(2,128)(2,1)S(1)}, u32[]{:S(2)}, u32[]{:S(2)}) async-start(bf16[64,2,768]{2,1,0:T(2,128)(2,1)} %reshape.357), calls=%async_computation.9 | async-start | bytes 393216 | tf_op jit(solution)/shard_map/all_to_all | solution.py:231
  209.3 13.1 %copy-start.13 = (bf16[1,256,256]{2,1,0:T(8,128)(2,1)S(1)}, bf16[1,256,256]{2,1,0:T(8,128)(2,1)}, u32[]{:S(2)}) copy-start(bf16[1,256,256]{2,1,0:T(8,128)(2,1)} %param.33) | copy-start | bytes 393220
  220.9 1.7 copy-start.12
  222.5 0.8 copy-start.14
  227.2 16.7 %all-to-all-start.10 = ((bf16[64,2,768]{2,1,0:T(2,128)(2,1)}), bf16[64,2,768]{2,1,0:T(2,128)(2,1)S(1)}, u32[]{:S(2)}, u32[]{:S(2)}) async-start(bf16[64,2,768]{2,1,0:T(2,128)(2,1)} %reshape.359), calls=%async_computation.10 | async-start | bytes 393216 | tf_op jit(solution)/shard_map/all_to_all | solution.py:253
Sparse Core Ops, SparseCore 0:
  31.2 103.2 all-gather.1

commit v3 on v2

--- a/solution.py
+++ b/solution.py
@@ -132,8 +132,6 @@
     my_model = lax.axis_index("mp")
     my_owner = lax.axis_index(DP)
 
-    own_z = lax.axis_index("z")
-
     full = jnp.concatenate(
         [
             jnp.moveaxis(attn_in[1], 0, 1).reshape(12, -1),
@@ -160,38 +158,38 @@
     sent = jnp.einsum("es,srf->erf", place, early, preferred_element_type=F32).astype(BF16)
     residual = tokens.astype(F32)
     normed = normalize(residual, norm_gains[0]).astype(BF16)
+    mask_row = jnp.pad(obs_mask.reshape(1, -1).astype(BF16), ((0, 15), (0, D - obs_mask.size)))
+    rows = jnp.concatenate([normed, mask_row], axis=0)
     first_piece = jnp.concatenate(
         [jnp.moveaxis(attn_in[0], 0, 1).reshape(12, -1), attn_out[0].T], axis=1
     )
-    piece, sent, normed, first_piece, obs_mask = lax.optimization_barrier(
-        (piece, sent, normed, first_piece, obs_mask)
-    )
+    piece, rows = lax.optimization_barrier((piece, rows))
     gathered_weights = lax.all_gather(piece, ("c", "z", "y"), axis=0, tiled=True)
 
-    for step in (1, 2, 4):
-        other = lax.ppermute(first_piece, "z", [(k, k ^ step) for k in range(8)])
-        upper = (own_z // step) % 2 == 1
+    for axis, step in (("z", 1), ("z", 2), ("z", 4), ("y", 1), ("y", 2), ("c", 1)):
+        swapped = [(k, k ^ step) for k in range(lax.axis_size(axis))]
+        other = lax.ppermute(first_piece, axis, swapped)
+        upper = (lax.axis_index(axis) // step) % 2 == 1
         low = jnp.where(upper, other, first_piece)
         high = jnp.where(upper, first_piece, other)
         first_piece = jnp.concatenate([low, high], axis=0)
-    first_weight = sent_to_all(first_piece, ("y", "c")).reshape(8, 8, 12, -1)
-    first_weight = jnp.moveaxis(first_weight, 0, 1).reshape(D, -1)
-    gathered = gather_rows(normed, "mp")
-    mask_group = gather_rows(obs_mask, "mp")
-    got = lax.all_to_all(sent, DP, split_axis=0, concat_axis=0, tiled=True)
-    gathered, mask_group, got, first_weight = lax.optimization_barrier(
-        (gathered, mask_group, got, first_weight)
-    )
-    got = got.reshape(peers * READ, 128)
+    first_weight = first_piece.reshape(2, 4, 8, 12, -1).transpose(2, 1, 0, 3, 4).reshape(D, -1)
+    arrived = sent_to_all(rows, "mp")
+    own_rows = normed.shape[0]
+    gathered = arrived[:, :own_rows].reshape(-1, D)
+    mask_group = arrived[:, own_rows, :own_rows].astype(jnp.int32).reshape(-1, SEQ)
     samples = mask_group.shape[0]
     projected = mm(gathered, first_weight[:, : 3 * width]).astype(BF16)
     projected = jnp.moveaxis(projected.reshape(-1, 3, width), 1, 0)
     projected = projected.reshape(3, samples, SEQ, heads, HDIM)
     context = attend(projected[0], projected[1], projected[2], allowed_keys(mask_group))
     partial_value = mm_t(context.reshape(-1, width), first_weight[:, 3 * width :])
-    residual = residual + summed_on_arrival(partial_value.astype(BF16), "mp")
-
-    residual, gathered_weights = lax.optimization_barrier((residual, gathered_weights))
+    partial_value, sent = lax.optimization_barrier((partial_value.astype(BF16), sent))
+    residual = residual + summed_on_arrival(partial_value, "mp")
+    got = lax.all_to_all(sent, DP, split_axis=0, concat_axis=0, tiled=True)
+    got = got.reshape(peers * READ, 128)
+
+    residual, got, gathered_weights = lax.optimization_barrier((residual, got, gathered_weights))
     sides = gathered_weights.reshape(2, D, -1)
 
     def weight(side, start, columns):

time: 253 us -> 232 us (0.917)
  blocking collectives: 32.3 us -> 6.55 us
  starting transfers between devices: 56.9 us -> 68.1 us
  waiting for transfers between devices: 72.8 us -> 67.5 us
    all_to_all x1 -> x0, blocking collectives: 25.8 us -> none  [sent_to_all(): return lax.all_to_all(copies, axis, split_axis=0, concat_axis=0, tiled=True)]
    all_to_all x5 -> x4, waiting for transfers between devices: 28.2 us -> 13.9 us  [sent_to_all(): return lax.all_to_all(copies, axis, split_axis=0, concat_axis=0, tiled=True)]
    ppermute x3 -> x6, starting transfers between devices: 9.82 us -> 18 us  [on_device(): other = lax.ppermute(first_piece, axis, swapped)]
    all_to_all x1, starting transfers between devices: 10.5 us -> 17.7 us  [on_device(): got = lax.all_to_all(sent, DP, split_axis=0, concat_axis=0, tiled=True)]
    ppermute x3 -> x6, waiting for transfers between devices: 3.06 us -> 9.75 us  [on_device(): other = lax.ppermute(first_piece, axis, swapped)]
    all_gather x1, waiting for transfers between devices: 0.02 us -> 5.79 us  [on_device(): lax.all_gather(piece, ('c', 'z', 'y'), axis=0, tiled=True)]
    all_to_all x5 -> x4, starting transfers between devices: 19.2 us -> 15.7 us  [sent_to_all(): return lax.all_to_all(copies, axis, split_axis=0, concat_axis=0, tiled=True)]
    all_to_all x1, waiting for transfers between devices: 13.5 us -> 10.4 us  [summed_on_arrival(): lax.all_to_all(pieces, axis, split_axis=0, concat_axis=0, tiled=True)]
  transfers between devices with their start and end apart: 13 -> 15, of which waited for: 11 -> 13; matrix products, arithmetic and copies ran while one was open for 12% -> 12% of each run, Pallas kernels for 0% -> 0%
where the time goes in v3:
time: 232 us; the launch traced here: 230 us
  starting transfers between devices  68.1 us (29%)
  waiting for transfers between devices  67.5 us (29%)
  matrix products  39.5 us (17%)
  local copies, waits for them, and re-layouts  23.6 us (10%)
  between operations  15.1 us (7%)
  other arithmetic  9.82 us (4%)
  blocking collectives  6.55 us (3%)
    ppermute x6, starting transfers between devices, on_device(): other = lax.ppermute(first_piece, axis, swapped)  18 us
    all_to_all x1, starting transfers between devices, on_device(): got = lax.all_to_all(sent, DP, split_axis=0, concat_axis=0, tiled=True)  17.7 us
    dot_general x7, matrix products, mm_t(): return jnp.einsum('tk,dk->td', a, b, preferred_element_type=F32)  16.8 us
    all_to_all x4, starting transfers between devices, sent_to_all(): return lax.all_to_all(copies, axis, split_axis=0, concat_axis=0, tiled=True)  15.7 us
    all_to_all x4, waiting for transfers between devices, sent_to_all(): return lax.all_to_all(copies, axis, split_axis=0, concat_axis=0, tiled=True)  13.9 us
    all_to_all x1, waiting for transfers between devices, on_device(): features = lax.all_to_all(send, DP, split_axis=0, concat_axis=0, tiled=True)  11.3 us
    dot_general x11, matrix products, mm(): return jnp.dot(a, b, preferred_element_type=F32)  11 us
    all_to_all x1, waiting for transfers between devices, summed_on_arrival(): lax.all_to_all(pieces, axis, split_axis=0, concat_axis=0, tiled=True)  10.4 us
  transfers between devices with their start and end apart: 15, of which 13 were waited for; matrix products, arithmetic and copies ran while one was open for 12% of the time, Pallas kernels for 0%

profile of v3, /device:TPU:1, one launch (start us, length us, event | category | flops | bytes accessed | tf_op | source)
XLA Modules:
  0.0 230.2 jit_solution(15349680349909402788)
XLA Ops:
  11.8 4.8 %all-to-all-start = ((bf16[4,12,2304]{2,1,0:T(8,128)(2,1)}), bf16[4,12,2304]{2,1,0:T(8,128)(2,1)S(1)}, u32[]{:S(2)}, u32[]{:S(2)}) async-start(bf16[4,12,2304]{2,1,0:T(8,128)(2,1)} %broadcast_in_dim.60), calls=%async_computation | async-start | bytes 589824 | tf_op jit(solution)/shard_map/all_to_all | solution.py:26
  18.2 4.2 %all-to-all-done = bf16[4,12,2304]{2,1,0:T(8,128)(2,1)S(1)} async-done(((bf16[4,12,2304]{2,1,0:T(8,128)(2,1)}), bf16[4,12,2304]{2,1,0:T(8,128)(2,1)S(1)}, u32[]{:S(2)}, u32[]{:S(2)}) %all-to-all-start) | async-done | bytes 221216 | tf_op jit(solution)/shard_map/all_to_all | solution.py:26
  23.7 6.6 %all_to_all.57 = bf16[2,12,5376]{2,1,0:T(8,128)(2,1)S(1)} all-to-all(bf16[2,12,5376]{2,1,0:T(8,128)(2,1)S(1)} %copy.236), channel_id=1, replica_groups=mesh['z'=8,'y'=4,'c'=2,'mp'=4] {'c'}, dimensions={0} | all-to-all | bytes 516096 | tf_op jit(solution)/shard_map/all_to_all | solution.py:150
  32.7 1.3 collective-permute-done
  34.1 2.6 %collective-permute-start.1 = (bf16[24,768]{1,0:T(8,128)(2,1)S(1)}, bf16[24,768]{1,0:T(8,128)(2,1)S(1)}, u32[]{:S(2)}, u32[]{:S(2)}) collective-permute-start(bf16[24,768]{1,0:T(8,128)(2,1)S(1)} %pad_maximum_fusion.6), channel_id=1, source_target_pairs={{0,64},{32,96},{64,0},{96,32},{128,192},{160,224},{192,128},{224,1... | collective-permute-start | bytes 110600 | tf_op jit(solution)/shard_map/ppermute | solution.py:171
  36.7 1.3 collective-permute-done.1
  38.1 6.2 %collective-permute-start.2 = (bf16[48,768]{1,0:T(8,128)(2,1)S(1)}, bf16[48,768]{1,0:T(8,128)(2,1)S(1)}, u32[]{:S(2)}, u32[]{:S(2)}) collective-permute-start(bf16[48,768]{1,0:T(8,128)(2,1)S(1)} %pad_maximum_fusion.5), channel_id=1, source_target_pairs={{0,128},{32,160},{64,192},{96,224},{128,0},{160,32},{192,64},{224,... | collective-permute-start | bytes 221192 | tf_op jit(solution)/shard_map/ppermute | solution.py:171
  44.5 2.4 %collective-permute-done.2 = bf16[48,768]{1,0:T(8,128)(2,1)S(1)} collective-permute-done((bf16[48,768]{1,0:T(8,128)(2,1)S(1)}, bf16[48,768]{1,0:T(8,128)(2,1)S(1)}, u32[]{:S(2)}, u32[]{:S(2)}) %collective-permute-start.2) | collective-permute-done | bytes 73760 | tf_op jit(solution)/shard_map/ppermute | solution.py:171
  46.9 1.3 collective-permute-start.3
  48.3 1.1 broadcast_in_dim.61
  49.5 3.5 %all-to-all-start.2 = ((bf16[4,208,768]{2,1,0:T(8,128)(2,1)}), bf16[4,208,768]{2,1,0:T(8,128)(2,1)S(1)}, u32[]{:S(2)}, u32[]{:S(2)}) async-start(bf16[4,208,768]{2,1,0:T(8,128)(2,1)} %broadcast_in_dim.61), calls=%async_computation.2 | async-start | bytes 2555904 | tf_op jit(solution)/shard_map/all_to_all | solution.py:26
  53.1 3.1 %collective-permute-start.4 = (bf16[192,768]{1,0:T(8,128)(2,1)S(1)}, bf16[192,768]{1,0:T(8,128)(2,1)S(1)}, u32[]{:S(2)}, u32[]{:S(2)}) collective-permute-start(bf16[192,768]{1,0:T(8,128)(2,1)S(1)} %pad_maximum_fusion.2), channel_id=1, source_target_pairs={{0,16},{8,24},{16,0},{24,8},{1,17},{9,25},{17,1},{25,9},{2,18},{10... | collective-permute-start | bytes 884744 | tf_op jit(solution)/shard_map/ppermute | solution.py:171
  57.1 4.7 %collective-permute-done.4 = bf16[192,768]{1,0:T(8,128)(2,1)S(1)} collective-permute-done((bf16[192,768]{1,0:T(8,128)(2,1)S(1)}, bf16[192,768]{1,0:T(8,128)(2,1)S(1)}, u32[]{:S(2)}, u32[]{:S(2)}) %collective-permute-start.4) | collective-permute-done | bytes 294944 | tf_op jit(solution)/shard_map/ppermute | solution.py:171
  62.0 3.9 %collective-permute-start.5 = (bf16[384,768]{1,0:T(8,128)(2,1)S(1)}, bf16[384,768]{1,0:T(8,128)(2,1)S(1)}, u32[]{:S(2)}, u32[]{:S(2)}) collective-permute-start(bf16[384,768]{1,0:T(8,128)(2,1)S(1)} %pad_maximum_fusion.1), channel_id=1, source_target_pairs={{0,4},{4,0},{1,5},{5,1},{2,6},{6,2},{3,7},{7,3},{8,12},{12,8},{9,1... | collective-permute-start | bytes 1769480 | tf_op jit(solution)/shard_map/ppermute | solution.py:171
  65.9 1.3 all-to-all-done.2
  69.9 1.2 reshape.355
  71.6 2.1 convolution_convert_fusion.3
  74.8 1.4 squeeze.106
  76.2 1.5 fusion.6
  77.7 2.1 fusion.9
  80.6 2.8 %convolution_convert_fusion.2 = bf16[768,768]{1,0:T(8,128)(2,1)} fusion(bf16[768,192]{0,1:T(8,128)(2,1)S(1)} %reshape.357, bf16[768,768]{1,0:T(8,128)(2,1)} %reshape.355), kind=kOutput, calls=%fused_computation.14 | convolution fusion | flops 227082240 | bytes 1867776 | tf_op jit(solution)/shard_map/tk,dk->td/dot_general | solution.py:55
  83.4 3.7 %all-to-all-start.3 = ((bf16[4,192,768]{2,1,0:T(8,128)(2,1)}), bf16[4,192,768]{2,1,0:T(8,128)(2,1)S(1)}, u32[]{:S(2)}, u32[]{:S(2)}) async-start(bf16[4,192,768]{2,1,0:T(8,128)(2,1)} %bitcast.24), calls=%async_computation.3 | async-start | bytes 2359296 | tf_op jit(solution)/shard_map/all_to_all | solution.py:36
  88.7 10.4 %all-to-all-done.3 = bf16[4,192,768]{2,1,0:T(8,128)(2,1)S(1)} async-done(((bf16[4,192,768]{2,1,0:T(8,128)(2,1)}), bf16[4,192,768]{2,1,0:T(8,128)(2,1)S(1)}, u32[]{:S(2)}, u32[]{:S(2)}) %all-to-all-start.3) | async-done | bytes 1179680 | tf_op jit(solution)/shard_map/all_to_all | solution.py:36
  99.1 17.7 %all-to-all-start.4 = ((bf16[64,2,128]{2,1,0:T(2,128)(2,1)}), bf16[64,2,128]{2,1,0:T(2,128)(2,1)S(1)}, u32[]{:S(2)}, u32[]{:S(2)}) async-start(bf16[64,2,128]{2,1,0:T(2,128)(2,1)} %copy.253), calls=%async_computation.4 | async-start | bytes 65536 | tf_op jit(solution)/shard_map/all_to_all | solution.py:189
  117.0 9.3 %all-to-all-done.4 = bf16[64,2,128]{2,1,0:T(2,128)(2,1)S(1)} async-done(((bf16[64,2,128]{2,1,0:T(2,128)(2,1)}), bf16[64,2,128]{2,1,0:T(2,128)(2,1)S(1)}, u32[]{:S(2)}, u32[]{:S(2)}) %all-to-all-start.4) | async-done | bytes 32800 | tf_op jit(solution)/shard_map/all_to_all | solution.py:189
  126.3 5.8 %all-gather.2.cloned.1.call-done = bf16[1536,5376]{1,0:T(8,128)(2,1)} async-done(((bf16[24,5376]{1,0:T(8,128)(2,1)}), bf16[1536,5376]{1,0:T(8,128)(2,1)}) %all-gather.2.cloned.1.call-update) | async-done | bytes 16515088 | tf_op jit(solution)/shard_map/all_gather | solution.py:167
  132.5 3.8 %fusion.7 = f32[192,768]{1,0:T(8,128)S(1)} fusion(f32[192,768]{1,0:T(8,128)S(1)} %convert_add_fusion, bf16[2,768,5376]{2,1,0:T(8,128)(2,1)} %bitcast.247, f32[768]{0:T(1024)S(1)} %copy-done.15, f32[192]{0:T(256)S(1)} %add_rsqrt_fusion.3, f32[192]{0:T(256)S(1)} %broadcast_multiply_fusion.3), kind=kOutput, calls=%fused_computation.20 | convolution fusion | flops 909361152 | bytes 6494208 | tf_op jit(solution)/shard_map/tk,dk->td/dot_general | solution.py:55
  136.3 3.9 %fusion.189 = (f32[192]{0:T(256)S(1)}, f32[192,768]{1,0:T(8,128)S(1)}) fusion(f32[192,768]{1,0:T(8,128)S(1)} %fusion.7, bf16[2,768,5376]{2,1,0:T(8,128)(2,1)} %bitcast.248, f32[192,768]{1,0:T(8,128)S(1)} %convert_add_fusion, f32[768]{0:T(1024)S(1)} %copy-done.15, f32[192]{0:T(256)S(1)} %add_rsqrt_fusion.3, f32[192]{0:T(256)S(1)} %broadcast_multiply_fusion.3), kind=kOutput, calls=%fused_computation.322 | convolution fusion | flops 909508416 | bytes 6493440 | tf_op jit(solution)/shard_map/tk,dk->td/dot_general | solution.py:55
  140.6 1.4 convolution_convert_fusion.9
  142.0 1.4 convolution_convert_fusion.8
  143.4 1.4 convolution_convert_fusion.7
  144.7 1.4 convolution_convert_fusion.6
  146.2 1.2 convolution_convert_fusion.17
  147.4 1.3 convolution_convert_fusion.16
  151.1 1.3 convolution_add_fusion.5
  152.4 1.3 fusion.30
  154.4 4.0 %all-to-all-start.5 = ((bf16[4,6,768]{2,1,0:T(8,128)(2,1)}), bf16[4,6,768]{2,1,0:T(8,128)(2,1)S(1)}, u32[]{:S(2)}, u32[]{:S(2)}) async-start(bf16[4,6,768]{2,1,0:T(8,128)(2,1)} %broadcast_in_dim.118), calls=%async_computation.5 | async-start | bytes 98304 | tf_op jit(solution)/shard_map/all_to_all | solution.py:26
  159.1 3.7 %all-to-all-done.5 = bf16[4,6,768]{2,1,0:T(8,128)(2,1)S(1)} async-done(((bf16[4,6,768]{2,1,0:T(8,128)(2,1)}), bf16[4,6,768]{2,1,0:T(8,128)(2,1)S(1)}, u32[]{:S(2)}, u32[]{:S(2)}) %all-to-all-start.5) | async-done | bytes 36896 | tf_op jit(solution)/shard_map/all_to_all | solution.py:26
  163.2 1.8 fusion.45
  165.0 1.8 fusion.29
  167.5 3.3 %all-to-all-start.6 = ((bf16[4,24,768]{2,1,0:T(8,128)(2,1)}), bf16[4,24,768]{2,1,0:T(8,128)(2,1)S(1)}, u32[]{:S(2)}, u32[]{:S(2)}) async-start(bf16[4,24,768]{2,1,0:T(8,128)(2,1)} %broadcast_in_dim.119), calls=%async_computation.6 | async-start | bytes 294912 | tf_op jit(solution)/shard_map/all_to_all | solution.py:26
  171.0 4.7 %all-to-all-done.6 = bf16[4,24,768]{2,1,0:T(8,128)(2,1)S(1)} async-done(((bf16[4,24,768]{2,1,0:T(8,128)(2,1)}), bf16[4,24,768]{2,1,0:T(8,128)(2,1)S(1)}, u32[]{:S(2)}, u32[]{:S(2)}) %all-to-all-start.6) | async-done | bytes 147488 | tf_op jit(solution)/shard_map/all_to_all | solution.py:26
  178.9 8.6 %all-to-all-start.7 = ((bf16[64,2,768]{2,1,0:T(2,128)(2,1)}), bf16[64,2,768]{2,1,0:T(2,128)(2,1)S(1)}, u32[]{:S(2)}, u32[]{:S(2)}) async-start(bf16[64,2,768]{2,1,0:T(2,128)(2,1)} %reshape.388), calls=%async_computation.7 | async-start | bytes 393216 | tf_op jit(solution)/shard_map/all_to_all | solution.py:229
  188.2 11.3 %all-to-all-done.7 = bf16[64,2,768]{2,1,0:T(2,128)(2,1)S(1)} async-done(((bf16[64,2,768]{2,1,0:T(2,128)(2,1)}), bf16[64,2,768]{2,1,0:T(2,128)(2,1)S(1)}, u32[]{:S(2)}, u32[]{:S(2)}) %all-to-all-start.7) | async-done | bytes 196640 | tf_op jit(solution)/shard_map/all_to_all | solution.py:229
  199.6 1.1 reduce.12
  203.3 1.8 reduce.24
  205.8 4.5 %all-to-all-start.8 = ((bf16[64,2,768]{2,1,0:T(2,128)(2,1)}), bf16[64,2,768]{2,1,0:T(2,128)(2,1)S(1)}, u32[]{:S(2)}, u32[]{:S(2)}) async-start(bf16[64,2,768]{2,1,0:T(2,128)(2,1)} %reshape.390), calls=%async_computation.8 | async-start | bytes 393216 | tf_op jit(solution)/shard_map/all_to_all | solution.py:251
  215.3 7.1 %all-to-all-done.8 = bf16[64,2,768]{2,1,0:T(2,128)(2,1)S(1)} async-done(((bf16[64,2,768]{2,1,0:T(2,128)(2,1)}), bf16[64,2,768]{2,1,0:T(2,128)(2,1)S(1)}, u32[]{:S(2)}, u32[]{:S(2)}) %all-to-all-start.8) | async-done | bytes 196640 | tf_op jit(solution)/shard_map/all_to_all | solution.py:251
  (223 shorter events, 36.9 us)
Async XLA Ops:
  7.2 193.7 %copy-start = (bf16[1,768,256]{2,1,0:T(8,128)(2,1)S(1)}, bf16[1,768,256]{2,1,0:T(8,128)(2,1)}, u32[]{:S(2)}) copy-start(bf16[1,768,256]{2,1,0:T(8,128)(2,1)} %param.30) | copy-start | bytes 1179652
  7.2 9.5 %copy-start.11 = (f32[5,768]{1,0:T(8,128)S(1)}, f32[5,768]{1,0:T(8,128)}, u32[]{:S(2)}) copy-start(f32[5,768]{1,0:T(8,128)} %param.20) | copy-start | bytes 46084
  7.2 10.2 %copy-start.2 = (bf16[192,768]{1,0:T(8,128)(2,1)S(1)}, bf16[192,768]{1,0:T(8,128)(2,1)}, u32[]{:S(2)}) copy-start(bf16[192,768]{1,0:T(8,128)(2,1)} %param.18) | copy-start | bytes 884740
  11.1 6.9 %copy-start.12 = (s32[3,64]{1,0:T(4,128)S(1)}, s32[3,64]{1,0:T(4,128)}, u32[]{:S(2)}) copy-start(s32[3,64]{1,0:T(4,128)} %param.19) | copy-start | bytes 2308
  11.8 10.5 %all-to-all-start = ((bf16[4,12,2304]{2,1,0:T(8,128)(2,1)}), bf16[4,12,2304]{2,1,0:T(8,128)(2,1)S(1)}, u32[]{:S(2)}, u32[]{:S(2)}) async-start(bf16[4,12,2304]{2,1,0:T(8,128)(2,1)} %broadcast_in_dim.60), calls=%async_computation | async-start | bytes 589824 | tf_op jit(solution)/shard_map/all_to_all | solution.py:26
  16.7 115.5 %all-gather.2.cloned.1.call-start = ((), (), s32[]{:S(2)}) async-start(), calls=%async_computation.9 | async-start | bytes 16773120 | tf_op jit(solution)/shard_map/all_gather | solution.py:167
  23.7 8.6 %copy-start.20 = (s32[12,2]{0,1:T(2,128)S(1)}, s32[12,2]{0,1:T(2,128)}, u32[]{:S(2)}) copy-start(s32[12,2]{0,1:T(2,128)} %param.26) | copy-start | bytes 292
  23.7 20.6 %copy-start.8 = (bf16[12,2,56]{2,1,0:T(2,128)(2,1)S(1)}, bf16[12,2,56]{2,1,0:T(2,128)(2,1)}, u32[]{:S(2)}) copy-start(bf16[12,2,56]{2,1,0:T(2,128)(2,1)} %param.28) | copy-start | bytes 8068
  30.3 18.0 %copy-start.14 = (bf16[12,2,56]{2,1,0:T(2,128)(2,1)S(1)}, bf16[12,2,56]{2,1,0:T(2,128)(2,1)}, u32[]{:S(2)}) copy-start(bf16[12,2,56]{2,1,0:T(2,128)(2,1)} %param.27) | copy-start | bytes 8068
  31.3 2.7 %collective-permute-start = (bf16[12,768]{1,0:T(8,128)(2,1)S(1)}, bf16[12,768]{1,0:T(8,128)(2,1)S(1)}, u32[]{:S(2)}, u32[]{:S(2)}) collective-permute-start(bf16[12,768]{1,0:T(8,128)(2,1)S(1)} %pad_maximum_fusion.7), channel_id=1, source_target_pairs={{0,32},{32,0},{64,96},{96,64},{128,160},{160,128},{192,224},{224,1... | collective-permute-start | bytes 55304 | tf_op jit(solution)/shard_map/ppermute | solution.py:171
  34.1 3.9 %collective-permute-start.1 = (bf16[24,768]{1,0:T(8,128)(2,1)S(1)}, bf16[24,768]{1,0:T(8,128)(2,1)S(1)}, u32[]{:S(2)}, u32[]{:S(2)}) collective-permute-start(bf16[24,768]{1,0:T(8,128)(2,1)S(1)} %pad_maximum_fusion.6), channel_id=1, source_target_pairs={{0,64},{32,96},{64,0},{96,32},{128,192},{160,224},{192,128},{224,1... | collective-permute-start | bytes 110600 | tf_op jit(solution)/shard_map/ppermute | solution.py:171
  38.1 8.8 %collective-permute-start.2 = (bf16[48,768]{1,0:T(8,128)(2,1)S(1)}, bf16[48,768]{1,0:T(8,128)(2,1)S(1)}, u32[]{:S(2)}, u32[]{:S(2)}) collective-permute-start(bf16[48,768]{1,0:T(8,128)(2,1)S(1)} %pad_maximum_fusion.5), channel_id=1, source_target_pairs={{0,128},{32,160},{64,192},{96,224},{128,0},{160,32},{192,64},{224,... | collective-permute-start | bytes 221192 | tf_op jit(solution)/shard_map/ppermute | solution.py:171
  46.9 6.1 %collective-permute-start.3 = (bf16[96,768]{1,0:T(8,128)(2,1)S(1)}, bf16[96,768]{1,0:T(8,128)(2,1)S(1)}, u32[]{:S(2)}, u32[]{:S(2)}) collective-permute-start(bf16[96,768]{1,0:T(8,128)(2,1)S(1)} %pad_maximum_fusion.4), channel_id=1, source_target_pairs={{0,8},{8,0},{16,24},{24,16},{1,9},{9,1},{17,25},{25,17},{2,10},{10... | collective-permute-start | bytes 442376 | tf_op jit(solution)/shard_map/ppermute | solution.py:171
  49.5 17.7 %all-to-all-start.2 = ((bf16[4,208,768]{2,1,0:T(8,128)(2,1)}), bf16[4,208,768]{2,1,0:T(8,128)(2,1)S(1)}, u32[]{:S(2)}, u32[]{:S(2)}) async-start(bf16[4,208,768]{2,1,0:T(8,128)(2,1)} %broadcast_in_dim.61), calls=%async_computation.2 | async-start | bytes 2555904 | tf_op jit(solution)/shard_map/all_to_all | solution.py:26
  53.0 3.2 %copy-start.18 = (s32[12,1]{0,1:T(1,128)S(1)}, s32[12,1]{0,1:T(1,128)}, u32[]{:S(2)}) copy-start(s32[12,1]{0,1:T(1,128)} %param.25) | copy-start | bytes 148
  53.1 8.7 %collective-permute-start.4 = (bf16[192,768]{1,0:T(8,128)(2,1)S(1)}, bf16[192,768]{1,0:T(8,128)(2,1)S(1)}, u32[]{:S(2)}, u32[]{:S(2)}) collective-permute-start(bf16[192,768]{1,0:T(8,128)(2,1)S(1)} %pad_maximum_fusion.2), channel_id=1, source_target_pairs={{0,16},{8,24},{16,0},{24,8},{1,17},{9,25},{17,1},{25,9},{2,18},{10... | collective-permute-start | bytes 884744 | tf_op jit(solution)/shard_map/ppermute | solution.py:171
  62.0 7.1 %collective-permute-start.5 = (bf16[384,768]{1,0:T(8,128)(2,1)S(1)}, bf16[384,768]{1,0:T(8,128)(2,1)S(1)}, u32[]{:S(2)}, u32[]{:S(2)}) collective-permute-start(bf16[384,768]{1,0:T(8,128)(2,1)S(1)} %pad_maximum_fusion.1), channel_id=1, source_target_pairs={{0,4},{4,0},{1,5},{5,1},{2,6},{6,2},{3,7},{7,3},{8,12},{12,8},{9,1... | collective-permute-start | bytes 1769480 | tf_op jit(solution)/shard_map/ppermute | solution.py:171
  65.9 1.4 copy-start.16
  67.2 1.1 copy-start.1
  69.9 1.7 slice-start
  74.3 1.9 copy-start.5
  76.2 1.5 copy-start.4
  83.4 3.9 %copy-start.24 = (s32[25]{0:T(128)S(1)}, s32[25]{0:T(128)}, u32[]{:S(2)}) copy-start(s32[25]{0:T(128)} %param.29) | copy-start | bytes 304
  83.4 4.5 %copy-start.19 = (s32[12,1]{0,1:T(1,128)S(1)}, s32[12,1]{0,1:T(1,128)}, u32[]{:S(2)}) copy-start(s32[12,1]{0,1:T(1,128)} %param.25) | copy-start | bytes 148
  83.4 4.6 %copy-start.13 = (s32[3,64]{1,0:T(4,128)S(1)}, s32[3,64]{1,0:T(4,128)}, u32[]{:S(2)}) copy-start(s32[3,64]{1,0:T(4,128)} %param.19) | copy-start | bytes 2308
  83.4 4.6 %copy-start.17 = (pred[64]{0:T(512)(128)(4,1)S(1)}, pred[64]{0:T(512)(128)(4,1)}, u32[]{:S(2)}) copy-start(pred[64]{0:T(512)(128)(4,1)} %copy-done.16) | copy-start | bytes 196
  83.4 4.6 %copy-start.6 = (bf16[64,2,128]{2,0,1:T(8,128)(2,1)S(1)}, bf16[64,2,128]{2,0,1:T(8,128)(2,1)}, u32[]{:S(2)}) copy-start(bf16[64,2,128]{2,0,1:T(8,128)(2,1)} %convolution_convert_fusion.13) | copy-start | bytes 98308
  83.4 15.7 %all-to-all-start.3 = ((bf16[4,192,768]{2,1,0:T(8,128)(2,1)}), bf16[4,192,768]{2,1,0:T(8,128)(2,1)S(1)}, u32[]{:S(2)}, u32[]{:S(2)}) async-start(bf16[4,192,768]{2,1,0:T(8,128)(2,1)} %bitcast.24), calls=%async_computation.3 | async-start | bytes 2359296 | tf_op jit(solution)/shard_map/all_to_all | solution.py:36
  87.1 29.8 %copy-start.3 = (bf16[192,768]{1,0:T(8,128)(2,1)S(1)}, bf16[192,768]{1,0:T(8,128)(2,1)}, u32[]{:S(2)}) copy-start(bf16[192,768]{1,0:T(8,128)(2,1)} %param.18) | copy-start | bytes 884740
  99.1 27.2 %all-to-all-start.4 = ((bf16[64,2,128]{2,1,0:T(2,128)(2,1)}), bf16[64,2,128]{2,1,0:T(2,128)(2,1)S(1)}, u32[]{:S(2)}, u32[]{:S(2)}) async-start(bf16[64,2,128]{2,1,0:T(2,128)(2,1)} %copy.253), calls=%async_computation.4 | async-start | bytes 65536 | tf_op jit(solution)/shard_map/all_to_all | solution.py:189
  117.0 15.5 %copy-start.15 = (f32[768]{0:T(1024)S(1)}, f32[768]{0:T(1024)}, u32[]{:S(2)}) copy-start(f32[768]{0:T(1024)} %get-tuple-element.72) | copy-start | bytes 9220
  150.7 12.4 %copy-start.9 = (f32[768]{0:T(1024)S(1)}, f32[768]{0:T(1024)}, u32[]{:S(2)}) copy-start(f32[768]{0:T(1024)} %get-tuple-element.74) | copy-start | bytes 9220
  154.4 8.4 %all-to-all-start.5 = ((bf16[4,6,768]{2,1,0:T(8,128)(2,1)}), bf16[4,6,768]{2,1,0:T(8,128)(2,1)S(1)}, u32[]{:S(2)}, u32[]{:S(2)}) async-start(bf16[4,6,768]{2,1,0:T(8,128)(2,1)} %broadcast_in_dim.118), calls=%async_computation.5 | async-start | bytes 98304 | tf_op jit(solution)/shard_map/all_to_all | solution.py:26
  165.0 5.9 %copy-start.7 = (bf16[1,56,256]{2,1,0:T(8,128)(2,1)S(1)}, bf16[1,56,256]{2,1,0:T(8,128)(2,1)}, u32[]{:S(2)}) copy-start(bf16[1,56,256]{2,1,0:T(8,128)(2,1)} %param.31) | copy-start | bytes 86020
  167.5 8.2 %all-to-all-start.6 = ((bf16[4,24,768]{2,1,0:T(8,128)(2,1)}), bf16[4,24,768]{2,1,0:T(8,128)(2,1)S(1)}, u32[]{:S(2)}, u32[]{:S(2)}) async-start(bf16[4,24,768]{2,1,0:T(8,128)(2,1)} %broadcast_in_dim.119), calls=%async_computation.6 | async-start | bytes 294912 | tf_op jit(solution)/shard_map/all_to_all | solution.py:26
  176.4 11.5 %copy-start.10 = (bf16[1,20,256]{2,1,0:T(8,128)(2,1)S(1)}, bf16[1,20,256]{2,1,0:T(8,128)(2,1)}, u32[]{:S(2)}) copy-start(bf16[1,20,256]{2,1,0:T(8,128)(2,1)} %param.32) | copy-start | bytes 30724
  178.9 20.6 %all-to-all-start.7 = ((bf16[64,2,768]{2,1,0:T(2,128)(2,1)}), bf16[64,2,768]{2,1,0:T(2,128)(2,1)S(1)}, u32[]{:S(2)}, u32[]{:S(2)}) async-start(bf16[64,2,768]{2,1,0:T(2,128)(2,1)} %reshape.388), calls=%async_computation.7 | async-start | bytes 393216 | tf_op jit(solution)/shard_map/all_to_all | solution.py:229
  188.2 12.9 %copy-start.22 = (bf16[1,256,256]{2,1,0:T(8,128)(2,1)S(1)}, bf16[1,256,256]{2,1,0:T(8,128)(2,1)}, u32[]{:S(2)}) copy-start(bf16[1,256,256]{2,1,0:T(8,128)(2,1)} %param.33) | copy-start | bytes 393220
  199.6 1.7 copy-start.21
  201.1 0.8 copy-start.23
  205.8 16.6 %all-to-all-start.8 = ((bf16[64,2,768]{2,1,0:T(2,128)(2,1)}), bf16[64,2,768]{2,1,0:T(2,128)(2,1)S(1)}, u32[]{:S(2)}, u32[]{:S(2)}) async-start(bf16[64,2,768]{2,1,0:T(2,128)(2,1)} %reshape.390), calls=%async_computation.8 | async-start | bytes 393216 | tf_op jit(solution)/shard_map/all_to_all | solution.py:251
Sparse Core Ops, SparseCore 0:
  31.2 100.8 all-gather.1

commit v4 on v3

--- a/solution.py
+++ b/solution.py
@@ -3,6 +3,8 @@
 import jax
 import jax.numpy as jnp
 from jax import lax
+from jax.experimental import pallas as pl
+from jax.experimental.pallas import tpu as pltpu
 from jax.sharding import Mesh, PartitionSpec as P
 
 D = 768
@@ -71,6 +73,115 @@
     shares = (weights / jnp.sum(weights, axis=-1, keepdims=True)).astype(BF16)
     context = jnp.einsum("shqk,skhd->sqhd", shares, value_rows, preferred_element_type=F32)
     return context.astype(BF16)
+
+
+def nt(a, b):
+    return lax.dot_general(a, b, (((1,), (1,)), ((), ())), preferred_element_type=F32)
+
+
+def trunk_rows_kernel(res_ref, mask_ref, gain_ref, all_ref, out_ref, mlp, att, mlp_sem, att_sem):
+    def block(side, part):
+        return pltpu.make_async_copy(
+            all_ref.at[pl.ds(side * D, D), pl.ds(1536 * (part + 1), 1536)],
+            mlp.at[side, part],
+            mlp_sem.at[side, part],
+        )
+
+    def attention(side):
+        return pltpu.make_async_copy(
+            all_ref.at[pl.ds(side * D, D), pl.ds(0, 1536)], att.at[side], att_sem.at[side]
+        )
+
+    for side in range(2):
+        for part in range(2):
+            block(side, part).start()
+    for side in range(2):
+        attention(side).start()
+    residual = res_ref[...]
+    normed = normalize(residual, gain_ref[1:2, :]).astype(BF16)
+    for side in range(2):
+        block(side, 0).wait()
+        hidden = jax.nn.gelu(mm(normed, mlp[side, 0]), approximate=True).astype(BF16)
+        block(side, 1).wait()
+        residual = residual + nt(hidden, mlp[side, 1])
+    normed = normalize(residual, gain_ref[2:3, :])
+    ends = [residual[SEQ * k + SEQ - READ : SEQ * (k + 1)] for k in (0, 1, 2, 2)]
+    ending = jnp.concatenate(ends, axis=0)
+    ends = [normed[SEQ * k + SEQ - READ : SEQ * (k + 1)] for k in (0, 1, 2, 2)]
+    normed_end = jnp.concatenate(ends, axis=0).astype(BF16)
+    normed = normed.astype(BF16)
+    rows, keys, width = 48, residual.shape[0], 384
+    row = lax.broadcasted_iota(jnp.int32, (rows, keys), 0) % 8
+    key = lax.broadcasted_iota(jnp.int32, (rows, keys), 1)
+    place = key % SEQ
+    seen = (mask_ref[...] == 1) & (place < SEQ - READ)
+    allowed = (key // SEQ == jnp.minimum(row // READ, 2)) & (
+        seen | (place == SEQ - READ + row % READ)
+    )
+    own_head = (
+        lax.broadcasted_iota(jnp.int32, (rows, width), 0) // 8
+        == lax.broadcasted_iota(jnp.int32, (rows, width), 1) // HDIM
+    )
+    for side in range(2):
+        attention(side).wait()
+        queries = mm(normed_end, att[side, :, 0:384]).astype(BF16).astype(F32)
+        key_rows = mm(normed, att[side, :, 384:768]).astype(BF16)
+        value_rows = mm(normed, att[side, :, 768:1152]).astype(BF16)
+        spread = jnp.where(own_head, jnp.concatenate([queries] * 6, axis=0), 0.0).astype(BF16)
+        scores = nt(spread, key_rows) * HDIM ** (-0.5)
+        weights = jnp.where(allowed, jnp.exp(scores), 0.0)
+        shares = (weights / jnp.sum(weights, axis=-1, keepdims=True)).astype(BF16)
+        context = jnp.where(own_head, mm(shares, value_rows), 0.0)
+        context = sum(context[8 * k : 8 * k + 8] for k in range(6)).astype(BF16)
+        ending = ending + nt(context, att[side, :, 1152:1536])
+    out_ref[...] = ending.astype(BF16)
+
+
+def trunk_rows(residual, mask_row, gains, weights):
+    vmem = pl.BlockSpec(memory_space=pltpu.VMEM)
+    return pl.pallas_call(
+        trunk_rows_kernel,
+        out_shape=jax.ShapeDtypeStruct((8, D), BF16),
+        in_specs=[vmem, vmem, vmem, pl.BlockSpec(memory_space=pl.ANY)],
+        out_specs=vmem,
+        scratch_shapes=[
+            pltpu.VMEM((2, 2, D, 1536), BF16),
+            pltpu.VMEM((2, D, 1536), BF16),
+            pltpu.SemaphoreType.DMA((2, 2)),
+            pltpu.SemaphoreType.DMA((2,)),
+        ],
+        compiler_params=pltpu.CompilerParams(vmem_limit_bytes=40 * 1024 * 1024),
+        name="trunk_rows",
+    )(residual, mask_row, gains, weights)
+
+
+def readout_mlp_kernel(end_ref, gain_ref, all_ref, out_ref, mlp, sem):
+    def block(side):
+        return pltpu.make_async_copy(
+            all_ref.at[pl.ds(side * D, D), pl.ds(4608, 768)], mlp.at[side], sem.at[side]
+        )
+
+    for side in range(2):
+        block(side).start()
+    normed = normalize(end_ref[...].astype(F32), gain_ref[3:4, :]).astype(BF16)
+    total = jnp.zeros(end_ref.shape, F32)
+    for side in range(2):
+        block(side).wait()
+        hidden = jax.nn.gelu(mm(normed, mlp[side, :, 0:384]), approximate=True).astype(BF16)
+        total = total + nt(hidden, mlp[side, :, 384:768])
+    out_ref[...] = total.astype(BF16)
+
+
+def readout_mlp(ending, gains, weights):
+    vmem = pl.BlockSpec(memory_space=pltpu.VMEM)
+    return pl.pallas_call(
+        readout_mlp_kernel,
+        out_shape=jax.ShapeDtypeStruct(ending.shape, BF16),
+        in_specs=[vmem, vmem, pl.BlockSpec(memory_space=pl.ANY)],
+        out_specs=vmem,
+        scratch_shapes=[pltpu.VMEM((2, D, 768), BF16), pltpu.SemaphoreType.DMA((2,))],
+        name="readout_mlp",
+    )(ending, gains, weights)
 
 
 def plan():
@@ -190,39 +301,10 @@
     got = got.reshape(peers * READ, 128)
 
     residual, got, gathered_weights = lax.optimization_barrier((residual, got, gathered_weights))
-    sides = gathered_weights.reshape(2, D, -1)
-
-    def weight(side, start, columns):
-        return sides[side, :, start : start + columns]
-
-    normed = normalize(residual, norm_gains[1]).astype(BF16)
-    for side in range(2):
-        hidden = jax.nn.gelu(mm(normed, weight(side, 1536, 1536)), approximate=True).astype(BF16)
-        residual = residual + mm_t(hidden, weight(side, 3072, 1536))
-    own_samples = obs_mask.shape[0]
-    normed = normalize(residual, norm_gains[2]).astype(BF16)
-    last = slice(SEQ - READ, SEQ)
-    ending = residual.reshape(own_samples, SEQ, D)[:, last].reshape(-1, D)
-    normed_end = normed.reshape(own_samples, SEQ, D)[:, last].reshape(-1, D)
-    allowed = allowed_keys(obs_mask)[:, last]
-    for side in range(2):
-        queries = mm(normed_end, weight(side, 0, 384)).astype(BF16)
-        key_rows = mm(normed, weight(side, 384, 384)).astype(BF16)
-        value_rows = mm(normed, weight(side, 768, 384)).astype(BF16)
-        context = attend(
-            queries.reshape(own_samples, READ, -1, HDIM),
-            key_rows.reshape(own_samples, SEQ, -1, HDIM),
-            value_rows.reshape(own_samples, SEQ, -1, HDIM),
-            allowed,
-        ).reshape(own_samples * READ, -1)
-        ending = ending + mm_t(context, weight(side, 1152, 384))
-    ending = gather_rows(ending.astype(BF16), "mp").astype(F32)
-    normed = normalize(ending, norm_gains[3]).astype(BF16)
-    partial_value = 0.0
-    for side in range(2):
-        hidden = jax.nn.gelu(mm(normed, weight(side, 4608, 384)), approximate=True).astype(BF16)
-        partial_value = partial_value + mm_t(hidden, weight(side, 4992, 384))
-    ending = ending + summed_for_all(partial_value.astype(BF16), "mp")
+    ending = trunk_rows(residual, obs_mask.reshape(1, -1), norm_gains, gathered_weights)
+    ending = gather_rows(ending[: 2 * obs_mask.shape[0]], "mp")
+    partial_value = readout_mlp(ending, norm_gains, gathered_weights)
+    ending = ending.astype(F32) + summed_for_all(partial_value, "mp")
     readouts = normalize(ending, norm_gains[4]).astype(BF16).reshape(samples, READ * D)
 
     send = mm(place, readouts).astype(BF16)

time: 232 us -> 220 us (0.948)
  matrix products: 39.5 us -> 15 us
  Pallas kernels: 0 us -> 11.7 us
    dot_general x7 -> x1, matrix products: 16.8 us -> 1.72 us  [mm_t(): return jnp.einsum('tk,dk->td', a, b, preferred_element_type=F32)]
    pallas_call x0 -> x2, Pallas kernels: none -> 11.7 us  [the longest x1 8.03 us: trunk_rows(): pl.pallas_call(trunk_rows_kernel, out_shape=jax.ShapeDtypeStruct((8, D),...]
    dot_general x11 -> x5, matrix products: 11 us -> 1.8 us  [mm(): return jnp.dot(a, b, preferred_element_type=F32)]
    all_gather x1, waiting for transfers between devices: 5.79 us -> 3.3 us  [on_device(): lax.all_gather(piece, ('c', 'z', 'y'), axis=0, tiled=True)]
  transfers between devices with their start and end apart: 15 -> 15, of which waited for: 13 -> 13; matrix products, arithmetic and copies ran while one was open for 12% -> 13% of each run, Pallas kernels for 0% -> 0%
where the time goes in v4:
time: 220 us; the launch traced here: 219 us
  starting transfers between devices  68.6 us (31%)
  waiting for transfers between devices  67.3 us (31%)
  local copies, waits for them, and re-layouts  25.4 us (12%)
  matrix products  15 us (7%)
  between operations  14.9 us (7%)
  Pallas kernels  11.7 us (5%)
  other arithmetic  9.23 us (4%)
  blocking collectives  6.55 us (3%)
    ppermute x6, starting transfers between devices, on_device(): other = lax.ppermute(first_piece, axis, swapped)  18 us
    all_to_all x1, starting transfers between devices, on_device(): got = lax.all_to_all(sent, DP, split_axis=0, concat_axis=0, tiled=True)  18 us
    all_to_all x4, starting transfers between devices, sent_to_all(): return lax.all_to_all(copies, axis, split_axis=0, concat_axis=0, tiled=True)  15.9 us
    all_to_all x4, waiting for transfers between devices, sent_to_all(): return lax.all_to_all(copies, axis, split_axis=0, concat_axis=0, tiled=True)  14.3 us
    all_to_all x1, waiting for transfers between devices, on_device(): features = lax.all_to_all(send, DP, split_axis=0, concat_axis=0, tiled=True)  11.3 us
    all_to_all x1, waiting for transfers between devices, summed_on_arrival(): lax.all_to_all(pieces, axis, split_axis=0, concat_axis=0, tiled=True)  10.6 us
    ppermute x6, waiting for transfers between devices, on_device(): other = lax.ppermute(first_piece, axis, swapped)  10.4 us
    all_to_all x1, waiting for transfers between devices, on_device(): got = lax.all_to_all(sent, DP, split_axis=0, concat_axis=0, tiled=True)  9.27 us
  transfers between devices with their start and end apart: 15, of which 13 were waited for; matrix products, arithmetic and copies ran while one was open for 13% of the time, Pallas kernels for 0%

profile of v4, /device:TPU:1, one launch (start us, length us, event | category | flops | bytes accessed | tf_op | source)
XLA Modules:
  0.0 218.7 jit_solution(8488503416966663885)
XLA Ops:
  7.2 0.9 fusion.79
  10.0 1.0 fusion.81
  11.8 4.8 %all-to-all-start = ((bf16[4,12,2304]{2,1,0:T(8,128)(2,1)}), bf16[4,12,2304]{2,1,0:T(8,128)(2,1)S(1)}, u32[]{:S(2)}, u32[]{:S(2)}) async-start(bf16[4,12,2304]{2,1,0:T(8,128)(2,1)} %broadcast_in_dim.78), calls=%async_computation | async-start | bytes 589824 | tf_op jit(solution)/shard_map/all_to_all | solution.py:28
  17.6 4.8 %all-to-all-done = bf16[4,12,2304]{2,1,0:T(8,128)(2,1)S(1)} async-done(((bf16[4,12,2304]{2,1,0:T(8,128)(2,1)}), bf16[4,12,2304]{2,1,0:T(8,128)(2,1)S(1)}, u32[]{:S(2)}, u32[]{:S(2)}) %all-to-all-start) | async-done | bytes 221216 | tf_op jit(solution)/shard_map/all_to_all | solution.py:28
  23.7 6.6 %all_to_all.57 = bf16[2,12,5376]{2,1,0:T(8,128)(2,1)S(1)} all-to-all(bf16[2,12,5376]{2,1,0:T(8,128)(2,1)S(1)} %copy.185), channel_id=1, replica_groups=mesh['z'=8,'y'=4,'c'=2,'mp'=4] {'c'}, dimensions={0} | all-to-all | bytes 516096 | tf_op jit(solution)/shard_map/all_to_all | solution.py:261
  31.3 1.0 collective-permute-start
  32.7 1.3 collective-permute-done
  34.1 2.6 %collective-permute-start.1 = (bf16[24,768]{1,0:T(8,128)(2,1)S(1)}, bf16[24,768]{1,0:T(8,128)(2,1)S(1)}, u32[]{:S(2)}, u32[]{:S(2)}) collective-permute-start(bf16[24,768]{1,0:T(8,128)(2,1)S(1)} %pad_maximum_fusion.6), channel_id=1, source_target_pairs={{0,64},{32,96},{64,0},{96,32},{128,192},{160,224},{192,128},{224,1... | collective-permute-start | bytes 110600 | tf_op jit(solution)/shard_map/ppermute | solution.py:282
  36.7 1.3 collective-permute-done.1
  38.1 6.2 %collective-permute-start.2 = (bf16[48,768]{1,0:T(8,128)(2,1)S(1)}, bf16[48,768]{1,0:T(8,128)(2,1)S(1)}, u32[]{:S(2)}, u32[]{:S(2)}) collective-permute-start(bf16[48,768]{1,0:T(8,128)(2,1)S(1)} %pad_maximum_fusion.5), channel_id=1, source_target_pairs={{0,128},{32,160},{64,192},{96,224},{128,0},{160,32},{192,64},{224,... | collective-permute-start | bytes 221192 | tf_op jit(solution)/shard_map/ppermute | solution.py:282
  44.5 2.4 %collective-permute-done.2 = bf16[48,768]{1,0:T(8,128)(2,1)S(1)} collective-permute-done((bf16[48,768]{1,0:T(8,128)(2,1)S(1)}, bf16[48,768]{1,0:T(8,128)(2,1)S(1)}, u32[]{:S(2)}, u32[]{:S(2)}) %collective-permute-start.2) | collective-permute-done | bytes 73760 | tf_op jit(solution)/shard_map/ppermute | solution.py:282
  46.9 1.3 collective-permute-start.3
  48.3 1.1 broadcast_in_dim.79
  49.5 3.5 %all-to-all-start.2 = ((bf16[4,208,768]{2,1,0:T(8,128)(2,1)}), bf16[4,208,768]{2,1,0:T(8,128)(2,1)S(1)}, u32[]{:S(2)}, u32[]{:S(2)}) async-start(bf16[4,208,768]{2,1,0:T(8,128)(2,1)} %broadcast_in_dim.79), calls=%async_computation.2 | async-start | bytes 2555904 | tf_op jit(solution)/shard_map/all_to_all | solution.py:28
  53.1 3.1 %collective-permute-start.4 = (bf16[192,768]{1,0:T(8,128)(2,1)S(1)}, bf16[192,768]{1,0:T(8,128)(2,1)S(1)}, u32[]{:S(2)}, u32[]{:S(2)}) collective-permute-start(bf16[192,768]{1,0:T(8,128)(2,1)S(1)} %pad_maximum_fusion.2), channel_id=1, source_target_pairs={{0,16},{8,24},{16,0},{24,8},{1,17},{9,25},{17,1},{25,9},{2,18},{10... | collective-permute-start | bytes 884744 | tf_op jit(solution)/shard_map/ppermute | solution.py:282
  56.5 5.4 %collective-permute-done.4 = bf16[192,768]{1,0:T(8,128)(2,1)S(1)} collective-permute-done((bf16[192,768]{1,0:T(8,128)(2,1)S(1)}, bf16[192,768]{1,0:T(8,128)(2,1)S(1)}, u32[]{:S(2)}, u32[]{:S(2)}) %collective-permute-start.4) | collective-permute-done | bytes 294944 | tf_op jit(solution)/shard_map/ppermute | solution.py:282
  62.0 3.9 %collective-permute-start.5 = (bf16[384,768]{1,0:T(8,128)(2,1)S(1)}, bf16[384,768]{1,0:T(8,128)(2,1)}, u32[]{:S(2)}, u32[]{:S(2)}) collective-permute-start(bf16[384,768]{1,0:T(8,128)(2,1)S(1)} %pad_maximum_fusion.1), channel_id=1, source_target_pairs={{0,4},{4,0},{1,5},{5,1},{2,6},{6,2},{3,7},{7,3},{8,12},{12,8},{9,1... | collective-permute-start | bytes 1769480 | tf_op jit(solution)/shard_map/ppermute | solution.py:282
  65.9 1.3 all-to-all-done.2
  67.3 0.9 copy-done.2
  68.4 1.3 broadcast_select_fusion.1
  70.1 1.4 copy.189
  71.5 2.3 %reshape.238 = bf16[768,768]{1,0:T(8,128)(2,1)S(1)} reshape(bf16[8,4,2,12,768]{4,3,2,1,0:T(8,128)(2,1)} %copy.189) | data formatting | bytes 2359296 | tf_op jit(solution)/shard_map/reshape | solution.py:287
  74.8 1.3 squeeze.59
  76.2 1.4 squeeze.60
  78.0 2.9 %fusion.2 = f32[12,3,64,64]{2,3,1,0:T(8,128)} fusion(bf16[12,64,3,64]{1,0,3,2:T(8,128)(2,1)} %squeeze.60, bf16[12,64,3,64]{1,0,3,2:T(8,128)(2,1)} %squeeze.59, pred[12,64,64]{1,2,0:T(8,128)(4,1)S(1)} %broadcast_or_fusion), kind=kOutput, calls=%fused_computation.8 | convolution fusion | flops 19169280 | bytes 1228800 | tf_op jit(solution)/shard_map/sqhd,skhd->shqk/dot_general | solution.py:69
  80.9 2.1 fusion.3
  83.9 1.7 convolution_convert_fusion.2
  85.6 3.7 %all-to-all-start.3 = ((bf16[4,192,768]{2,1,0:T(8,128)(2,1)}), bf16[4,192,768]{2,1,0:T(8,128)(2,1)S(1)}, u32[]{:S(2)}, u32[]{:S(2)}) async-start(bf16[4,192,768]{2,1,0:T(8,128)(2,1)} %bitcast.24), calls=%async_computation.3 | async-start | bytes 2359296 | tf_op jit(solution)/shard_map/all_to_all | solution.py:38
  90.7 10.6 %all-to-all-done.3 = bf16[4,192,768]{2,1,0:T(8,128)(2,1)S(1)} async-done(((bf16[4,192,768]{2,1,0:T(8,128)(2,1)}), bf16[4,192,768]{2,1,0:T(8,128)(2,1)S(1)}, u32[]{:S(2)}, u32[]{:S(2)}) %all-to-all-start.3) | async-done | bytes 1179680 | tf_op jit(solution)/shard_map/all_to_all | solution.py:38
  101.3 18.0 %all-to-all-start.4 = ((bf16[64,2,128]{2,1,0:T(2,128)(2,1)}), bf16[64,2,128]{2,1,0:T(2,128)(2,1)S(1)}, u32[]{:S(2)}, u32[]{:S(2)}) async-start(bf16[64,2,128]{2,1,0:T(2,128)(2,1)} %copy.202), calls=%async_computation.4 | async-start | bytes 65536 | tf_op jit(solution)/shard_map/all_to_all | solution.py:300
  119.5 9.3 %all-to-all-done.4 = bf16[64,2,128]{2,1,0:T(2,128)(2,1)S(1)} async-done(((bf16[64,2,128]{2,1,0:T(2,128)(2,1)}), bf16[64,2,128]{2,1,0:T(2,128)(2,1)S(1)}, u32[]{:S(2)}, u32[]{:S(2)}) %all-to-all-start.4) | async-done | bytes 32800 | tf_op jit(solution)/shard_map/all_to_all | solution.py:300
  128.8 3.3 %all-gather.2.cloned.1.call-done.all_ref = bf16[1536,5376]{1,0:T(8,128)(2,1)} async-done(((bf16[24,5376]{1,0:T(8,128)(2,1)}), bf16[1536,5376]{1,0:T(8,128)(2,1)}) %all-gather.2.cloned.1.call-update) | async-done | bytes 16515088 | tf_op jit(solution)/shard_map/all_gather | solution.py:278
  132.1 8.0 %trunk_rows.1 = bf16[8,768]{1,0:T(8,128)(2,1)S(1)} custom-call(f32[192,768]{1,0:T(8,128)S(1)} %convert_add_fusion.res_ref, s32[1,192]{1,0:T(1,128)S(1)} %reshape.234.mask_ref, f32[5,768]{1,0:T(8,128)S(1)} %copy-done.1, bf16[1536,5376]{1,0:T(8,128)(2,1)} %all-gather.2.cloned.1.call-done.all_ref), custom_call_target="tpu_custom_call" | custom-call | tf_op jit(solution)/shard_map/trunk_rows/pallas_call | solution.py:142
  140.8 4.0 %all-to-all-start.5 = ((bf16[4,6,768]{2,1,0:T(8,128)(2,1)}), bf16[4,6,768]{2,1,0:T(8,128)(2,1)S(1)}, u32[]{:S(2)}, u32[]{:S(2)}) async-start(bf16[4,6,768]{2,1,0:T(8,128)(2,1)} %broadcast_in_dim.85), calls=%async_computation.5 | async-start | bytes 98304 | tf_op jit(solution)/shard_map/all_to_all | solution.py:28
  145.4 3.7 %all-to-all-done.5 = bf16[4,6,768]{2,1,0:T(8,128)(2,1)S(1)} async-done(((bf16[4,6,768]{2,1,0:T(8,128)(2,1)}), bf16[4,6,768]{2,1,0:T(8,128)(2,1)S(1)}, u32[]{:S(2)}, u32[]{:S(2)}) %all-to-all-start.5) | async-done | bytes 36896 | tf_op jit(solution)/shard_map/all_to_all | solution.py:28
  149.7 3.6 %readout_mlp.1 = bf16[24,768]{1,0:T(8,128)(2,1)} custom-call(bf16[24,768]{1,0:T(8,128)(2,1)} %reshape.243.end_ref, f32[5,768]{1,0:T(8,128)} %gain_ref.3, bf16[1536,5376]{1,0:T(8,128)(2,1)} %all-gather.2.cloned.1.call-done.all_ref), custom_call_target="tpu_custom_call" | custom-call | tf_op jit(solution)/shard_map/readout_mlp/pallas_call | solution.py:177
  153.4 1.4 broadcast_in_dim.86
  154.8 3.6 %all-to-all-start.6 = ((bf16[4,24,768]{2,1,0:T(8,128)(2,1)}), bf16[4,24,768]{2,1,0:T(8,128)(2,1)S(1)}, u32[]{:S(2)}, u32[]{:S(2)}) async-start(bf16[4,24,768]{2,1,0:T(8,128)(2,1)} %broadcast_in_dim.86), calls=%async_computation.6 | async-start | bytes 294912 | tf_op jit(solution)/shard_map/all_to_all | solution.py:28
  158.6 4.5 %all-to-all-done.6 = bf16[4,24,768]{2,1,0:T(8,128)(2,1)S(1)} async-done(((bf16[4,24,768]{2,1,0:T(8,128)(2,1)}), bf16[4,24,768]{2,1,0:T(8,128)(2,1)S(1)}, u32[]{:S(2)}, u32[]{:S(2)}) %all-to-all-start.6) | async-done | bytes 147488 | tf_op jit(solution)/shard_map/all_to_all | solution.py:28
  166.2 8.6 %all-to-all-start.7 = ((bf16[64,2,768]{2,1,0:T(2,128)(2,1)}), bf16[64,2,768]{2,1,0:T(2,128)(2,1)S(1)}, u32[]{:S(2)}, u32[]{:S(2)}) async-start(bf16[64,2,768]{2,1,0:T(2,128)(2,1)} %reshape.256), calls=%async_computation.7 | async-start | bytes 393216 | tf_op jit(solution)/shard_map/all_to_all | solution.py:311
  175.5 11.3 %all-to-all-done.7 = bf16[64,2,768]{2,1,0:T(2,128)(2,1)S(1)} async-done(((bf16[64,2,768]{2,1,0:T(2,128)(2,1)}), bf16[64,2,768]{2,1,0:T(2,128)(2,1)S(1)}, u32[]{:S(2)}, u32[]{:S(2)}) %all-to-all-start.7) | async-done | bytes 196640 | tf_op jit(solution)/shard_map/all_to_all | solution.py:311
  186.9 1.2 reduce.7
  190.6 1.0 convolution_bitcast_fusion.2
  191.6 1.8 reduce.16
  194.2 4.5 %all-to-all-start.8 = ((bf16[64,2,768]{2,1,0:T(2,128)(2,1)}), bf16[64,2,768]{2,1,0:T(2,128)(2,1)S(1)}, u32[]{:S(2)}, u32[]{:S(2)}) async-start(bf16[64,2,768]{2,1,0:T(2,128)(2,1)} %reshape.258), calls=%async_computation.8 | async-start | bytes 393216 | tf_op jit(solution)/shard_map/all_to_all | solution.py:333
  200.8 0.9 convolution_bitcast_fusion.1
  201.8 0.9 convolution_bitcast_fusion
  202.7 8.1 %all-to-all-done.8 = bf16[64,2,768]{2,1,0:T(2,128)(2,1)S(1)} async-done(((bf16[64,2,768]{2,1,0:T(2,128)(2,1)}), bf16[64,2,768]{2,1,0:T(2,128)(2,1)S(1)}, u32[]{:S(2)}, u32[]{:S(2)}) %all-to-all-start.8) | async-done | bytes 196640 | tf_op jit(solution)/shard_map/all_to_all | solution.py:333
  (160 shorter events, 24.0 us)
Async XLA Ops:
  7.2 181.1 %copy-start = (bf16[1,768,256]{2,1,0:T(8,128)(2,1)S(1)}, bf16[1,768,256]{2,1,0:T(8,128)(2,1)}, u32[]{:S(2)}) copy-start(bf16[1,768,256]{2,1,0:T(8,128)(2,1)} %param.30) | copy-start | bytes 1179652
  7.2 9.5 %copy-start.1 = (f32[5,768]{1,0:T(8,128)S(1)}, f32[5,768]{1,0:T(8,128)}, u32[]{:S(2)}) copy-start(f32[5,768]{1,0:T(8,128)} %gain_ref.3) | copy-start | bytes 46084
  7.2 9.5 %copy-start.3 = (bf16[192,768]{1,0:T(8,128)(2,1)S(1)}, bf16[192,768]{1,0:T(8,128)(2,1)}, u32[]{:S(2)}) copy-start(bf16[192,768]{1,0:T(8,128)(2,1)} %param.18) | copy-start | bytes 884740
  11.1 6.3 %copy-start.9 = (s32[3,64]{1,0:T(4,128)S(1)}, s32[3,64]{1,0:T(4,128)}, u32[]{:S(2)}) copy-start(s32[3,64]{1,0:T(4,128)} %param.19) | copy-start | bytes 2308
  11.8 10.5 %all-to-all-start = ((bf16[4,12,2304]{2,1,0:T(8,128)(2,1)}), bf16[4,12,2304]{2,1,0:T(8,128)(2,1)S(1)}, u32[]{:S(2)}, u32[]{:S(2)}) async-start(bf16[4,12,2304]{2,1,0:T(8,128)(2,1)} %broadcast_in_dim.78), calls=%async_computation | async-start | bytes 589824 | tf_op jit(solution)/shard_map/all_to_all | solution.py:28
  16.7 115.4 %all-gather.2.cloned.1.call-start = ((), (), s32[]{:S(2)}) async-start(), calls=%async_computation.9 | async-start | bytes 16773120 | tf_op jit(solution)/shard_map/all_gather | solution.py:278
  23.7 8.6 %copy-start.11 = (s32[12,2]{0,1:T(2,128)S(1)}, s32[12,2]{0,1:T(2,128)}, u32[]{:S(2)}) copy-start(s32[12,2]{0,1:T(2,128)} %param.26) | copy-start | bytes 292
  23.7 20.6 %copy-start.6 = (bf16[12,2,56]{2,1,0:T(2,128)(2,1)S(1)}, bf16[12,2,56]{2,1,0:T(2,128)(2,1)}, u32[]{:S(2)}) copy-start(bf16[12,2,56]{2,1,0:T(2,128)(2,1)} %param.28) | copy-start | bytes 8068
  30.3 18.0 %copy-start.8 = (bf16[12,2,56]{2,1,0:T(2,128)(2,1)S(1)}, bf16[12,2,56]{2,1,0:T(2,128)(2,1)}, u32[]{:S(2)}) copy-start(bf16[12,2,56]{2,1,0:T(2,128)(2,1)} %param.27) | copy-start | bytes 8068
  31.3 2.7 %collective-permute-start = (bf16[12,768]{1,0:T(8,128)(2,1)S(1)}, bf16[12,768]{1,0:T(8,128)(2,1)S(1)}, u32[]{:S(2)}, u32[]{:S(2)}) collective-permute-start(bf16[12,768]{1,0:T(8,128)(2,1)S(1)} %pad_maximum_fusion.7), channel_id=1, source_target_pairs={{0,32},{32,0},{64,96},{96,64},{128,160},{160,128},{192,224},{224,1... | collective-permute-start | bytes 55304 | tf_op jit(solution)/shard_map/ppermute | solution.py:282
  34.1 3.9 %collective-permute-start.1 = (bf16[24,768]{1,0:T(8,128)(2,1)S(1)}, bf16[24,768]{1,0:T(8,128)(2,1)S(1)}, u32[]{:S(2)}, u32[]{:S(2)}) collective-permute-start(bf16[24,768]{1,0:T(8,128)(2,1)S(1)} %pad_maximum_fusion.6), channel_id=1, source_target_pairs={{0,64},{32,96},{64,0},{96,32},{128,192},{160,224},{192,128},{224,1... | collective-permute-start | bytes 110600 | tf_op jit(solution)/shard_map/ppermute | solution.py:282
  38.1 8.8 %collective-permute-start.2 = (bf16[48,768]{1,0:T(8,128)(2,1)S(1)}, bf16[48,768]{1,0:T(8,128)(2,1)S(1)}, u32[]{:S(2)}, u32[]{:S(2)}) collective-permute-start(bf16[48,768]{1,0:T(8,128)(2,1)S(1)} %pad_maximum_fusion.5), channel_id=1, source_target_pairs={{0,128},{32,160},{64,192},{96,224},{128,0},{160,32},{192,64},{224,... | collective-permute-start | bytes 221192 | tf_op jit(solution)/shard_map/ppermute | solution.py:282
  46.9 6.1 %collective-permute-start.3 = (bf16[96,768]{1,0:T(8,128)(2,1)S(1)}, bf16[96,768]{1,0:T(8,128)(2,1)S(1)}, u32[]{:S(2)}, u32[]{:S(2)}) collective-permute-start(bf16[96,768]{1,0:T(8,128)(2,1)S(1)} %pad_maximum_fusion.4), channel_id=1, source_target_pairs={{0,8},{8,0},{16,24},{24,16},{1,9},{9,1},{17,25},{25,17},{2,10},{10... | collective-permute-start | bytes 442376 | tf_op jit(solution)/shard_map/ppermute | solution.py:282
  49.5 17.7 %all-to-all-start.2 = ((bf16[4,208,768]{2,1,0:T(8,128)(2,1)}), bf16[4,208,768]{2,1,0:T(8,128)(2,1)S(1)}, u32[]{:S(2)}, u32[]{:S(2)}) async-start(bf16[4,208,768]{2,1,0:T(8,128)(2,1)} %broadcast_in_dim.79), calls=%async_computation.2 | async-start | bytes 2555904 | tf_op jit(solution)/shard_map/all_to_all | solution.py:28
  53.0 3.2 %copy-start.10 = (s32[12,1]{0,1:T(1,128)S(1)}, s32[12,1]{0,1:T(1,128)}, u32[]{:S(2)}) copy-start(s32[12,1]{0,1:T(1,128)} %param.25) | copy-start | bytes 148
  53.1 8.7 %collective-permute-start.4 = (bf16[192,768]{1,0:T(8,128)(2,1)S(1)}, bf16[192,768]{1,0:T(8,128)(2,1)S(1)}, u32[]{:S(2)}, u32[]{:S(2)}) collective-permute-start(bf16[192,768]{1,0:T(8,128)(2,1)S(1)} %pad_maximum_fusion.2), channel_id=1, source_target_pairs={{0,16},{8,24},{16,0},{24,8},{1,17},{9,25},{17,1},{25,9},{2,18},{10... | collective-permute-start | bytes 884744 | tf_op jit(solution)/shard_map/ppermute | solution.py:282
  62.0 6.4 %collective-permute-start.5 = (bf16[384,768]{1,0:T(8,128)(2,1)S(1)}, bf16[384,768]{1,0:T(8,128)(2,1)}, u32[]{:S(2)}, u32[]{:S(2)}) collective-permute-start(bf16[384,768]{1,0:T(8,128)(2,1)S(1)} %pad_maximum_fusion.1), channel_id=1, source_target_pairs={{0,4},{4,0},{1,5},{5,1},{2,6},{6,2},{3,7},{7,3},{8,12},{12,8},{9,1... | collective-permute-start | bytes 1769480 | tf_op jit(solution)/shard_map/ppermute | solution.py:282
  67.2 1.0 copy-start.2
  71.5 2.4 %slice-start = ((bf16[4,208,768]{2,1,0:T(8,128)(2,1)}), bf16[4,192,768]{2,1,0:T(8,128)(2,1)S(1)}, s32[]{:S(2)}) async-start(bf16[4,208,768]{2,1,0:T(8,128)(2,1)} %copy-done.2), calls=%async_computation.10 | async-start | bytes 2359296 | tf_op jit(solution)/shard_map/slice | solution.py:290
  85.6 3.7 %copy-start.15 = (s32[25]{0:T(128)S(1)}, s32[25]{0:T(128)}, u32[]{:S(2)}) copy-start(s32[25]{0:T(128)} %param.29) | copy-start | bytes 304
  85.6 15.7 %all-to-all-start.3 = ((bf16[4,192,768]{2,1,0:T(8,128)(2,1)}), bf16[4,192,768]{2,1,0:T(8,128)(2,1)S(1)}, u32[]{:S(2)}, u32[]{:S(2)}) async-start(bf16[4,192,768]{2,1,0:T(8,128)(2,1)} %bitcast.24), calls=%async_computation.3 | async-start | bytes 2359296 | tf_op jit(solution)/shard_map/all_to_all | solution.py:38
  89.3 30.2 %copy-start.4 = (bf16[192,768]{1,0:T(8,128)(2,1)S(1)}, bf16[192,768]{1,0:T(8,128)(2,1)}, u32[]{:S(2)}) copy-start(bf16[192,768]{1,0:T(8,128)(2,1)} %param.18) | copy-start | bytes 884740
  101.3 27.5 %all-to-all-start.4 = ((bf16[64,2,128]{2,1,0:T(2,128)(2,1)}), bf16[64,2,128]{2,1,0:T(2,128)(2,1)S(1)}, u32[]{:S(2)}, u32[]{:S(2)}) async-start(bf16[64,2,128]{2,1,0:T(2,128)(2,1)} %copy.202), calls=%async_computation.4 | async-start | bytes 65536 | tf_op jit(solution)/shard_map/all_to_all | solution.py:300
  140.8 8.4 %all-to-all-start.5 = ((bf16[4,6,768]{2,1,0:T(8,128)(2,1)}), bf16[4,6,768]{2,1,0:T(8,128)(2,1)S(1)}, u32[]{:S(2)}, u32[]{:S(2)}) async-start(bf16[4,6,768]{2,1,0:T(8,128)(2,1)} %broadcast_in_dim.85), calls=%async_computation.5 | async-start | bytes 98304 | tf_op jit(solution)/shard_map/all_to_all | solution.py:28
  149.7 8.7 %copy-start.5 = (bf16[1,56,256]{2,1,0:T(8,128)(2,1)S(1)}, bf16[1,56,256]{2,1,0:T(8,128)(2,1)}, u32[]{:S(2)}) copy-start(bf16[1,56,256]{2,1,0:T(8,128)(2,1)} %param.31) | copy-start | bytes 86020
  154.8 8.2 %all-to-all-start.6 = ((bf16[4,24,768]{2,1,0:T(8,128)(2,1)}), bf16[4,24,768]{2,1,0:T(8,128)(2,1)S(1)}, u32[]{:S(2)}, u32[]{:S(2)}) async-start(bf16[4,24,768]{2,1,0:T(8,128)(2,1)} %broadcast_in_dim.86), calls=%async_computation.6 | async-start | bytes 294912 | tf_op jit(solution)/shard_map/all_to_all | solution.py:28
  163.7 11.5 %copy-start.7 = (bf16[1,20,256]{2,1,0:T(8,128)(2,1)S(1)}, bf16[1,20,256]{2,1,0:T(8,128)(2,1)}, u32[]{:S(2)}) copy-start(bf16[1,20,256]{2,1,0:T(8,128)(2,1)} %param.32) | copy-start | bytes 30724
  166.2 20.6 %all-to-all-start.7 = ((bf16[64,2,768]{2,1,0:T(2,128)(2,1)}), bf16[64,2,768]{2,1,0:T(2,128)(2,1)S(1)}, u32[]{:S(2)}, u32[]{:S(2)}) async-start(bf16[64,2,768]{2,1,0:T(2,128)(2,1)} %reshape.256), calls=%async_computation.7 | async-start | bytes 393216 | tf_op jit(solution)/shard_map/all_to_all | solution.py:311
  175.5 13.0 %copy-start.13 = (bf16[1,256,256]{2,1,0:T(8,128)(2,1)S(1)}, bf16[1,256,256]{2,1,0:T(8,128)(2,1)}, u32[]{:S(2)}) copy-start(bf16[1,256,256]{2,1,0:T(8,128)(2,1)} %param.33) | copy-start | bytes 393220
  186.9 1.7 copy-start.12
  188.5 0.8 copy-start.14
  194.2 16.7 %all-to-all-start.8 = ((bf16[64,2,768]{2,1,0:T(2,128)(2,1)}), bf16[64,2,768]{2,1,0:T(2,128)(2,1)S(1)}, u32[]{:S(2)}, u32[]{:S(2)}) async-start(bf16[64,2,768]{2,1,0:T(2,128)(2,1)} %reshape.258), calls=%async_computation.8 | async-start | bytes 393216 | tf_op jit(solution)/shard_map/all_to_all | solution.py:333
Sparse Core Ops, SparseCore 0:
  31.2 100.8 all-gather.1

commit v5 on v4

--- a/solution.py
+++ b/solution.py
@@ -28,19 +28,10 @@
     return lax.all_to_all(copies, axis, split_axis=0, concat_axis=0, tiled=True)
 
 
-def gather_rows(x, axis):
-    pieces = sent_to_all(x, axis)
-    return pieces.reshape(-1, *x.shape[1:])
-
-
 def summed_on_arrival(x, axis):
     pieces = x.reshape(lax.axis_size(axis), -1, x.shape[1])
     arrived = lax.all_to_all(pieces, axis, split_axis=0, concat_axis=0, tiled=True)
     return arrived.astype(F32).sum(axis=0)
-
-
-def summed_for_all(x, axis):
-    return sent_to_all(x, axis).astype(F32).sum(axis=0)
 
 
 def normalize(values, scale_gain):
@@ -134,14 +125,16 @@
         context = jnp.where(own_head, mm(shares, value_rows), 0.0)
         context = sum(context[8 * k : 8 * k + 8] for k in range(6)).astype(BF16)
         ending = ending + nt(context, att[side, :, 1152:1536])
-    out_ref[...] = ending.astype(BF16)
+    for member in range(4):
+        out_ref[member] = ending.astype(BF16)
 
 
 def trunk_rows(residual, mask_row, gains, weights):
     vmem = pl.BlockSpec(memory_space=pltpu.VMEM)
+    rows = (residual, mask_row, gains)
     return pl.pallas_call(
         trunk_rows_kernel,
-        out_shape=jax.ShapeDtypeStruct((8, D), BF16),
+        out_shape=jax.ShapeDtypeStruct((4, 8, D), BF16),
         in_specs=[vmem, vmem, vmem, pl.BlockSpec(memory_space=pl.ANY)],
         out_specs=vmem,
         scratch_shapes=[
@@ -152,36 +145,29 @@
         ],
         compiler_params=pltpu.CompilerParams(vmem_limit_bytes=40 * 1024 * 1024),
         name="trunk_rows",
-    )(residual, mask_row, gains, weights)
-
-
-def readout_mlp_kernel(end_ref, gain_ref, all_ref, out_ref, mlp, sem):
-    def block(side):
-        return pltpu.make_async_copy(
-            all_ref.at[pl.ds(side * D, D), pl.ds(4608, 768)], mlp.at[side], sem.at[side]
-        )
-
-    for side in range(2):
-        block(side).start()
+    )(*(pltpu.with_memory_space_constraint(a, pltpu.VMEM) for a in rows), weights)
+
+
+def readout_mlp_kernel(end_ref, gain_ref, first_ref, second_ref, out_ref):
     normed = normalize(end_ref[...].astype(F32), gain_ref[3:4, :]).astype(BF16)
     total = jnp.zeros(end_ref.shape, F32)
-    for side in range(2):
-        block(side).wait()
-        hidden = jax.nn.gelu(mm(normed, mlp[side, :, 0:384]), approximate=True).astype(BF16)
-        total = total + nt(hidden, mlp[side, :, 384:768])
-    out_ref[...] = total.astype(BF16)
-
-
-def readout_mlp(ending, gains, weights):
+    for side_ref in (first_ref, second_ref):
+        hidden = jax.nn.gelu(mm(normed, side_ref[:, 0:384]), approximate=True).astype(BF16)
+        total = total + nt(hidden, side_ref[:, 384:768])
+    for member in range(4):
+        out_ref[member] = total.astype(BF16)
+
+
+def readout_mlp(ending, gains, first_side, second_side):
     vmem = pl.BlockSpec(memory_space=pltpu.VMEM)
+    operands = (ending, gains, first_side, second_side)
     return pl.pallas_call(
         readout_mlp_kernel,
-        out_shape=jax.ShapeDtypeStruct(ending.shape, BF16),
-        in_specs=[vmem, vmem, pl.BlockSpec(memory_space=pl.ANY)],
+        out_shape=jax.ShapeDtypeStruct((4, *ending.shape), BF16),
+        in_specs=[vmem] * 4,
         out_specs=vmem,
-        scratch_shapes=[pltpu.VMEM((2, D, 768), BF16), pltpu.SemaphoreType.DMA((2,))],
         name="readout_mlp",
-    )(ending, gains, weights)
+    )(*(pltpu.with_memory_space_constraint(a, pltpu.VMEM) for a in operands))
 
 
 def plan():
@@ -258,11 +244,22 @@
     share = jnp.stack([mlp_in[1], mlp_out[1].T], axis=1).reshape(12, 2, 2, -1)
     share = share.transpose(2, 0, 1, 3).reshape(2, 12, -1)
     halves = jnp.concatenate([full, share], axis=2)
-    halves = lax.all_to_all(halves, "c", split_axis=0, concat_axis=0, tiled=True)
-    piece = halves.reshape(24, -1)
+    upper = lax.axis_index("c") == 1
+    mine = jnp.where(upper, halves[1], halves[0])
+    other = lax.ppermute(jnp.where(upper, halves[0], halves[1]), "c", [(0, 1), (1, 0)])
+    piece = jnp.concatenate(
+        [jnp.where(upper, other, mine), jnp.where(upper, mine, other)], axis=0
+    )
 
     owners = embodiment[:, 0]
     place = (jnp.arange(peers)[:, None] == owners[None, :]).astype(BF16)
+    row_owner = jnp.pad(owners.reshape(4, 3), ((0, 0), (0, 1)), constant_values=-1)
+    row_owner = jnp.repeat(row_owner.reshape(-1), READ)
+    target = jnp.arange(peers * READ)
+    row_place = (target[:, None] // READ == row_owner[None, :]) & (
+        target[:, None] % READ == jnp.arange(row_owner.size)[None, :] % READ
+    )
+    row_place = row_place.astype(BF16)
     noisy = noisy_pair(levels, actions, noise, plan())
     marks = (levels + 1).astype(BF16)[..., None]
     early = jnp.concatenate([noisy, noise, marks, jnp.zeros((*levels.shape, 15), BF16)], axis=-1)
@@ -301,13 +298,16 @@
     got = got.reshape(peers * READ, 128)
 
     residual, got, gathered_weights = lax.optimization_barrier((residual, got, gathered_weights))
-    ending = trunk_rows(residual, obs_mask.reshape(1, -1), norm_gains, gathered_weights)
-    ending = gather_rows(ending[: 2 * obs_mask.shape[0]], "mp")
-    partial_value = readout_mlp(ending, norm_gains, gathered_weights)
-    ending = ending.astype(F32) + summed_for_all(partial_value, "mp")
-    readouts = normalize(ending, norm_gains[4]).astype(BF16).reshape(samples, READ * D)
-
-    send = mm(place, readouts).astype(BF16)
+    sides = [gathered_weights[D * k : D * (k + 1), 4608:5376] for k in range(2)]
+    copies = trunk_rows(residual, obs_mask.reshape(1, -1), norm_gains, gathered_weights)
+    ending = lax.all_to_all(copies, "mp", split_axis=0, concat_axis=0, tiled=True)
+    ending = ending.reshape(-1, D)
+    copies = readout_mlp(ending, norm_gains, *sides)
+    terms = lax.all_to_all(copies, "mp", split_axis=0, concat_axis=0, tiled=True)
+    ending = ending.astype(F32) + terms.astype(F32).sum(axis=0)
+    readouts = normalize(ending, norm_gains[4]).astype(BF16)
+
+    send = mm(row_place, readouts).astype(BF16).reshape(peers, READ, D)
     features = lax.all_to_all(send, DP, split_axis=0, concat_axis=0, tiled=True)
     features = features.reshape(peers * READ, D)
     head_noisy = got[:, :ACT]
@@ -329,12 +329,13 @@
     )
     grad_bf = grad_first.astype(BF16)
     backward = jnp.einsum("nc,dc->nd", grad_bf, head_read[0], preferred_element_type=F32)
-    backward = backward.astype(BF16).reshape(peers, READ * D)
+    backward = backward.astype(BF16).reshape(peers, READ, D)
+    backward, features = lax.optimization_barrier((backward, features))
     arrived = lax.all_to_all(backward, DP, split_axis=0, concat_axis=0, tiled=True)
     mine = samples // 4
     own_place = lax.dynamic_slice_in_dim(place, my_model * mine, mine, 1)
-    arrived = jnp.einsum("es,ef->sf", own_place, arrived, preferred_element_type=F32)
-    arrived = arrived.astype(BF16).reshape(mine, READ, D)
+    arrived = jnp.einsum("es,erf->srf", own_place, arrived, preferred_element_type=F32)
+    arrived = arrived.astype(BF16)
     part = lax.dynamic_slice_in_dim(features, my_model * width, width, 1)
     grad_read = jnp.einsum("nd,nc->dc", part, grad_bf, preferred_element_type=F32)
     grad_act = jnp.einsum("na,nc->ac", head_noisy, grad_bf, preferred_element_type=F32)

time: 220 us -> 217 us (0.986)
  waiting for transfers between devices: 67.3 us -> 78.8 us
  blocking collectives: 6.55 us -> 0 us
  starting transfers between devices: 68.6 us -> 63.8 us
  other arithmetic: 9.23 us -> 6.67 us
    all_to_all x0 -> x2, waiting for transfers between devices: none -> 7.34 us  [on_device(): lax.all_to_all(copies, 'mp', split_axis=0, concat_axis=0, tiled=True)]
    all_to_all x4 -> x2, starting transfers between devices: 15.9 us -> 8.68 us  [sent_to_all(): return lax.all_to_all(copies, axis, split_axis=0, concat_axis=0, tiled=True)]
    all_to_all x0 -> x2, starting transfers between devices: none -> 7 us  [on_device(): lax.all_to_all(copies, 'mp', split_axis=0, concat_axis=0, tiled=True)]
    all_to_all x1 -> x0, blocking collectives: 6.55 us -> none  [on_device(): lax.all_to_all(halves, 'c', split_axis=0, concat_axis=0, tiled=True)]
    all_to_all x1, starting transfers between devices: 18 us -> 12.4 us  [on_device(): got = lax.all_to_all(sent, DP, split_axis=0, concat_axis=0, tiled=True)]
    ppermute x6, waiting for transfers between devices: 10.4 us -> 15.9 us  [on_device(): other = lax.ppermute(first_piece, axis, swapped)]
    all_to_all x3 -> x0, other arithmetic: 3.77 us -> none  [the longest x2 1.93 us: on_device(): features = lax.all_to_all(send, DP, split_axis=0, concat_axis=0, tiled=True)]
    all_gather x1, waiting for transfers between devices: 3.3 us -> 0.01 us  [on_device(): lax.all_gather(piece, ('c', 'z', 'y'), axis=0, tiled=True)]
  transfers between devices with their start and end apart: 15 -> 16, of which waited for: 13 -> 14; matrix products, arithmetic and copies ran while one was open for 13% -> 17% of each run, Pallas kernels for 0% -> 0%
where the time goes in v5:
time: 217 us; the launch traced here: 216 us
  waiting for transfers between devices  78.8 us (36%)
  starting transfers between devices  63.8 us (29%)
  local copies, waits for them, and re-layouts  26.9 us (12%)
  matrix products  14.9 us (7%)
  between operations  14.8 us (7%)
  Pallas kernels  10.2 us (5%)
  other arithmetic  6.67 us (3%)
    ppermute x6, starting transfers between devices, on_device(): other = lax.ppermute(first_piece, axis, swapped)  17.5 us
    ppermute x6, waiting for transfers between devices, on_device(): other = lax.ppermute(first_piece, axis, swapped)  15.9 us
    all_to_all x2, waiting for transfers between devices, sent_to_all(): return lax.all_to_all(copies, axis, split_axis=0, concat_axis=0, tiled=True)  15 us
    all_to_all x1, starting transfers between devices, on_device(): got = lax.all_to_all(sent, DP, split_axis=0, concat_axis=0, tiled=True)  12.4 us
    all_to_all x1, waiting for transfers between devices, summed_on_arrival(): lax.all_to_all(pieces, axis, split_axis=0, concat_axis=0, tiled=True)  12 us
    all_to_all x1, waiting for transfers between devices, on_device(): features = lax.all_to_all(send, DP, split_axis=0, concat_axis=0, tiled=True)  11.5 us
    all_to_all x1, waiting for transfers between devices, on_device(): got = lax.all_to_all(sent, DP, split_axis=0, concat_axis=0, tiled=True)  9.1 us
    all_to_all x2, starting transfers between devices, sent_to_all(): return lax.all_to_all(copies, axis, split_axis=0, concat_axis=0, tiled=True)  8.68 us
  transfers between devices with their start and end apart: 16, of which 14 were waited for; matrix products, arithmetic and copies ran while one was open for 17% of the time, Pallas kernels for 0%

profile of v5, /device:TPU:1, one launch (start us, length us, event | category | flops | bytes accessed | tf_op | source)
XLA Modules:
  0.0 216.1 jit_solution(9125877065480297944)
XLA Ops:
  7.2 0.9 fusion.87
  9.1 1.0 slice_reduce_fusion
  11.8 4.8 %all-to-all-start = ((bf16[4,12,2304]{2,1,0:T(8,128)(2,1)}), bf16[4,12,2304]{2,1,0:T(8,128)(2,1)S(1)}, u32[]{:S(2)}, u32[]{:S(2)}) async-start(bf16[4,12,2304]{2,1,0:T(8,128)(2,1)} %broadcast_in_dim.42), calls=%async_computation | async-start | bytes 589824 | tf_op jit(solution)/shard_map/all_to_all | solution.py:28
  17.3 5.1 %all-to-all-done = bf16[4,12,2304]{2,1,0:T(8,128)(2,1)S(1)} async-done(((bf16[4,12,2304]{2,1,0:T(8,128)(2,1)}), bf16[4,12,2304]{2,1,0:T(8,128)(2,1)S(1)}, u32[]{:S(2)}, u32[]{:S(2)}) %all-to-all-start) | async-done | bytes 221216 | tf_op jit(solution)/shard_map/all_to_all | solution.py:28
  23.5 3.0 %collective-permute-start = (bf16[12,5376]{1,0:T(8,128)(2,1)S(1)}, bf16[12,5376]{1,0:T(8,128)(2,1)S(1)}, u32[]{:S(2)}, u32[]{:S(2)}) collective-permute-start(bf16[12,5376]{1,0:T(8,128)(2,1)S(1)} %select_bitcast_fusion), channel_id=1, source_target_pairs={{0,4},{4,0},{1,5},{5,1},{2,6},{6,2},{3,7},{7,3},{8,12},{12,8},{9,1... | collective-permute-start | bytes 387080 | tf_op jit(solution)/shard_map/ppermute | solution.py:249
  28.6 1.0 collective-permute-start.1
  29.6 1.7 collective-permute-done.1
  31.4 2.6 %collective-permute-start.2 = (bf16[24,768]{1,0:T(8,128)(2,1)S(1)}, bf16[24,768]{1,0:T(8,128)(2,1)S(1)}, u32[]{:S(2)}, u32[]{:S(2)}) collective-permute-start(bf16[24,768]{1,0:T(8,128)(2,1)S(1)} %pad_maximum_fusion.6), channel_id=1, source_target_pairs={{0,64},{32,96},{64,0},{96,32},{128,192},{160,224},{192,128},{224,1... | collective-permute-start | bytes 110600 | tf_op jit(solution)/shard_map/ppermute | solution.py:279
  34.0 1.3 collective-permute-done.2
  35.4 6.2 %collective-permute-start.3 = (bf16[48,768]{1,0:T(8,128)(2,1)S(1)}, bf16[48,768]{1,0:T(8,128)(2,1)S(1)}, u32[]{:S(2)}, u32[]{:S(2)}) collective-permute-start(bf16[48,768]{1,0:T(8,128)(2,1)S(1)} %pad_maximum_fusion.5), channel_id=1, source_target_pairs={{0,128},{32,160},{64,192},{96,224},{128,0},{160,32},{192,64},{224,... | collective-permute-start | bytes 221192 | tf_op jit(solution)/shard_map/ppermute | solution.py:279
  41.6 2.7 %collective-permute-done.3 = bf16[48,768]{1,0:T(8,128)(2,1)S(1)} collective-permute-done((bf16[48,768]{1,0:T(8,128)(2,1)S(1)}, bf16[48,768]{1,0:T(8,128)(2,1)S(1)}, u32[]{:S(2)}, u32[]{:S(2)}) %collective-permute-start.3) | collective-permute-done | bytes 73760 | tf_op jit(solution)/shard_map/ppermute | solution.py:279
  44.4 1.3 collective-permute-start.4
  45.8 3.2 %collective-permute-done.4 = bf16[96,768]{1,0:T(8,128)(2,1)S(1)} collective-permute-done((bf16[96,768]{1,0:T(8,128)(2,1)S(1)}, bf16[96,768]{1,0:T(8,128)(2,1)S(1)}, u32[]{:S(2)}, u32[]{:S(2)}) %collective-permute-start.4) | collective-permute-done | bytes 147488 | tf_op jit(solution)/shard_map/ppermute | solution.py:279
  49.2 2.9 %collective-permute-start.5 = (bf16[192,768]{1,0:T(8,128)(2,1)S(1)}, bf16[192,768]{1,0:T(8,128)(2,1)S(1)}, u32[]{:S(2)}, u32[]{:S(2)}) collective-permute-start(bf16[192,768]{1,0:T(8,128)(2,1)S(1)} %pad_maximum_fusion.2), channel_id=1, source_target_pairs={{0,16},{8,24},{16,0},{24,8},{1,17},{9,25},{17,1},{25,9},{2,18},{10... | collective-permute-start | bytes 884744 | tf_op jit(solution)/shard_map/ppermute | solution.py:279
  52.3 6.9 %collective-permute-done.5 = bf16[192,768]{1,0:T(8,128)(2,1)S(1)} collective-permute-done((bf16[192,768]{1,0:T(8,128)(2,1)S(1)}, bf16[192,768]{1,0:T(8,128)(2,1)S(1)}, u32[]{:S(2)}, u32[]{:S(2)}) %collective-permute-start.5) | collective-permute-done | bytes 294944 | tf_op jit(solution)/shard_map/ppermute | solution.py:279
  59.4 3.6 %collective-permute-start.6 = (bf16[384,768]{1,0:T(8,128)(2,1)S(1)}, bf16[384,768]{1,0:T(8,128)(2,1)S(1)}, u32[]{:S(2)}, u32[]{:S(2)}) collective-permute-start(bf16[384,768]{1,0:T(8,128)(2,1)S(1)} %pad_maximum_fusion.1), channel_id=1, source_target_pairs={{0,4},{4,0},{1,5},{5,1},{2,6},{6,2},{3,7},{7,3},{8,12},{12,8},{9,1... | collective-permute-start | bytes 1769480 | tf_op jit(solution)/shard_map/ppermute | solution.py:279
  63.2 1.1 broadcast_in_dim.43
  64.3 3.8 %all-to-all-start.1 = ((bf16[4,208,768]{2,1,0:T(8,128)(2,1)}), bf16[4,208,768]{2,1,0:T(8,128)(2,1)S(1)}, u32[]{:S(2)}, u32[]{:S(2)}) async-start(bf16[4,208,768]{2,1,0:T(8,128)(2,1)} %broadcast_in_dim.43), calls=%async_computation.1 | async-start | bytes 2555904 | tf_op jit(solution)/shard_map/all_to_all | solution.py:28
  68.8 1.1 pad_maximum_fusion
  69.9 2.2 reshape.292
  72.0 1.4 copy.172
  73.4 2.2 %reshape.293 = bf16[768,768]{1,0:T(8,128)(2,1)S(1)} reshape(bf16[8,4,2,12,768]{4,3,2,1,0:T(8,128)(2,1)} %copy.172) | data formatting | bytes 2359296 | tf_op jit(solution)/shard_map/reshape | solution.py:284
  75.7 9.9 %all-to-all-done.1 = bf16[4,208,768]{2,1,0:T(8,128)(2,1)S(1)} async-done(((bf16[4,208,768]{2,1,0:T(8,128)(2,1)}), bf16[4,208,768]{2,1,0:T(8,128)(2,1)S(1)}, u32[]{:S(2)}, u32[]{:S(2)}) %all-to-all-start.1) | async-done | bytes 1277984 | tf_op jit(solution)/shard_map/all_to_all | solution.py:28
  85.6 0.9 convolution_convert_fusion.1
  87.4 2.3 %squeeze.64 = bf16[12,64,3,64]{1,0,3,2:T(8,128)(2,1)} reshape(bf16[1,768,192]{1,2,0:T(8,128)(2,1)} %get-tuple-element.74) | data formatting | bytes 589824 | tf_op jit(solution)/shard_map/squeeze | solution.py:293
  89.7 1.4 squeeze.63
  91.2 1.3 squeeze.62
  92.7 2.6 %fusion.1 = f32[12,3,64,64]{2,3,1,0:T(8,128)} fusion(bf16[12,64,3,64]{1,0,3,2:T(8,128)(2,1)S(1)} %copy-done.4, bf16[12,64,3,64]{1,0,3,2:T(8,128)(2,1)} %squeeze.63, pred[12,64,64]{1,2,0:T(8,128)(4,1)S(1)} %broadcast_or_fusion), kind=kOutput, calls=%fused_computation.5 | convolution fusion | flops 19169280 | bytes 1228800 | tf_op jit(solution)/shard_map/sqhd,skhd->shqk/dot_general | solution.py:60
  95.3 2.3 %fusion.2 = bf16[12,64,3,64]{1,3,2,0:T(8,128)(2,1)S(1)} fusion(f32[12,3,64,64]{2,3,1,0:T(8,128)} %fusion.1, bf16[12,64,3,64]{1,0,3,2:T(8,128)(2,1)} %squeeze.62), kind=kOutput, calls=%fused_computation.7 | convolution fusion | flops 19319104 | bytes 1179648 | tf_op jit(solution)/shard_map/shqk,skhd->sqhd/dot_general | solution.py:65
  98.5 1.7 convolution_convert_fusion
  100.2 3.7 %all-to-all-start.2 = ((bf16[4,192,768]{2,1,0:T(8,128)(2,1)}), bf16[4,192,768]{2,1,0:T(8,128)(2,1)S(1)}, u32[]{:S(2)}, u32[]{:S(2)}) async-start(bf16[4,192,768]{2,1,0:T(8,128)(2,1)} %bitcast.27), calls=%async_computation.2 | async-start | bytes 2359296 | tf_op jit(solution)/shard_map/all_to_all | solution.py:33
  107.5 12.0 %all-to-all-done.2 = bf16[4,192,768]{2,1,0:T(8,128)(2,1)S(1)} async-done(((bf16[4,192,768]{2,1,0:T(8,128)(2,1)}), bf16[4,192,768]{2,1,0:T(8,128)(2,1)S(1)}, u32[]{:S(2)}, u32[]{:S(2)}) %all-to-all-start.2) | async-done | bytes 1179680 | tf_op jit(solution)/shard_map/all_to_all | solution.py:33
  119.5 12.4 %all-to-all-start.3 = ((bf16[64,2,128]{2,1,0:T(2,128)(2,1)}), bf16[64,2,128]{2,1,0:T(2,128)(2,1)S(1)}, u32[]{:S(2)}, u32[]{:S(2)}) async-start(bf16[64,2,128]{2,1,0:T(2,128)(2,1)} %copy.185), calls=%async_computation.3 | async-start | bytes 65536 | tf_op jit(solution)/shard_map/all_to_all | solution.py:297
  132.2 9.1 %all-to-all-done.3 = bf16[64,2,128]{2,1,0:T(2,128)(2,1)S(1)} async-done(((bf16[64,2,128]{2,1,0:T(2,128)(2,1)}), bf16[64,2,128]{2,1,0:T(2,128)(2,1)S(1)}, u32[]{:S(2)}, u32[]{:S(2)}) %all-to-all-start.3) | async-done | bytes 32800 | tf_op jit(solution)/shard_map/all_to_all | solution.py:297
  141.3 8.7 %trunk_rows.1 = bf16[4,8,768]{2,1,0:T(8,128)(2,1)} custom-call(f32[192,768]{1,0:T(8,128)S(1)} %convert_add_fusion.res_ref, s32[1,192]{1,0:T(1,128)S(1)} %reshape.289.mask_ref, f32[5,768]{1,0:T(8,128)S(1)} %copy-done.1, bf16[1536,5376]{1,0:T(8,128)(2,1)} %all-gather.2.cloned.1.call-done.all_ref), custom_call_target="tpu_custom_call" | custom-call | tf_op jit(solution)/shard_map/trunk_rows/pallas_call | solution.py:135
  149.9 3.5 %all-to-all-start.4 = ((bf16[4,8,768]{2,1,0:T(8,128)(2,1)}), bf16[4,8,768]{2,1,0:T(8,128)(2,1)S(1)}, u32[]{:S(2)}, u32[]{:S(2)}) async-start(bf16[4,8,768]{2,1,0:T(8,128)(2,1)} %trunk_rows.1), calls=%async_computation.4 | async-start | bytes 98304 | tf_op jit(solution)/shard_map/all_to_all | solution.py:303
  153.4 1.8 fusion.85
  155.2 2.3 %all-to-all-done.4 = bf16[4,8,768]{2,1,0:T(8,128)(2,1)S(1)} async-done(((bf16[4,8,768]{2,1,0:T(8,128)(2,1)}), bf16[4,8,768]{2,1,0:T(8,128)(2,1)S(1)}, u32[]{:S(2)}, u32[]{:S(2)}) %all-to-all-start.4) | async-done | bytes 49184 | tf_op jit(solution)/shard_map/all_to_all | solution.py:303
  157.6 1.5 readout_mlp.1
  159.1 3.5 %all-to-all-start.5 = ((bf16[4,32,768]{2,1,0:T(8,128)(2,1)}), bf16[4,32,768]{2,1,0:T(8,128)(2,1)S(1)}, u32[]{:S(2)}, u32[]{:S(2)}) async-start(bf16[4,32,768]{2,1,0:T(8,128)(2,1)} %readout_mlp.1), calls=%async_computation.5 | async-start | bytes 393216 | tf_op jit(solution)/shard_map/all_to_all | solution.py:306
  162.8 5.0 %all-to-all-done.5 = bf16[4,32,768]{2,1,0:T(8,128)(2,1)S(1)} async-done(((bf16[4,32,768]{2,1,0:T(8,128)(2,1)}), bf16[4,32,768]{2,1,0:T(8,128)(2,1)S(1)}, u32[]{:S(2)}, u32[]{:S(2)}) %all-to-all-start.5) | async-done | bytes 196640 | tf_op jit(solution)/shard_map/all_to_all | solution.py:306
  169.3 7.0 %all-to-all-start.6 = ((bf16[64,2,768]{2,1,0:T(2,128)(2,1)}), bf16[64,2,768]{2,1,0:T(2,128)(2,1)S(1)}, u32[]{:S(2)}, u32[]{:S(2)}) async-start(bf16[64,2,768]{2,1,0:T(2,128)(2,1)} %reshape.300), calls=%async_computation.6 | async-start | bytes 393216 | tf_op jit(solution)/shard_map/all_to_all | solution.py:311
  177.1 11.5 %all-to-all-done.6 = bf16[64,2,768]{2,1,0:T(2,128)(2,1)S(1)} async-done(((bf16[64,2,768]{2,1,0:T(2,128)(2,1)}), bf16[64,2,768]{2,1,0:T(2,128)(2,1)S(1)}, u32[]{:S(2)}, u32[]{:S(2)}) %all-to-all-start.6) | async-done | bytes 196640 | tf_op jit(solution)/shard_map/all_to_all | solution.py:311
  191.8 4.4 %all-to-all-start.7 = ((bf16[64,2,768]{2,1,0:T(2,128)(2,1)}), bf16[64,2,768]{2,1,0:T(2,128)(2,1)S(1)}, u32[]{:S(2)}, u32[]{:S(2)}) async-start(bf16[64,2,768]{2,1,0:T(2,128)(2,1)} %reshape.302), calls=%async_computation.7 | async-start | bytes 393216 | tf_op jit(solution)/shard_map/all_to_all | solution.py:334
  196.2 1.0 convolution_bitcast_fusion.2
  199.4 0.9 convolution_bitcast_fusion.1
  200.3 0.9 convolution_bitcast_fusion
  201.2 7.2 %all-to-all-done.7 = bf16[64,2,768]{2,1,0:T(2,128)(2,1)S(1)} async-done(((bf16[64,2,768]{2,1,0:T(2,128)(2,1)}), bf16[64,2,768]{2,1,0:T(2,128)(2,1)S(1)}, u32[]{:S(2)}, u32[]{:S(2)}) %all-to-all-start.7) | async-done | bytes 196640 | tf_op jit(solution)/shard_map/all_to_all | solution.py:334
  (152 shorter events, 22.1 us)
Async XLA Ops:
  7.2 181.5 %copy-start = (bf16[1,768,256]{2,1,0:T(8,128)(2,1)S(1)}, bf16[1,768,256]{2,1,0:T(8,128)(2,1)}, u32[]{:S(2)}) copy-start(bf16[1,768,256]{2,1,0:T(8,128)(2,1)} %param.30) | copy-start | bytes 1179652
  7.2 9.5 %copy-start.2 = (bf16[192,768]{1,0:T(8,128)(2,1)S(1)}, bf16[192,768]{1,0:T(8,128)(2,1)}, u32[]{:S(2)}) copy-start(bf16[192,768]{1,0:T(8,128)(2,1)} %param.18) | copy-start | bytes 884740
  10.1 7.2 %copy-start.1 = (f32[5,768]{1,0:T(8,128)S(1)}, f32[5,768]{1,0:T(8,128)}, u32[]{:S(2)}) copy-start(f32[5,768]{1,0:T(8,128)} %gain_ref.3) | copy-start | bytes 46084
  11.8 10.5 %all-to-all-start = ((bf16[4,12,2304]{2,1,0:T(8,128)(2,1)}), bf16[4,12,2304]{2,1,0:T(8,128)(2,1)S(1)}, u32[]{:S(2)}, u32[]{:S(2)}) async-start(bf16[4,12,2304]{2,1,0:T(8,128)(2,1)} %broadcast_in_dim.42), calls=%async_computation | async-start | bytes 589824 | tf_op jit(solution)/shard_map/all_to_all | solution.py:28
  16.7 124.6 %all-gather.2.cloned.1.call-start = ((), (), s32[]{:S(2)}) async-start(), calls=%async_computation.8 | async-start | bytes 16773120 | tf_op jit(solution)/shard_map/all_gather | solution.py:275
  23.1 3.6 %copy-start.9 = (s32[3,64]{1,0:T(4,128)S(1)}, s32[3,64]{1,0:T(4,128)}, u32[]{:S(2)}) copy-start(s32[3,64]{1,0:T(4,128)} %param.19) | copy-start | bytes 2308
  23.5 4.1 %collective-permute-start = (bf16[12,5376]{1,0:T(8,128)(2,1)S(1)}, bf16[12,5376]{1,0:T(8,128)(2,1)S(1)}, u32[]{:S(2)}, u32[]{:S(2)}) collective-permute-start(bf16[12,5376]{1,0:T(8,128)(2,1)S(1)} %select_bitcast_fusion), channel_id=1, source_target_pairs={{0,4},{4,0},{1,5},{5,1},{2,6},{6,2},{3,7},{7,3},{8,12},{12,8},{9,1... | collective-permute-start | bytes 387080 | tf_op jit(solution)/shard_map/ppermute | solution.py:249
  27.6 18.1 %copy-start.10 = (s32[12,2]{0,1:T(2,128)S(1)}, s32[12,2]{0,1:T(2,128)}, u32[]{:S(2)}) copy-start(s32[12,2]{0,1:T(2,128)} %param.26) | copy-start | bytes 292
  28.6 2.7 %collective-permute-start.1 = (bf16[12,768]{1,0:T(8,128)(2,1)S(1)}, bf16[12,768]{1,0:T(8,128)(2,1)S(1)}, u32[]{:S(2)}, u32[]{:S(2)}) collective-permute-start(bf16[12,768]{1,0:T(8,128)(2,1)S(1)} %pad_maximum_fusion.7), channel_id=1, source_target_pairs={{0,32},{32,0},{64,96},{96,64},{128,160},{160,128},{192,224},{224,1... | collective-permute-start | bytes 55304 | tf_op jit(solution)/shard_map/ppermute | solution.py:279
  31.4 3.9 %collective-permute-start.2 = (bf16[24,768]{1,0:T(8,128)(2,1)S(1)}, bf16[24,768]{1,0:T(8,128)(2,1)S(1)}, u32[]{:S(2)}, u32[]{:S(2)}) collective-permute-start(bf16[24,768]{1,0:T(8,128)(2,1)S(1)} %pad_maximum_fusion.6), channel_id=1, source_target_pairs={{0,64},{32,96},{64,0},{96,32},{128,192},{160,224},{192,128},{224,1... | collective-permute-start | bytes 110600 | tf_op jit(solution)/shard_map/ppermute | solution.py:279
  35.4 8.9 %collective-permute-start.3 = (bf16[48,768]{1,0:T(8,128)(2,1)S(1)}, bf16[48,768]{1,0:T(8,128)(2,1)S(1)}, u32[]{:S(2)}, u32[]{:S(2)}) collective-permute-start(bf16[48,768]{1,0:T(8,128)(2,1)S(1)} %pad_maximum_fusion.5), channel_id=1, source_target_pairs={{0,128},{32,160},{64,192},{96,224},{128,0},{160,32},{192,64},{224,... | collective-permute-start | bytes 221192 | tf_op jit(solution)/shard_map/ppermute | solution.py:279
  44.4 4.7 %collective-permute-start.4 = (bf16[96,768]{1,0:T(8,128)(2,1)S(1)}, bf16[96,768]{1,0:T(8,128)(2,1)S(1)}, u32[]{:S(2)}, u32[]{:S(2)}) collective-permute-start(bf16[96,768]{1,0:T(8,128)(2,1)S(1)} %pad_maximum_fusion.4), channel_id=1, source_target_pairs={{0,8},{8,0},{16,24},{24,16},{1,9},{9,1},{17,25},{25,17},{2,10},{10... | collective-permute-start | bytes 442376 | tf_op jit(solution)/shard_map/ppermute | solution.py:279
  49.2 10.1 %collective-permute-start.5 = (bf16[192,768]{1,0:T(8,128)(2,1)S(1)}, bf16[192,768]{1,0:T(8,128)(2,1)S(1)}, u32[]{:S(2)}, u32[]{:S(2)}) collective-permute-start(bf16[192,768]{1,0:T(8,128)(2,1)S(1)} %pad_maximum_fusion.2), channel_id=1, source_target_pairs={{0,16},{8,24},{16,0},{24,8},{1,17},{9,25},{17,1},{25,9},{2,18},{10... | collective-permute-start | bytes 884744 | tf_op jit(solution)/shard_map/ppermute | solution.py:279
  52.3 10.7 %copy-start.6 = (bf16[12,2,56]{2,1,0:T(2,128)(2,1)S(1)}, bf16[12,2,56]{2,1,0:T(2,128)(2,1)}, u32[]{:S(2)}) copy-start(bf16[12,2,56]{2,1,0:T(2,128)(2,1)} %param.28) | copy-start | bytes 8068
  59.4 9.2 %collective-permute-start.6 = (bf16[384,768]{1,0:T(8,128)(2,1)S(1)}, bf16[384,768]{1,0:T(8,128)(2,1)S(1)}, u32[]{:S(2)}, u32[]{:S(2)}) collective-permute-start(bf16[384,768]{1,0:T(8,128)(2,1)S(1)} %pad_maximum_fusion.1), channel_id=1, source_target_pairs={{0,4},{4,0},{1,5},{5,1},{2,6},{6,2},{3,7},{7,3},{8,12},{12,8},{9,1... | collective-permute-start | bytes 1769480 | tf_op jit(solution)/shard_map/ppermute | solution.py:279
  64.3 3.9 %copy-start.8 = (bf16[12,2,56]{2,1,0:T(2,128)(2,1)S(1)}, bf16[12,2,56]{2,1,0:T(2,128)(2,1)}, u32[]{:S(2)}) copy-start(bf16[12,2,56]{2,1,0:T(2,128)(2,1)} %param.27) | copy-start | bytes 8068
  64.3 4.0 %copy-start.11 = (s32[12,1]{0,1:T(1,128)S(1)}, s32[12,1]{0,1:T(1,128)}, u32[]{:S(2)}) copy-start(s32[12,1]{0,1:T(1,128)} %param.25) | copy-start | bytes 148
  64.3 21.3 %all-to-all-start.1 = ((bf16[4,208,768]{2,1,0:T(8,128)(2,1)}), bf16[4,208,768]{2,1,0:T(8,128)(2,1)S(1)}, u32[]{:S(2)}, u32[]{:S(2)}) async-start(bf16[4,208,768]{2,1,0:T(8,128)(2,1)} %broadcast_in_dim.43), calls=%async_computation.1 | async-start | bytes 2555904 | tf_op jit(solution)/shard_map/all_to_all | solution.py:28
  91.1 1.6 copy-start.4
  100.2 5.2 %copy-start.15 = (s32[25]{0:T(128)S(1)}, s32[25]{0:T(128)}, u32[]{:S(2)}) copy-start(s32[25]{0:T(128)} %param.29) | copy-start | bytes 304
  100.2 19.3 %all-to-all-start.2 = ((bf16[4,192,768]{2,1,0:T(8,128)(2,1)}), bf16[4,192,768]{2,1,0:T(8,128)(2,1)S(1)}, u32[]{:S(2)}, u32[]{:S(2)}) async-start(bf16[4,192,768]{2,1,0:T(8,128)(2,1)} %bitcast.27), calls=%async_computation.2 | async-start | bytes 2359296 | tf_op jit(solution)/shard_map/all_to_all | solution.py:33
  103.9 28.2 %copy-start.3 = (bf16[192,768]{1,0:T(8,128)(2,1)S(1)}, bf16[192,768]{1,0:T(8,128)(2,1)}, u32[]{:S(2)}) copy-start(bf16[192,768]{1,0:T(8,128)(2,1)} %param.18) | copy-start | bytes 884740
  119.5 21.7 %all-to-all-start.3 = ((bf16[64,2,128]{2,1,0:T(2,128)(2,1)}), bf16[64,2,128]{2,1,0:T(2,128)(2,1)S(1)}, u32[]{:S(2)}, u32[]{:S(2)}) async-start(bf16[64,2,128]{2,1,0:T(2,128)(2,1)} %copy.185), calls=%async_computation.3 | async-start | bytes 65536 | tf_op jit(solution)/shard_map/all_to_all | solution.py:297
  149.9 7.6 %all-to-all-start.4 = ((bf16[4,8,768]{2,1,0:T(8,128)(2,1)}), bf16[4,8,768]{2,1,0:T(8,128)(2,1)S(1)}, u32[]{:S(2)}, u32[]{:S(2)}) async-start(bf16[4,8,768]{2,1,0:T(8,128)(2,1)} %trunk_rows.1), calls=%async_computation.4 | async-start | bytes 98304 | tf_op jit(solution)/shard_map/all_to_all | solution.py:303
  157.6 5.0 %copy-start.5 = (bf16[1,56,256]{2,1,0:T(8,128)(2,1)S(1)}, bf16[1,56,256]{2,1,0:T(8,128)(2,1)}, u32[]{:S(2)}) copy-start(bf16[1,56,256]{2,1,0:T(8,128)(2,1)} %param.31) | copy-start | bytes 86020
  159.1 17.7 %copy-start.7 = (bf16[1,20,256]{2,1,0:T(8,128)(2,1)S(1)}, bf16[1,20,256]{2,1,0:T(8,128)(2,1)}, u32[]{:S(2)}) copy-start(bf16[1,20,256]{2,1,0:T(8,128)(2,1)} %param.32) | copy-start | bytes 30724
  159.1 8.6 %all-to-all-start.5 = ((bf16[4,32,768]{2,1,0:T(8,128)(2,1)}), bf16[4,32,768]{2,1,0:T(8,128)(2,1)S(1)}, u32[]{:S(2)}, u32[]{:S(2)}) async-start(bf16[4,32,768]{2,1,0:T(8,128)(2,1)} %readout_mlp.1), calls=%async_computation.5 | async-start | bytes 393216 | tf_op jit(solution)/shard_map/all_to_all | solution.py:306
  168.5 20.4 %copy-start.13 = (bf16[1,256,256]{2,1,0:T(8,128)(2,1)S(1)}, bf16[1,256,256]{2,1,0:T(8,128)(2,1)}, u32[]{:S(2)}) copy-start(bf16[1,256,256]{2,1,0:T(8,128)(2,1)} %param.33) | copy-start | bytes 393220
  169.3 19.3 %all-to-all-start.6 = ((bf16[64,2,768]{2,1,0:T(2,128)(2,1)}), bf16[64,2,768]{2,1,0:T(2,128)(2,1)S(1)}, u32[]{:S(2)}, u32[]{:S(2)}) async-start(bf16[64,2,768]{2,1,0:T(2,128)(2,1)} %reshape.300), calls=%async_computation.6 | async-start | bytes 393216 | tf_op jit(solution)/shard_map/all_to_all | solution.py:311
  176.3 12.8 %copy-start.12 = (bf16[1,256,256]{2,1,0:T(8,128)(2,1)S(1)}, bf16[1,256,256]{2,1,0:T(8,128)(2,1)}, u32[]{:S(2)}) copy-start(bf16[1,256,256]{2,1,0:T(8,128)(2,1)} %param.34) | copy-start | bytes 393220
  188.9 0.8 copy-start.14
  191.8 16.7 %all-to-all-start.7 = ((bf16[64,2,768]{2,1,0:T(2,128)(2,1)}), bf16[64,2,768]{2,1,0:T(2,128)(2,1)S(1)}, u32[]{:S(2)}, u32[]{:S(2)}) async-start(bf16[64,2,768]{2,1,0:T(2,128)(2,1)} %reshape.302), calls=%async_computation.7 | async-start | bytes 393216 | tf_op jit(solution)/shard_map/all_to_all | solution.py:334
Sparse Core Ops, SparseCore 0:
  28.5 99.3 all-gather.1

commit v6 on v5

--- a/solution.py
+++ b/solution.py
@@ -274,15 +274,21 @@
     piece, rows = lax.optimization_barrier((piece, rows))
     gathered_weights = lax.all_gather(piece, ("c", "z", "y"), axis=0, tiled=True)
 
+    arrived = sent_to_all(rows, "mp")
     for axis, step in (("z", 1), ("z", 2), ("z", 4), ("y", 1), ("y", 2), ("c", 1)):
+        if step == 2 and axis == "y":
+            first_piece, arrived = lax.optimization_barrier((first_piece, arrived))
         swapped = [(k, k ^ step) for k in range(lax.axis_size(axis))]
         other = lax.ppermute(first_piece, axis, swapped)
         upper = (lax.axis_index(axis) // step) % 2 == 1
         low = jnp.where(upper, other, first_piece)
         high = jnp.where(upper, first_piece, other)
         first_piece = jnp.concatenate([low, high], axis=0)
-    first_weight = first_piece.reshape(2, 4, 8, 12, -1).transpose(2, 1, 0, 3, 4).reshape(D, -1)
-    arrived = sent_to_all(rows, "mp")
+    index = jnp.arange(D)
+    owner = index // 12
+    held = (owner % 2) * 32 + (owner // 2 % 4) * 8 + owner // 8
+    order = (held * 12 + index % 12)[:, None] == index[None, :]
+    first_weight = mm(order.astype(BF16), first_piece).astype(BF16)
     own_rows = normed.shape[0]
     gathered = arrived[:, :own_rows].reshape(-1, D)
     mask_group = arrived[:, own_rows, :own_rows].astype(jnp.int32).reshape(-1, SEQ)

time: 217 us -> 207 us (0.954)
  local copies, waits for them, and re-layouts: 26.9 us -> 17.7 us
    all_to_all x1, starting transfers between devices: 12.4 us -> 7.94 us  [on_device(): got = lax.all_to_all(sent, DP, split_axis=0, concat_axis=0, tiled=True)]
    reshape x2 -> x0, local copies, waits for them, and re-layouts: 4.4 us -> none  [on_device(): first_piece.reshape(2, 4, 8, 12, -1).transpose(2, 1, 0, 3, 4).reshape(D, -1)]
    ppermute x6, waiting for transfers between devices: 15.9 us -> 11.9 us  [on_device(): other = lax.ppermute(first_piece, axis, swapped)]
    all_gather x1, waiting for transfers between devices: 0.01 us -> 2.41 us  [on_device(): lax.all_gather(piece, ('c', 'z', 'y'), axis=0, tiled=True)]
  transfers between devices with their start and end apart: 16 -> 16, of which waited for: 14 -> 15; matrix products, arithmetic and copies ran while one was open for 17% -> 14% of each run, Pallas kernels for 0% -> 0%
where the time goes in v6:
time: 207 us; the launch traced here: 205 us
  waiting for transfers between devices  76.7 us (37%)
  starting transfers between devices  62.8 us (30%)
  local copies, waits for them, and re-layouts  17.7 us (9%)
  matrix products  16.9 us (8%)
  between operations  14.8 us (7%)
  Pallas kernels  10.2 us (5%)
  other arithmetic  6.37 us (3%)
    ppermute x6, starting transfers between devices, on_device(): other = lax.ppermute(first_piece, axis, swapped)  19.3 us
    all_to_all x2, waiting for transfers between devices, sent_to_all(): return lax.all_to_all(copies, axis, split_axis=0, concat_axis=0, tiled=True)  13.8 us
    all_to_all x1, waiting for transfers between devices, summed_on_arrival(): lax.all_to_all(pieces, axis, split_axis=0, concat_axis=0, tiled=True)  12.5 us
    ppermute x6, waiting for transfers between devices, on_device(): other = lax.ppermute(first_piece, axis, swapped)  11.9 us
    all_to_all x1, waiting for transfers between devices, on_device(): features = lax.all_to_all(send, DP, split_axis=0, concat_axis=0, tiled=True)  11.3 us
    all_to_all x1, waiting for transfers between devices, on_device(): got = lax.all_to_all(sent, DP, split_axis=0, concat_axis=0, tiled=True)  9.41 us
    pallas_call x1, Pallas kernels, trunk_rows(): pl.pallas_call(trunk_rows_kernel, out_shape=jax.ShapeDtypeStruct((4, 8, D...  8.66 us
    all_to_all x1, starting transfers between devices, on_device(): features = lax.all_to_all(send, DP, split_axis=0, concat_axis=0, tiled=True)  8.56 us
  transfers between devices with their start and end apart: 16, of which 15 were waited for; matrix products, arithmetic and copies ran while one was open for 14% of the time, Pallas kernels for 0%

profile of v6, /device:TPU:1, one launch (start us, length us, event | category | flops | bytes accessed | tf_op | source)
XLA Modules:
  0.0 205.4 jit_solution(6225450227725809486)
XLA Ops:
  7.2 0.8 fusion.115
  8.0 0.9 fusion.114
  9.1 1.0 slice_reduce_fusion
  10.1 0.9 fusion.113
  11.8 4.8 %all-to-all-start = ((bf16[4,12,2304]{2,1,0:T(8,128)(2,1)}), bf16[4,12,2304]{2,1,0:T(8,128)(2,1)S(1)}, u32[]{:S(2)}, u32[]{:S(2)}) async-start(bf16[4,12,2304]{2,1,0:T(8,128)(2,1)} %broadcast_in_dim.42), calls=%async_computation | async-start | bytes 589824 | tf_op jit(solution)/shard_map/all_to_all | solution.py:28
  17.2 5.1 %all-to-all-done = bf16[4,12,2304]{2,1,0:T(8,128)(2,1)S(1)} async-done(((bf16[4,12,2304]{2,1,0:T(8,128)(2,1)}), bf16[4,12,2304]{2,1,0:T(8,128)(2,1)S(1)}, u32[]{:S(2)}, u32[]{:S(2)}) %all-to-all-start) | async-done | bytes 221216 | tf_op jit(solution)/shard_map/all_to_all | solution.py:28
  23.5 3.0 %collective-permute-start.4 = (bf16[12,5376]{1,0:T(8,128)(2,1)S(1)}, bf16[12,5376]{1,0:T(8,128)(2,1)S(1)}, u32[]{:S(2)}, u32[]{:S(2)}) collective-permute-start(bf16[12,5376]{1,0:T(8,128)(2,1)S(1)} %select_bitcast_fusion), channel_id=1, source_target_pairs={{0,4},{4,0},{1,5},{5,1},{2,6},{6,2},{3,7},{7,3},{8,12},{12,8},{9,1... | collective-permute-start | bytes 387080 | tf_op jit(solution)/shard_map/ppermute | solution.py:249
  28.6 1.0 collective-permute-start
  30.0 1.3 collective-permute-done
  31.4 2.6 %collective-permute-start.1 = (bf16[24,768]{1,0:T(8,128)(2,1)S(1)}, bf16[24,768]{1,0:T(8,128)(2,1)S(1)}, u32[]{:S(2)}, u32[]{:S(2)}) collective-permute-start(bf16[24,768]{1,0:T(8,128)(2,1)S(1)} %pad_maximum_fusion.5), channel_id=1, source_target_pairs={{0,64},{32,96},{64,0},{96,32},{128,192},{160,224},{192,128},{224,1... | collective-permute-start | bytes 110600 | tf_op jit(solution)/shard_map/ppermute | solution.py:282
  34.0 1.3 collective-permute-done.1
  35.4 6.2 %collective-permute-start.2 = (bf16[48,768]{1,0:T(8,128)(2,1)S(1)}, bf16[48,768]{1,0:T(8,128)(2,1)S(1)}, u32[]{:S(2)}, u32[]{:S(2)}) collective-permute-start(bf16[48,768]{1,0:T(8,128)(2,1)S(1)} %pad_maximum_fusion.4), channel_id=1, source_target_pairs={{0,128},{32,160},{64,192},{96,224},{128,0},{160,32},{192,64},{224,... | collective-permute-start | bytes 221192 | tf_op jit(solution)/shard_map/ppermute | solution.py:282
  41.6 1.1 broadcast_in_dim.43
  42.8 3.5 %all-to-all-start.1 = ((bf16[4,208,768]{2,1,0:T(8,128)(2,1)}), bf16[4,208,768]{2,1,0:T(8,128)(2,1)S(1)}, u32[]{:S(2)}, u32[]{:S(2)}) async-start(bf16[4,208,768]{2,1,0:T(8,128)(2,1)} %broadcast_in_dim.43), calls=%async_computation.1 | async-start | bytes 2555904 | tf_op jit(solution)/shard_map/all_to_all | solution.py:28
  46.4 1.4 collective-permute-start.3
  48.0 3.9 %collective-permute-done.3 = bf16[96,768]{1,0:T(8,128)(2,1)S(1)} collective-permute-done((bf16[96,768]{1,0:T(8,128)(2,1)S(1)}, bf16[96,768]{1,0:T(8,128)(2,1)S(1)}, u32[]{:S(2)}, u32[]{:S(2)}) %collective-permute-start.3) | collective-permute-done | bytes 147488 | tf_op jit(solution)/shard_map/ppermute | solution.py:282
  52.0 8.7 %all-to-all-done.1 = bf16[4,208,768]{2,1,0:T(8,128)(2,1)S(1)} async-done(((bf16[4,208,768]{2,1,0:T(8,128)(2,1)}), bf16[4,208,768]{2,1,0:T(8,128)(2,1)S(1)}, u32[]{:S(2)}, u32[]{:S(2)}) %all-to-all-start.1) | async-done | bytes 1277984 | tf_op jit(solution)/shard_map/all_to_all | solution.py:28
  60.7 2.9 %collective-permute-start.5 = (bf16[192,768]{1,0:T(8,128)(2,1)S(1)}, bf16[192,768]{1,0:T(8,128)(2,1)S(1)}, u32[]{:S(2)}, u32[]{:S(2)}) collective-permute-start(bf16[192,768]{1,0:T(8,128)(2,1)S(1)} %pad_maximum_fusion.1), channel_id=1, source_target_pairs={{0,16},{8,24},{16,0},{24,8},{1,17},{9,25},{17,1},{25,9},{2,18},{10... | collective-permute-start | bytes 884744 | tf_op jit(solution)/shard_map/ppermute | solution.py:282
  63.9 3.8 %collective-permute-done.5 = bf16[192,768]{1,0:T(8,128)(2,1)S(1)} collective-permute-done((bf16[192,768]{1,0:T(8,128)(2,1)S(1)}, bf16[192,768]{1,0:T(8,128)(2,1)S(1)}, u32[]{:S(2)}, u32[]{:S(2)}) %collective-permute-start.5) | collective-permute-done | bytes 294944 | tf_op jit(solution)/shard_map/ppermute | solution.py:282
  67.8 0.8 pad_maximum_fusion
  68.6 5.3 %collective-permute-start.6 = (bf16[384,768]{1,0:T(8,128)(2,1)}, bf16[384,768]{1,0:T(8,128)(2,1)S(1)}, u32[]{:S(2)}, u32[]{:S(2)}) collective-permute-start(bf16[384,768]{1,0:T(8,128)(2,1)} %pad_maximum_fusion), channel_id=1, source_target_pairs={{0,4},{4,0},{1,5},{5,1},{2,6},{6,2},{3,7},{7,3},{8,12},{12,8},{9,1... | collective-permute-start | bytes 1769480 | tf_op jit(solution)/shard_map/ppermute | solution.py:282
  74.2 1.5 collective-permute-done.6
  76.0 1.3 fusion.1
  77.3 0.9 convolution_convert_fusion.1
  78.8 1.4 squeeze.63
  80.7 2.6 %fusion.3 = f32[12,3,64,64]{2,3,1,0:T(8,128)} fusion(bf16[12,64,3,64]{1,0,3,2:T(8,128)(2,1)S(1)} %squeeze.64, bf16[12,64,3,64]{1,0,3,2:T(8,128)(2,1)} %squeeze.63, pred[12,64,64]{1,2,0:T(8,128)(4,1)S(1)} %broadcast_or_fusion), kind=kOutput, calls=%fused_computation.8 | convolution fusion | flops 19169280 | bytes 1228800 | tf_op jit(solution)/shard_map/sqhd,skhd->shqk/dot_general | solution.py:60
  83.3 2.1 %fusion.4 = bf16[12,64,3,64]{1,3,2,0:T(8,128)(2,1)S(1)} fusion(f32[12,3,64,64]{2,3,1,0:T(8,128)} %fusion.3, bf16[12,64,3,64]{1,0,3,2:T(8,128)(2,1)S(1)} %squeeze.62), kind=kOutput, calls=%fused_computation.10 | convolution fusion | flops 19319104 | bytes 1179648 | tf_op jit(solution)/shard_map/shqk,skhd->sqhd/dot_general | solution.py:65
  86.3 2.5 %convolution_convert_fusion = bf16[768,768]{1,0:T(8,128)(2,1)} fusion(bf16[768,192]{0,1:T(8,128)(2,1)S(1)} %reshape.357, bf16[768,768]{0,1:T(8,128)(2,1)} %copy-done.4), kind=kOutput, calls=%fused_computation.4 | convolution fusion | flops 227082240 | bytes 1769472 | tf_op jit(solution)/shard_map/tk,dk->td/dot_general | solution.py:48
  88.9 3.7 %all-to-all-start.2 = ((bf16[4,192,768]{2,1,0:T(8,128)(2,1)}), bf16[4,192,768]{2,1,0:T(8,128)(2,1)S(1)}, u32[]{:S(2)}, u32[]{:S(2)}) async-start(bf16[4,192,768]{2,1,0:T(8,128)(2,1)} %bitcast.26), calls=%async_computation.2 | async-start | bytes 2359296 | tf_op jit(solution)/shard_map/all_to_all | solution.py:33
  96.1 12.5 %all-to-all-done.2 = bf16[4,192,768]{2,1,0:T(8,128)(2,1)S(1)} async-done(((bf16[4,192,768]{2,1,0:T(8,128)(2,1)}), bf16[4,192,768]{2,1,0:T(8,128)(2,1)S(1)}, u32[]{:S(2)}, u32[]{:S(2)}) %all-to-all-start.2) | async-done | bytes 1179680 | tf_op jit(solution)/shard_map/all_to_all | solution.py:33
  108.7 7.9 %all-to-all-start.3 = ((bf16[64,2,128]{2,1,0:T(2,128)(2,1)}), bf16[64,2,128]{2,1,0:T(2,128)(2,1)S(1)}, u32[]{:S(2)}, u32[]{:S(2)}) async-start(bf16[64,2,128]{2,1,0:T(2,128)(2,1)} %copy.180), calls=%async_computation.3 | async-start | bytes 65536 | tf_op jit(solution)/shard_map/all_to_all | solution.py:303
  116.8 9.4 %all-to-all-done.3 = bf16[64,2,128]{2,1,0:T(2,128)(2,1)S(1)} async-done(((bf16[64,2,128]{2,1,0:T(2,128)(2,1)}), bf16[64,2,128]{2,1,0:T(2,128)(2,1)S(1)}, u32[]{:S(2)}, u32[]{:S(2)}) %all-to-all-start.3) | async-done | bytes 32800 | tf_op jit(solution)/shard_map/all_to_all | solution.py:303
  126.2 2.4 %all-gather.2.cloned.1.call-done.all_ref = bf16[1536,5376]{1,0:T(8,128)(2,1)} async-done(((bf16[24,5376]{1,0:T(8,128)(2,1)}), bf16[1536,5376]{1,0:T(8,128)(2,1)}) %all-gather.2.cloned.1.call-update) | async-done | bytes 16515088 | tf_op jit(solution)/shard_map/all_gather | solution.py:275
  128.7 8.7 %trunk_rows.1 = bf16[4,8,768]{2,1,0:T(8,128)(2,1)} custom-call(f32[192,768]{1,0:T(8,128)S(1)} %convert_add_fusion.res_ref, s32[1,192]{1,0:T(1,128)S(1)} %reshape.354.mask_ref, f32[5,768]{1,0:T(8,128)S(1)} %copy-done.1, bf16[1536,5376]{1,0:T(8,128)(2,1)} %all-gather.2.cloned.1.call-done.all_ref), custom_call_target="tpu_custom_call" | custom-call | tf_op jit(solution)/shard_map/trunk_rows/pallas_call | solution.py:135
  137.3 4.0 %all-to-all-start.4 = ((bf16[4,8,768]{2,1,0:T(8,128)(2,1)}), bf16[4,8,768]{2,1,0:T(8,128)(2,1)S(1)}, u32[]{:S(2)}, u32[]{:S(2)}) async-start(bf16[4,8,768]{2,1,0:T(8,128)(2,1)} %trunk_rows.1), calls=%async_computation.4 | async-start | bytes 98304 | tf_op jit(solution)/shard_map/all_to_all | solution.py:309
  141.3 1.8 fusion.111
  143.1 2.6 %all-to-all-done.4 = bf16[4,8,768]{2,1,0:T(8,128)(2,1)S(1)} async-done(((bf16[4,8,768]{2,1,0:T(8,128)(2,1)}), bf16[4,8,768]{2,1,0:T(8,128)(2,1)S(1)}, u32[]{:S(2)}, u32[]{:S(2)}) %all-to-all-start.4) | async-done | bytes 49184 | tf_op jit(solution)/shard_map/all_to_all | solution.py:309
  145.7 1.5 readout_mlp.1
  147.2 3.5 %all-to-all-start.5 = ((bf16[4,32,768]{2,1,0:T(8,128)(2,1)}), bf16[4,32,768]{2,1,0:T(8,128)(2,1)S(1)}, u32[]{:S(2)}, u32[]{:S(2)}) async-start(bf16[4,32,768]{2,1,0:T(8,128)(2,1)} %readout_mlp.1), calls=%async_computation.5 | async-start | bytes 393216 | tf_op jit(solution)/shard_map/all_to_all | solution.py:312
  150.9 5.0 %all-to-all-done.5 = bf16[4,32,768]{2,1,0:T(8,128)(2,1)S(1)} async-done(((bf16[4,32,768]{2,1,0:T(8,128)(2,1)}), bf16[4,32,768]{2,1,0:T(8,128)(2,1)S(1)}, u32[]{:S(2)}, u32[]{:S(2)}) %all-to-all-start.5) | async-done | bytes 196640 | tf_op jit(solution)/shard_map/all_to_all | solution.py:312
  157.4 8.6 %all-to-all-start.6 = ((bf16[64,2,768]{2,1,0:T(2,128)(2,1)}), bf16[64,2,768]{2,1,0:T(2,128)(2,1)S(1)}, u32[]{:S(2)}, u32[]{:S(2)}) async-start(bf16[64,2,768]{2,1,0:T(2,128)(2,1)} %reshape.362), calls=%async_computation.6 | async-start | bytes 393216 | tf_op jit(solution)/shard_map/all_to_all | solution.py:317
  166.7 11.3 %all-to-all-done.6 = bf16[64,2,768]{2,1,0:T(2,128)(2,1)S(1)} async-done(((bf16[64,2,768]{2,1,0:T(2,128)(2,1)}), bf16[64,2,768]{2,1,0:T(2,128)(2,1)S(1)}, u32[]{:S(2)}, u32[]{:S(2)}) %all-to-all-start.6) | async-done | bytes 196640 | tf_op jit(solution)/shard_map/all_to_all | solution.py:317
  181.2 4.5 %all-to-all-start.7 = ((bf16[64,2,768]{2,1,0:T(2,128)(2,1)}), bf16[64,2,768]{2,1,0:T(2,128)(2,1)S(1)}, u32[]{:S(2)}, u32[]{:S(2)}) async-start(bf16[64,2,768]{2,1,0:T(2,128)(2,1)} %reshape.364), calls=%async_computation.7 | async-start | bytes 393216 | tf_op jit(solution)/shard_map/all_to_all | solution.py:340
  185.6 1.0 convolution_bitcast_fusion.2
  188.0 0.8 convolution_bitcast_fusion.4
  188.8 0.9 convolution_bitcast_fusion.1
  189.7 0.9 convolution_bitcast_fusion
  190.7 7.1 %all-to-all-done.7 = bf16[64,2,768]{2,1,0:T(2,128)(2,1)S(1)} async-done(((bf16[64,2,768]{2,1,0:T(2,128)(2,1)}), bf16[64,2,768]{2,1,0:T(2,128)(2,1)S(1)}, u32[]{:S(2)}, u32[]{:S(2)}) %all-to-all-start.7) | async-done | bytes 196640 | tf_op jit(solution)/shard_map/all_to_all | solution.py:340
  (151 shorter events, 19.7 us)
Async XLA Ops:
  7.2 170.9 %copy-start = (bf16[1,768,256]{2,1,0:T(8,128)(2,1)S(1)}, bf16[1,768,256]{2,1,0:T(8,128)(2,1)}, u32[]{:S(2)}) copy-start(bf16[1,768,256]{2,1,0:T(8,128)(2,1)} %param.30) | copy-start | bytes 1179652
  7.2 9.5 %copy-start.3 = (bf16[192,768]{1,0:T(8,128)(2,1)S(1)}, bf16[192,768]{1,0:T(8,128)(2,1)}, u32[]{:S(2)}) copy-start(bf16[192,768]{1,0:T(8,128)(2,1)} %param.18) | copy-start | bytes 884740
  10.0 7.2 %copy-start.1 = (f32[5,768]{1,0:T(8,128)S(1)}, f32[5,768]{1,0:T(8,128)}, u32[]{:S(2)}) copy-start(f32[5,768]{1,0:T(8,128)} %gain_ref.3) | copy-start | bytes 46084
  11.8 10.5 %all-to-all-start = ((bf16[4,12,2304]{2,1,0:T(8,128)(2,1)}), bf16[4,12,2304]{2,1,0:T(8,128)(2,1)S(1)}, u32[]{:S(2)}, u32[]{:S(2)}) async-start(bf16[4,12,2304]{2,1,0:T(8,128)(2,1)} %broadcast_in_dim.42), calls=%async_computation | async-start | bytes 589824 | tf_op jit(solution)/shard_map/all_to_all | solution.py:28
  16.6 112.0 %all-gather.2.cloned.1.call-start = ((), (), s32[]{:S(2)}) async-start(), calls=%async_computation.8 | async-start | bytes 16773120 | tf_op jit(solution)/shard_map/all_gather | solution.py:275
  23.1 3.6 %copy-start.9 = (s32[3,64]{1,0:T(4,128)S(1)}, s32[3,64]{1,0:T(4,128)}, u32[]{:S(2)}) copy-start(s32[3,64]{1,0:T(4,128)} %param.19) | copy-start | bytes 2308
  23.5 4.1 %collective-permute-start.4 = (bf16[12,5376]{1,0:T(8,128)(2,1)S(1)}, bf16[12,5376]{1,0:T(8,128)(2,1)S(1)}, u32[]{:S(2)}, u32[]{:S(2)}) collective-permute-start(bf16[12,5376]{1,0:T(8,128)(2,1)S(1)} %select_bitcast_fusion), channel_id=1, source_target_pairs={{0,4},{4,0},{1,5},{5,1},{2,6},{6,2},{3,7},{7,3},{8,12},{12,8},{9,1... | collective-permute-start | bytes 387080 | tf_op jit(solution)/shard_map/ppermute | solution.py:249
  26.8 2.8 %copy-start.10 = (s32[12,2]{0,1:T(2,128)S(1)}, s32[12,2]{0,1:T(2,128)}, u32[]{:S(2)}) copy-start(s32[12,2]{0,1:T(2,128)} %param.26) | copy-start | bytes 292
  26.8 14.7 %copy-start.6 = (bf16[12,2,56]{2,1,0:T(2,128)(2,1)S(1)}, bf16[12,2,56]{2,1,0:T(2,128)(2,1)}, u32[]{:S(2)}) copy-start(bf16[12,2,56]{2,1,0:T(2,128)(2,1)} %param.28) | copy-start | bytes 8068
  26.9 14.7 %copy-start.8 = (bf16[12,2,56]{2,1,0:T(2,128)(2,1)S(1)}, bf16[12,2,56]{2,1,0:T(2,128)(2,1)}, u32[]{:S(2)}) copy-start(bf16[12,2,56]{2,1,0:T(2,128)(2,1)} %param.27) | copy-start | bytes 8068
  28.6 2.7 %collective-permute-start = (bf16[12,768]{1,0:T(8,128)(2,1)S(1)}, bf16[12,768]{1,0:T(8,128)(2,1)S(1)}, u32[]{:S(2)}, u32[]{:S(2)}) collective-permute-start(bf16[12,768]{1,0:T(8,128)(2,1)S(1)} %pad_maximum_fusion.6), channel_id=1, source_target_pairs={{0,32},{32,0},{64,96},{96,64},{128,160},{160,128},{192,224},{224,1... | collective-permute-start | bytes 55304 | tf_op jit(solution)/shard_map/ppermute | solution.py:282
  31.4 3.9 %collective-permute-start.1 = (bf16[24,768]{1,0:T(8,128)(2,1)S(1)}, bf16[24,768]{1,0:T(8,128)(2,1)S(1)}, u32[]{:S(2)}, u32[]{:S(2)}) collective-permute-start(bf16[24,768]{1,0:T(8,128)(2,1)S(1)} %pad_maximum_fusion.5), channel_id=1, source_target_pairs={{0,64},{32,96},{64,0},{96,32},{128,192},{160,224},{192,128},{224,1... | collective-permute-start | bytes 110600 | tf_op jit(solution)/shard_map/ppermute | solution.py:282
  35.4 11.0 %collective-permute-start.2 = (bf16[48,768]{1,0:T(8,128)(2,1)S(1)}, bf16[48,768]{1,0:T(8,128)(2,1)S(1)}, u32[]{:S(2)}, u32[]{:S(2)}) collective-permute-start(bf16[48,768]{1,0:T(8,128)(2,1)S(1)} %pad_maximum_fusion.4), channel_id=1, source_target_pairs={{0,128},{32,160},{64,192},{96,224},{128,0},{160,32},{192,64},{224,... | collective-permute-start | bytes 221192 | tf_op jit(solution)/shard_map/ppermute | solution.py:282
  42.8 17.9 %all-to-all-start.1 = ((bf16[4,208,768]{2,1,0:T(8,128)(2,1)}), bf16[4,208,768]{2,1,0:T(8,128)(2,1)S(1)}, u32[]{:S(2)}, u32[]{:S(2)}) async-start(bf16[4,208,768]{2,1,0:T(8,128)(2,1)} %broadcast_in_dim.43), calls=%async_computation.1 | async-start | bytes 2555904 | tf_op jit(solution)/shard_map/all_to_all | solution.py:28
  46.3 17.3 %copy-start.11 = (s32[12,1]{0,1:T(1,128)S(1)}, s32[12,1]{0,1:T(1,128)}, u32[]{:S(2)}) copy-start(s32[12,1]{0,1:T(1,128)} %param.25) | copy-start | bytes 148
  46.4 5.5 %collective-permute-start.3 = (bf16[96,768]{1,0:T(8,128)(2,1)S(1)}, bf16[96,768]{1,0:T(8,128)(2,1)S(1)}, u32[]{:S(2)}, u32[]{:S(2)}) collective-permute-start(bf16[96,768]{1,0:T(8,128)(2,1)S(1)} %pad_maximum_fusion.3), channel_id=1, source_target_pairs={{0,8},{8,0},{16,24},{24,16},{1,9},{9,1},{17,25},{25,17},{2,10},{10... | collective-permute-start | bytes 442376 | tf_op jit(solution)/shard_map/ppermute | solution.py:282
  60.7 13.2 %copy-start.2 = (bf16[4,208,768]{2,1,0:T(8,128)(2,1)}, bf16[4,208,768]{2,1,0:T(8,128)(2,1)S(1)}, u32[]{:S(2)}) copy-start(bf16[4,208,768]{2,1,0:T(8,128)(2,1)S(1)} %all-to-all-done.1) | copy-start | bytes 3833860
  60.7 7.1 %collective-permute-start.5 = (bf16[192,768]{1,0:T(8,128)(2,1)S(1)}, bf16[192,768]{1,0:T(8,128)(2,1)S(1)}, u32[]{:S(2)}, u32[]{:S(2)}) collective-permute-start(bf16[192,768]{1,0:T(8,128)(2,1)S(1)} %pad_maximum_fusion.1), channel_id=1, source_target_pairs={{0,16},{8,24},{16,0},{24,8},{1,17},{9,25},{17,1},{25,9},{2,18},{10... | collective-permute-start | bytes 884744 | tf_op jit(solution)/shard_map/ppermute | solution.py:282
  68.6 7.1 %collective-permute-start.6 = (bf16[384,768]{1,0:T(8,128)(2,1)}, bf16[384,768]{1,0:T(8,128)(2,1)S(1)}, u32[]{:S(2)}, u32[]{:S(2)}) collective-permute-start(bf16[384,768]{1,0:T(8,128)(2,1)} %pad_maximum_fusion), channel_id=1, source_target_pairs={{0,4},{4,0},{1,5},{5,1},{2,6},{6,2},{3,7},{7,3},{8,12},{12,8},{9,1... | collective-permute-start | bytes 1769480 | tf_op jit(solution)/shard_map/ppermute | solution.py:282
  76.0 1.3 slice-start
  77.3 1.0 copy-start.4
  88.9 5.2 %copy-start.15 = (s32[25]{0:T(128)S(1)}, s32[25]{0:T(128)}, u32[]{:S(2)}) copy-start(s32[25]{0:T(128)} %param.29) | copy-start | bytes 304
  88.9 19.8 %all-to-all-start.2 = ((bf16[4,192,768]{2,1,0:T(8,128)(2,1)}), bf16[4,192,768]{2,1,0:T(8,128)(2,1)S(1)}, u32[]{:S(2)}, u32[]{:S(2)}) async-start(bf16[4,192,768]{2,1,0:T(8,128)(2,1)} %bitcast.26), calls=%async_computation.2 | async-start | bytes 2359296 | tf_op jit(solution)/shard_map/all_to_all | solution.py:33
  108.7 17.6 %all-to-all-start.3 = ((bf16[64,2,128]{2,1,0:T(2,128)(2,1)}), bf16[64,2,128]{2,1,0:T(2,128)(2,1)S(1)}, u32[]{:S(2)}, u32[]{:S(2)}) async-start(bf16[64,2,128]{2,1,0:T(2,128)(2,1)} %copy.180), calls=%async_computation.3 | async-start | bytes 65536 | tf_op jit(solution)/shard_map/all_to_all | solution.py:303
  137.3 8.4 %all-to-all-start.4 = ((bf16[4,8,768]{2,1,0:T(8,128)(2,1)}), bf16[4,8,768]{2,1,0:T(8,128)(2,1)S(1)}, u32[]{:S(2)}, u32[]{:S(2)}) async-start(bf16[4,8,768]{2,1,0:T(8,128)(2,1)} %trunk_rows.1), calls=%async_computation.4 | async-start | bytes 98304 | tf_op jit(solution)/shard_map/all_to_all | solution.py:309
  145.7 5.0 %copy-start.5 = (bf16[1,56,256]{2,1,0:T(8,128)(2,1)S(1)}, bf16[1,56,256]{2,1,0:T(8,128)(2,1)}, u32[]{:S(2)}) copy-start(bf16[1,56,256]{2,1,0:T(8,128)(2,1)} %param.31) | copy-start | bytes 86020
  147.2 19.3 %copy-start.7 = (bf16[1,20,256]{2,1,0:T(8,128)(2,1)S(1)}, bf16[1,20,256]{2,1,0:T(8,128)(2,1)}, u32[]{:S(2)}) copy-start(bf16[1,20,256]{2,1,0:T(8,128)(2,1)} %param.32) | copy-start | bytes 30724
  147.2 8.6 %all-to-all-start.5 = ((bf16[4,32,768]{2,1,0:T(8,128)(2,1)}), bf16[4,32,768]{2,1,0:T(8,128)(2,1)S(1)}, u32[]{:S(2)}, u32[]{:S(2)}) async-start(bf16[4,32,768]{2,1,0:T(8,128)(2,1)} %readout_mlp.1), calls=%async_computation.5 | async-start | bytes 393216 | tf_op jit(solution)/shard_map/all_to_all | solution.py:312
  156.6 21.6 %copy-start.13 = (bf16[1,256,256]{2,1,0:T(8,128)(2,1)S(1)}, bf16[1,256,256]{2,1,0:T(8,128)(2,1)}, u32[]{:S(2)}) copy-start(bf16[1,256,256]{2,1,0:T(8,128)(2,1)} %param.33) | copy-start | bytes 393220
  157.4 20.6 %all-to-all-start.6 = ((bf16[64,2,768]{2,1,0:T(2,128)(2,1)}), bf16[64,2,768]{2,1,0:T(2,128)(2,1)S(1)}, u32[]{:S(2)}, u32[]{:S(2)}) async-start(bf16[64,2,768]{2,1,0:T(2,128)(2,1)} %reshape.362), calls=%async_computation.6 | async-start | bytes 393216 | tf_op jit(solution)/shard_map/all_to_all | solution.py:317
  166.0 12.5 %copy-start.12 = (bf16[1,256,256]{2,1,0:T(8,128)(2,1)S(1)}, bf16[1,256,256]{2,1,0:T(8,128)(2,1)}, u32[]{:S(2)}) copy-start(bf16[1,256,256]{2,1,0:T(8,128)(2,1)} %param.34) | copy-start | bytes 393220
  178.3 0.8 copy-start.14
  181.2 16.6 %all-to-all-start.7 = ((bf16[64,2,768]{2,1,0:T(2,128)(2,1)}), bf16[64,2,768]{2,1,0:T(2,128)(2,1)S(1)}, u32[]{:S(2)}, u32[]{:S(2)}) async-start(bf16[64,2,768]{2,1,0:T(2,128)(2,1)} %reshape.364), calls=%async_computation.7 | async-start | bytes 393216 | tf_op jit(solution)/shard_map/all_to_all | solution.py:340
Sparse Core Ops, SparseCore 0:
  28.5 100.1 all-gather.1

commit v7 on v6

--- a/solution.py
+++ b/solution.py
@@ -239,7 +239,17 @@
         axis=1,
     )
     groups = full.shape[1] // width
-    full = sent_to_all(full, "mp").reshape(2, 2, 12, groups, width)
+    pieces = [full] + [
+        lax.ppermute(full, "mp", [(k, k ^ step) for k in range(4)]) for step in (1, 2, 3)
+    ]
+    ordered = []
+    for member in range(4):
+        apart = my_model ^ member
+        piece = pieces[3]
+        for step in range(3):
+            piece = jnp.where(apart == step, pieces[step], piece)
+        ordered.append(piece)
+    full = jnp.stack(ordered).reshape(2, 2, 12, groups, width)
     full = full.transpose(0, 2, 3, 1, 4).reshape(2, 12, -1)
     share = jnp.stack([mlp_in[1], mlp_out[1].T], axis=1).reshape(12, 2, 2, -1)
     share = share.transpose(2, 0, 1, 3).reshape(2, 12, -1)

time: 207 us -> 204 us (0.986)
    all_to_all x2 -> x1, waiting for transfers between devices: 13.8 us -> 8.68 us  [sent_to_all(): return lax.all_to_all(copies, axis, split_axis=0, concat_axis=0, tiled=True)]
    all_to_all x2 -> x1, starting transfers between devices: 8.37 us -> 3.54 us  [sent_to_all(): return lax.all_to_all(copies, axis, split_axis=0, concat_axis=0, tiled=True)]
    ppermute x0 -> x3, starting transfers between devices: none -> 4.45 us  [on_device(): lax.ppermute(full, 'mp', [(k, k ^ step) for k in range(4)])]
    ppermute x0 -> x3, waiting for transfers between devices: none -> 3.2 us  [on_device(): lax.ppermute(full, 'mp', [(k, k ^ step) for k in range(4)])]
  transfers between devices with their start and end apart: 16 -> 18, of which waited for: 15 -> 16; matrix products, arithmetic and copies ran while one was open for 14% -> 14% of each run, Pallas kernels for 0% -> 0%
where the time goes in v7:
time: 204 us; the launch traced here: 203 us
  waiting for transfers between devices  75.6 us (37%)
  starting transfers between devices  62.2 us (30%)
  local copies, waits for them, and re-layouts  16.9 us (8%)
  matrix products  16.3 us (8%)
  between operations  14.8 us (7%)
  Pallas kernels  10.2 us (5%)
  other arithmetic  6.5 us (3%)
    ppermute x6, starting transfers between devices, on_device(): other = lax.ppermute(first_piece, axis, swapped)  20.5 us
    all_to_all x1, waiting for transfers between devices, summed_on_arrival(): lax.all_to_all(pieces, axis, split_axis=0, concat_axis=0, tiled=True)  12.6 us
    all_to_all x1, waiting for transfers between devices, on_device(): features = lax.all_to_all(send, DP, split_axis=0, concat_axis=0, tiled=True)  11.3 us
    ppermute x6, waiting for transfers between devices, on_device(): other = lax.ppermute(first_piece, axis, swapped)  10.8 us
    all_to_all x1, waiting for transfers between devices, on_device(): got = lax.all_to_all(sent, DP, split_axis=0, concat_axis=0, tiled=True)  9.2 us
    all_to_all x1, waiting for transfers between devices, sent_to_all(): return lax.all_to_all(copies, axis, split_axis=0, concat_axis=0, tiled=True)  8.68 us
    pallas_call x1, Pallas kernels, trunk_rows(): pl.pallas_call(trunk_rows_kernel, out_shape=jax.ShapeDtypeStruct((4, 8, D...  8.66 us
    all_to_all x1, starting transfers between devices, on_device(): features = lax.all_to_all(send, DP, split_axis=0, concat_axis=0, tiled=True)  8.59 us
  transfers between devices with their start and end apart: 18, of which 16 were waited for; matrix products, arithmetic and copies ran while one was open for 14% of the time, Pallas kernels for 0%

profile of v7, /device:TPU:1, one launch (start us, length us, event | category | flops | bytes accessed | tf_op | source)
XLA Modules:
  0.0 202.5 jit_solution(14248299035063105822)
XLA Ops:
  7.2 0.8 fusion.115
  8.1 0.9 fusion.114
  9.1 1.0 slice_reduce_fusion
  10.1 0.9 fusion.113
  11.1 3.6 %collective-permute-start.4 = (bf16[12,2304]{1,0:T(8,128)(2,1)S(1)}, bf16[12,2304]{1,0:T(8,128)(2,1)S(1)}, u32[]{:S(2)}, u32[]{:S(2)}) collective-permute-start(bf16[12,2304]{1,0:T(8,128)(2,1)S(1)} %concatenate.42), channel_id=1, source_target_pairs={{0,2},{1,3},{2,0},{3,1},{4,6},{5,7},{6,4},{7,5},{8,10},{9,11},{10,... | collective-permute-start | bytes 165896 | tf_op jit(solution)/shard_map/ppermute | solution.py:243
  15.6 0.8 slice_reduce_fusion.1
  17.0 2.0 collective-permute-done.5
  19.0 1.2 collective-permute-done.6
  21.5 1.7 collective-permute-start.7
  25.2 1.7 collective-permute-start
  28.2 3.1 %collective-permute-start.1 = (bf16[24,768]{1,0:T(8,128)(2,1)S(1)}, bf16[24,768]{1,0:T(8,128)(2,1)S(1)}, u32[]{:S(2)}, u32[]{:S(2)}) collective-permute-start(bf16[24,768]{1,0:T(8,128)(2,1)S(1)} %pad_maximum_fusion.6), channel_id=1, source_target_pairs={{0,64},{32,96},{64,0},{96,32},{128,192},{160,224},{192,128},{224,1... | collective-permute-start | bytes 110600 | tf_op jit(solution)/shard_map/ppermute | solution.py:292
  31.3 1.3 collective-permute-done.1
  32.7 6.2 %collective-permute-start.2 = (bf16[48,768]{1,0:T(8,128)(2,1)S(1)}, bf16[48,768]{1,0:T(8,128)(2,1)S(1)}, u32[]{:S(2)}, u32[]{:S(2)}) collective-permute-start(bf16[48,768]{1,0:T(8,128)(2,1)S(1)} %pad_maximum_fusion.5), channel_id=1, source_target_pairs={{0,128},{32,160},{64,192},{96,224},{128,0},{160,32},{192,64},{224,... | collective-permute-start | bytes 221192 | tf_op jit(solution)/shard_map/ppermute | solution.py:292
  39.0 1.1 broadcast_in_dim.40
  40.1 3.5 %all-to-all-start = ((bf16[4,208,768]{2,1,0:T(8,128)(2,1)}), bf16[4,208,768]{2,1,0:T(8,128)(2,1)S(1)}, u32[]{:S(2)}, u32[]{:S(2)}) async-start(bf16[4,208,768]{2,1,0:T(8,128)(2,1)} %broadcast_in_dim.40), calls=%async_computation | async-start | bytes 2555904 | tf_op jit(solution)/shard_map/all_to_all | solution.py:28
  43.7 1.4 collective-permute-start.3
  45.3 3.9 %collective-permute-done.3 = bf16[96,768]{1,0:T(8,128)(2,1)S(1)} collective-permute-done((bf16[96,768]{1,0:T(8,128)(2,1)S(1)}, bf16[96,768]{1,0:T(8,128)(2,1)S(1)}, u32[]{:S(2)}, u32[]{:S(2)}) %collective-permute-start.3) | collective-permute-done | bytes 147488 | tf_op jit(solution)/shard_map/ppermute | solution.py:292
  49.3 8.7 %all-to-all-done = bf16[4,208,768]{2,1,0:T(8,128)(2,1)S(1)} async-done(((bf16[4,208,768]{2,1,0:T(8,128)(2,1)}), bf16[4,208,768]{2,1,0:T(8,128)(2,1)S(1)}, u32[]{:S(2)}, u32[]{:S(2)}) %all-to-all-start) | async-done | bytes 1277984 | tf_op jit(solution)/shard_map/all_to_all | solution.py:28
  58.0 2.9 %collective-permute-start.8 = (bf16[192,768]{1,0:T(8,128)(2,1)S(1)}, bf16[192,768]{1,0:T(8,128)(2,1)S(1)}, u32[]{:S(2)}, u32[]{:S(2)}) collective-permute-start(bf16[192,768]{1,0:T(8,128)(2,1)S(1)} %pad_maximum_fusion.1), channel_id=1, source_target_pairs={{0,16},{8,24},{16,0},{24,8},{1,17},{9,25},{17,1},{25,9},{2,18},{10... | collective-permute-start | bytes 884744 | tf_op jit(solution)/shard_map/ppermute | solution.py:292
  61.0 0.9 convolution_convert_fusion.8
  61.8 3.2 %collective-permute-done.8 = bf16[192,768]{1,0:T(8,128)(2,1)S(1)} collective-permute-done((bf16[192,768]{1,0:T(8,128)(2,1)S(1)}, bf16[192,768]{1,0:T(8,128)(2,1)S(1)}, u32[]{:S(2)}, u32[]{:S(2)}) %collective-permute-start.8) | collective-permute-done | bytes 294944 | tf_op jit(solution)/shard_map/ppermute | solution.py:292
  65.1 0.9 pad_maximum_fusion
  66.0 5.3 %collective-permute-start.9 = (bf16[384,768]{1,0:T(8,128)(2,1)}, bf16[384,768]{1,0:T(8,128)(2,1)S(1)}, u32[]{:S(2)}, u32[]{:S(2)}) collective-permute-start(bf16[384,768]{1,0:T(8,128)(2,1)} %pad_maximum_fusion), channel_id=1, source_target_pairs={{0,4},{4,0},{1,5},{5,1},{2,6},{6,2},{3,7},{7,3},{8,12},{12,8},{9,1... | collective-permute-start | bytes 1769480 | tf_op jit(solution)/shard_map/ppermute | solution.py:292
  71.6 1.5 collective-permute-done.9
  73.4 1.3 fusion.1
  74.7 0.9 convolution_convert_fusion.1
  77.2 1.5 fusion.3
  78.7 2.1 %fusion.4 = bf16[12,64,3,64]{1,3,2,0:T(8,128)(2,1)S(1)} fusion(f32[12,3,64,64]{2,3,1,0:T(8,128)} %fusion.3, bf16[12,64,3,64]{1,0,3,2:T(8,128)(2,1)S(1)} %squeeze.62), kind=kOutput, calls=%fused_computation.10 | convolution fusion | flops 19319104 | bytes 1179648 | tf_op jit(solution)/shard_map/shqk,skhd->sqhd/dot_general | solution.py:65
  81.7 2.5 %convolution_convert_fusion = bf16[768,768]{1,0:T(8,128)(2,1)} fusion(bf16[768,192]{0,1:T(8,128)(2,1)S(1)} %reshape.357, bf16[768,768]{0,1:T(8,128)(2,1)} %copy-done.4), kind=kOutput, calls=%fused_computation.4 | convolution fusion | flops 227082240 | bytes 1769472 | tf_op jit(solution)/shard_map/tk,dk->td/dot_general | solution.py:48
  84.2 3.7 %all-to-all-start.1 = ((bf16[4,192,768]{2,1,0:T(8,128)(2,1)}), bf16[4,192,768]{2,1,0:T(8,128)(2,1)S(1)}, u32[]{:S(2)}, u32[]{:S(2)}) async-start(bf16[4,192,768]{2,1,0:T(8,128)(2,1)} %bitcast.30), calls=%async_computation.1 | async-start | bytes 2359296 | tf_op jit(solution)/shard_map/all_to_all | solution.py:33
  91.5 12.6 %all-to-all-done.1 = bf16[4,192,768]{2,1,0:T(8,128)(2,1)S(1)} async-done(((bf16[4,192,768]{2,1,0:T(8,128)(2,1)}), bf16[4,192,768]{2,1,0:T(8,128)(2,1)S(1)}, u32[]{:S(2)}, u32[]{:S(2)}) %all-to-all-start.1) | async-done | bytes 1179680 | tf_op jit(solution)/shard_map/all_to_all | solution.py:33
  104.0 7.8 %all-to-all-start.2 = ((bf16[64,2,128]{2,1,0:T(2,128)(2,1)}), bf16[64,2,128]{2,1,0:T(2,128)(2,1)S(1)}, u32[]{:S(2)}, u32[]{:S(2)}) async-start(bf16[64,2,128]{2,1,0:T(2,128)(2,1)} %copy.183), calls=%async_computation.2 | async-start | bytes 65536 | tf_op jit(solution)/shard_map/all_to_all | solution.py:313
  112.1 9.2 %all-to-all-done.2 = bf16[64,2,128]{2,1,0:T(2,128)(2,1)S(1)} async-done(((bf16[64,2,128]{2,1,0:T(2,128)(2,1)}), bf16[64,2,128]{2,1,0:T(2,128)(2,1)S(1)}, u32[]{:S(2)}, u32[]{:S(2)}) %all-to-all-start.2) | async-done | bytes 32800 | tf_op jit(solution)/shard_map/all_to_all | solution.py:313
  121.3 4.4 %all-gather.2.cloned.1.call-done.all_ref = bf16[1536,5376]{1,0:T(8,128)(2,1)} async-done(((bf16[24,5376]{1,0:T(8,128)(2,1)}), bf16[1536,5376]{1,0:T(8,128)(2,1)}) %all-gather.2.cloned.1.call-update) | async-done | bytes 16515088 | tf_op jit(solution)/shard_map/all_gather | solution.py:285
  125.7 8.7 %trunk_rows.1 = bf16[4,8,768]{2,1,0:T(8,128)(2,1)} custom-call(f32[192,768]{1,0:T(8,128)S(1)} %convert_add_fusion.res_ref, s32[1,192]{1,0:T(1,128)S(1)} %reshape.354.mask_ref, f32[5,768]{1,0:T(8,128)S(1)} %copy-done.1, bf16[1536,5376]{1,0:T(8,128)(2,1)} %all-gather.2.cloned.1.call-done.all_ref), custom_call_target="tpu_custom_call" | custom-call | tf_op jit(solution)/shard_map/trunk_rows/pallas_call | solution.py:135
  134.4 4.0 %all-to-all-start.3 = ((bf16[4,8,768]{2,1,0:T(8,128)(2,1)}), bf16[4,8,768]{2,1,0:T(8,128)(2,1)S(1)}, u32[]{:S(2)}, u32[]{:S(2)}) async-start(bf16[4,8,768]{2,1,0:T(8,128)(2,1)} %trunk_rows.1), calls=%async_computation.3 | async-start | bytes 98304 | tf_op jit(solution)/shard_map/all_to_all | solution.py:319
  138.3 1.8 fusion.111
  140.1 2.6 %all-to-all-done.3 = bf16[4,8,768]{2,1,0:T(8,128)(2,1)S(1)} async-done(((bf16[4,8,768]{2,1,0:T(8,128)(2,1)}), bf16[4,8,768]{2,1,0:T(8,128)(2,1)S(1)}, u32[]{:S(2)}, u32[]{:S(2)}) %all-to-all-start.3) | async-done | bytes 49184 | tf_op jit(solution)/shard_map/all_to_all | solution.py:319
  142.7 1.5 readout_mlp.1
  144.2 3.5 %all-to-all-start.4 = ((bf16[4,32,768]{2,1,0:T(8,128)(2,1)}), bf16[4,32,768]{2,1,0:T(8,128)(2,1)S(1)}, u32[]{:S(2)}, u32[]{:S(2)}) async-start(bf16[4,32,768]{2,1,0:T(8,128)(2,1)} %readout_mlp.1), calls=%async_computation.4 | async-start | bytes 393216 | tf_op jit(solution)/shard_map/all_to_all | solution.py:322
  147.9 5.0 %all-to-all-done.4 = bf16[4,32,768]{2,1,0:T(8,128)(2,1)S(1)} async-done(((bf16[4,32,768]{2,1,0:T(8,128)(2,1)}), bf16[4,32,768]{2,1,0:T(8,128)(2,1)S(1)}, u32[]{:S(2)}, u32[]{:S(2)}) %all-to-all-start.4) | async-done | bytes 196640 | tf_op jit(solution)/shard_map/all_to_all | solution.py:322
  154.4 8.6 %all-to-all-start.5 = ((bf16[64,2,768]{2,1,0:T(2,128)(2,1)}), bf16[64,2,768]{2,1,0:T(2,128)(2,1)S(1)}, u32[]{:S(2)}, u32[]{:S(2)}) async-start(bf16[64,2,768]{2,1,0:T(2,128)(2,1)} %reshape.362), calls=%async_computation.5 | async-start | bytes 393216 | tf_op jit(solution)/shard_map/all_to_all | solution.py:327
  163.7 11.3 %all-to-all-done.5 = bf16[64,2,768]{2,1,0:T(2,128)(2,1)S(1)} async-done(((bf16[64,2,768]{2,1,0:T(2,128)(2,1)}), bf16[64,2,768]{2,1,0:T(2,128)(2,1)S(1)}, u32[]{:S(2)}, u32[]{:S(2)}) %all-to-all-start.5) | async-done | bytes 196640 | tf_op jit(solution)/shard_map/all_to_all | solution.py:327
  178.2 4.5 %all-to-all-start.6 = ((bf16[64,2,768]{2,1,0:T(2,128)(2,1)}), bf16[64,2,768]{2,1,0:T(2,128)(2,1)S(1)}, u32[]{:S(2)}, u32[]{:S(2)}) async-start(bf16[64,2,768]{2,1,0:T(2,128)(2,1)} %reshape.364), calls=%async_computation.6 | async-start | bytes 393216 | tf_op jit(solution)/shard_map/all_to_all | solution.py:350
  182.7 1.0 convolution_bitcast_fusion.2
  185.8 0.9 convolution_bitcast_fusion.1
  186.8 0.9 convolution_bitcast_fusion
  187.7 7.2 %all-to-all-done.6 = bf16[64,2,768]{2,1,0:T(2,128)(2,1)S(1)} async-done(((bf16[64,2,768]{2,1,0:T(2,128)(2,1)}), bf16[64,2,768]{2,1,0:T(2,128)(2,1)S(1)}, u32[]{:S(2)}, u32[]{:S(2)}) %all-to-all-start.6) | async-done | bytes 196640 | tf_op jit(solution)/shard_map/all_to_all | solution.py:350
  (159 shorter events, 21.8 us)
Async XLA Ops:
  7.2 167.9 %copy-start = (bf16[1,768,256]{2,1,0:T(8,128)(2,1)S(1)}, bf16[1,768,256]{2,1,0:T(8,128)(2,1)}, u32[]{:S(2)}) copy-start(bf16[1,768,256]{2,1,0:T(8,128)(2,1)} %param.30) | copy-start | bytes 1179652
  7.2 9.3 %copy-start.3 = (bf16[192,768]{1,0:T(8,128)(2,1)S(1)}, bf16[192,768]{1,0:T(8,128)(2,1)}, u32[]{:S(2)}) copy-start(bf16[192,768]{1,0:T(8,128)(2,1)} %param.18) | copy-start | bytes 884740
  7.2 118.5 %all-gather.2.cloned.1.call-start = ((), (), s32[]{:S(2)}) async-start(), calls=%async_computation.7 | async-start | bytes 16773120 | tf_op jit(solution)/shard_map/all_gather | solution.py:285
  11.1 5.9 %collective-permute-start.4 = (bf16[12,2304]{1,0:T(8,128)(2,1)S(1)}, bf16[12,2304]{1,0:T(8,128)(2,1)S(1)}, u32[]{:S(2)}, u32[]{:S(2)}) collective-permute-start(bf16[12,2304]{1,0:T(8,128)(2,1)S(1)} %concatenate.42), channel_id=1, source_target_pairs={{0,2},{1,3},{2,0},{3,1},{4,6},{5,7},{6,4},{7,5},{8,10},{9,11},{10,... | collective-permute-start | bytes 165896 | tf_op jit(solution)/shard_map/ppermute | solution.py:243
  14.7 4.3 %collective-permute-start.5 = (bf16[12,2304]{1,0:T(8,128)(2,1)S(1)}, bf16[12,2304]{1,0:T(8,128)(2,1)S(1)}, u32[]{:S(2)}, u32[]{:S(2)}) collective-permute-start(bf16[12,2304]{1,0:T(8,128)(2,1)S(1)} %concatenate.42), channel_id=1, source_target_pairs={{0,1},{1,0},{2,3},{3,2},{4,5},{5,4},{6,7},{7,6},{8,9},{9,8},{10,11... | collective-permute-start | bytes 165896 | tf_op jit(solution)/shard_map/ppermute | solution.py:243
  15.0 5.2 %collective-permute-start.6 = (bf16[12,2304]{1,0:T(8,128)(2,1)S(1)}, bf16[12,2304]{1,0:T(8,128)(2,1)S(1)}, u32[]{:S(2)}, u32[]{:S(2)}) collective-permute-start(bf16[12,2304]{1,0:T(8,128)(2,1)S(1)} %concatenate.42), channel_id=1, source_target_pairs={{0,3},{1,2},{2,1},{3,0},{4,7},{5,6},{6,5},{7,4},{8,11},{9,10},{10,... | collective-permute-start | bytes 165896 | tf_op jit(solution)/shard_map/ppermute | solution.py:243
  21.1 2.3 %copy-start.10 = (s32[3,64]{1,0:T(4,128)S(1)}, s32[3,64]{1,0:T(4,128)}, u32[]{:S(2)}) copy-start(s32[3,64]{1,0:T(4,128)} %param.19) | copy-start | bytes 2308
  21.5 2.7 %collective-permute-start.7 = (bf16[12,5376]{1,0:T(8,128)(2,1)S(1)}, bf16[12,5376]{1,0:T(8,128)(2,1)S(1)}, u32[]{:S(2)}, u32[]{:S(2)}) collective-permute-start(bf16[12,5376]{1,0:T(8,128)(2,1)S(1)} %select_bitcast_fusion), channel_id=1, source_target_pairs={{0,4},{4,0},{1,5},{5,1},{2,6},{6,2},{3,7},{7,3},{8,12},{12,8},{9,1... | collective-permute-start | bytes 387080 | tf_op jit(solution)/shard_map/ppermute | solution.py:259
  23.5 3.4 %copy-start.11 = (s32[12,2]{0,1:T(2,128)S(1)}, s32[12,2]{0,1:T(2,128)}, u32[]{:S(2)}) copy-start(s32[12,2]{0,1:T(2,128)} %param.26) | copy-start | bytes 292
  23.5 15.4 %copy-start.7 = (bf16[12,2,56]{2,1,0:T(2,128)(2,1)S(1)}, bf16[12,2,56]{2,1,0:T(2,128)(2,1)}, u32[]{:S(2)}) copy-start(bf16[12,2,56]{2,1,0:T(2,128)(2,1)} %param.28) | copy-start | bytes 8068
  23.5 15.4 %copy-start.9 = (bf16[12,2,56]{2,1,0:T(2,128)(2,1)S(1)}, bf16[12,2,56]{2,1,0:T(2,128)(2,1)}, u32[]{:S(2)}) copy-start(bf16[12,2,56]{2,1,0:T(2,128)(2,1)} %param.27) | copy-start | bytes 8068
  25.2 2.9 %collective-permute-start = (bf16[12,768]{1,0:T(8,128)(2,1)S(1)}, bf16[12,768]{1,0:T(8,128)(2,1)S(1)}, u32[]{:S(2)}, u32[]{:S(2)}) collective-permute-start(bf16[12,768]{1,0:T(8,128)(2,1)S(1)} %pad_maximum_fusion.7), channel_id=1, source_target_pairs={{0,32},{32,0},{64,96},{96,64},{128,160},{160,128},{192,224},{224,1... | collective-permute-start | bytes 55304 | tf_op jit(solution)/shard_map/ppermute | solution.py:292
  28.2 4.4 %collective-permute-start.1 = (bf16[24,768]{1,0:T(8,128)(2,1)S(1)}, bf16[24,768]{1,0:T(8,128)(2,1)S(1)}, u32[]{:S(2)}, u32[]{:S(2)}) collective-permute-start(bf16[24,768]{1,0:T(8,128)(2,1)S(1)} %pad_maximum_fusion.6), channel_id=1, source_target_pairs={{0,64},{32,96},{64,0},{96,32},{128,192},{160,224},{192,128},{224,1... | collective-permute-start | bytes 110600 | tf_op jit(solution)/shard_map/ppermute | solution.py:292
  32.7 11.0 %collective-permute-start.2 = (bf16[48,768]{1,0:T(8,128)(2,1)S(1)}, bf16[48,768]{1,0:T(8,128)(2,1)S(1)}, u32[]{:S(2)}, u32[]{:S(2)}) collective-permute-start(bf16[48,768]{1,0:T(8,128)(2,1)S(1)} %pad_maximum_fusion.5), channel_id=1, source_target_pairs={{0,128},{32,160},{64,192},{96,224},{128,0},{160,32},{192,64},{224,... | collective-permute-start | bytes 221192 | tf_op jit(solution)/shard_map/ppermute | solution.py:292
  40.1 17.9 %all-to-all-start = ((bf16[4,208,768]{2,1,0:T(8,128)(2,1)}), bf16[4,208,768]{2,1,0:T(8,128)(2,1)S(1)}, u32[]{:S(2)}, u32[]{:S(2)}) async-start(bf16[4,208,768]{2,1,0:T(8,128)(2,1)} %broadcast_in_dim.40), calls=%async_computation | async-start | bytes 2555904 | tf_op jit(solution)/shard_map/all_to_all | solution.py:28
  43.6 17.3 %copy-start.12 = (s32[12,1]{0,1:T(1,128)S(1)}, s32[12,1]{0,1:T(1,128)}, u32[]{:S(2)}) copy-start(s32[12,1]{0,1:T(1,128)} %param.25) | copy-start | bytes 148
  43.7 5.5 %collective-permute-start.3 = (bf16[96,768]{1,0:T(8,128)(2,1)S(1)}, bf16[96,768]{1,0:T(8,128)(2,1)S(1)}, u32[]{:S(2)}, u32[]{:S(2)}) collective-permute-start(bf16[96,768]{1,0:T(8,128)(2,1)S(1)} %pad_maximum_fusion.4), channel_id=1, source_target_pairs={{0,8},{8,0},{16,24},{24,16},{1,9},{9,1},{17,25},{25,17},{2,10},{10... | collective-permute-start | bytes 442376 | tf_op jit(solution)/shard_map/ppermute | solution.py:292
  58.0 13.3 %copy-start.2 = (bf16[4,208,768]{2,1,0:T(8,128)(2,1)}, bf16[4,208,768]{2,1,0:T(8,128)(2,1)S(1)}, u32[]{:S(2)}) copy-start(bf16[4,208,768]{2,1,0:T(8,128)(2,1)S(1)} %all-to-all-done) | copy-start | bytes 3833860
  58.0 7.1 %collective-permute-start.8 = (bf16[192,768]{1,0:T(8,128)(2,1)S(1)}, bf16[192,768]{1,0:T(8,128)(2,1)S(1)}, u32[]{:S(2)}, u32[]{:S(2)}) collective-permute-start(bf16[192,768]{1,0:T(8,128)(2,1)S(1)} %pad_maximum_fusion.1), channel_id=1, source_target_pairs={{0,16},{8,24},{16,0},{24,8},{1,17},{9,25},{17,1},{25,9},{2,18},{10... | collective-permute-start | bytes 884744 | tf_op jit(solution)/shard_map/ppermute | solution.py:292
  66.0 7.1 %collective-permute-start.9 = (bf16[384,768]{1,0:T(8,128)(2,1)}, bf16[384,768]{1,0:T(8,128)(2,1)S(1)}, u32[]{:S(2)}, u32[]{:S(2)}) collective-permute-start(bf16[384,768]{1,0:T(8,128)(2,1)} %pad_maximum_fusion), channel_id=1, source_target_pairs={{0,4},{4,0},{1,5},{5,1},{2,6},{6,2},{3,7},{7,3},{8,12},{12,8},{9,1... | collective-permute-start | bytes 1769480 | tf_op jit(solution)/shard_map/ppermute | solution.py:292
  73.3 1.3 slice-start
  74.7 1.0 copy-start.4
  84.2 5.2 %copy-start.16 = (s32[25]{0:T(128)S(1)}, s32[25]{0:T(128)}, u32[]{:S(2)}) copy-start(s32[25]{0:T(128)} %param.29) | copy-start | bytes 304
  84.2 6.6 %copy-start.5 = (bf16[64,2,128]{2,0,1:T(8,128)(2,1)S(1)}, bf16[64,2,128]{2,0,1:T(8,128)(2,1)}, u32[]{:S(2)}) copy-start(bf16[64,2,128]{2,0,1:T(8,128)(2,1)} %convolution_convert_fusion.8) | copy-start | bytes 98308
  84.2 19.8 %all-to-all-start.1 = ((bf16[4,192,768]{2,1,0:T(8,128)(2,1)}), bf16[4,192,768]{2,1,0:T(8,128)(2,1)S(1)}, u32[]{:S(2)}, u32[]{:S(2)}) async-start(bf16[4,192,768]{2,1,0:T(8,128)(2,1)} %bitcast.30), calls=%async_computation.1 | async-start | bytes 2359296 | tf_op jit(solution)/shard_map/all_to_all | solution.py:33
  104.0 17.2 %all-to-all-start.2 = ((bf16[64,2,128]{2,1,0:T(2,128)(2,1)}), bf16[64,2,128]{2,1,0:T(2,128)(2,1)S(1)}, u32[]{:S(2)}, u32[]{:S(2)}) async-start(bf16[64,2,128]{2,1,0:T(2,128)(2,1)} %copy.183), calls=%async_computation.2 | async-start | bytes 65536 | tf_op jit(solution)/shard_map/all_to_all | solution.py:313
  112.0 13.7 %copy-start.1 = (f32[5,768]{1,0:T(8,128)S(1)}, f32[5,768]{1,0:T(8,128)}, u32[]{:S(2)}) copy-start(f32[5,768]{1,0:T(8,128)} %gain_ref.3) | copy-start | bytes 46084
  134.4 8.3 %all-to-all-start.3 = ((bf16[4,8,768]{2,1,0:T(8,128)(2,1)}), bf16[4,8,768]{2,1,0:T(8,128)(2,1)S(1)}, u32[]{:S(2)}, u32[]{:S(2)}) async-start(bf16[4,8,768]{2,1,0:T(8,128)(2,1)} %trunk_rows.1), calls=%async_computation.3 | async-start | bytes 98304 | tf_op jit(solution)/shard_map/all_to_all | solution.py:319
  142.7 5.0 %copy-start.6 = (bf16[1,56,256]{2,1,0:T(8,128)(2,1)S(1)}, bf16[1,56,256]{2,1,0:T(8,128)(2,1)}, u32[]{:S(2)}) copy-start(bf16[1,56,256]{2,1,0:T(8,128)(2,1)} %param.31) | copy-start | bytes 86020
  144.2 19.3 %copy-start.8 = (bf16[1,20,256]{2,1,0:T(8,128)(2,1)S(1)}, bf16[1,20,256]{2,1,0:T(8,128)(2,1)}, u32[]{:S(2)}) copy-start(bf16[1,20,256]{2,1,0:T(8,128)(2,1)} %param.32) | copy-start | bytes 30724
  144.2 8.6 %all-to-all-start.4 = ((bf16[4,32,768]{2,1,0:T(8,128)(2,1)}), bf16[4,32,768]{2,1,0:T(8,128)(2,1)S(1)}, u32[]{:S(2)}, u32[]{:S(2)}) async-start(bf16[4,32,768]{2,1,0:T(8,128)(2,1)} %readout_mlp.1), calls=%async_computation.4 | async-start | bytes 393216 | tf_op jit(solution)/shard_map/all_to_all | solution.py:322
  153.7 21.7 %copy-start.14 = (bf16[1,256,256]{2,1,0:T(8,128)(2,1)S(1)}, bf16[1,256,256]{2,1,0:T(8,128)(2,1)}, u32[]{:S(2)}) copy-start(bf16[1,256,256]{2,1,0:T(8,128)(2,1)} %param.33) | copy-start | bytes 393220
  154.4 20.6 %all-to-all-start.5 = ((bf16[64,2,768]{2,1,0:T(2,128)(2,1)}), bf16[64,2,768]{2,1,0:T(2,128)(2,1)S(1)}, u32[]{:S(2)}, u32[]{:S(2)}) async-start(bf16[64,2,768]{2,1,0:T(2,128)(2,1)} %reshape.362), calls=%async_computation.5 | async-start | bytes 393216 | tf_op jit(solution)/shard_map/all_to_all | solution.py:327
  163.0 12.5 %copy-start.13 = (bf16[1,256,256]{2,1,0:T(8,128)(2,1)S(1)}, bf16[1,256,256]{2,1,0:T(8,128)(2,1)}, u32[]{:S(2)}) copy-start(bf16[1,256,256]{2,1,0:T(8,128)(2,1)} %param.34) | copy-start | bytes 393220
  175.3 0.8 copy-start.15
  178.2 16.7 %all-to-all-start.6 = ((bf16[64,2,768]{2,1,0:T(2,128)(2,1)}), bf16[64,2,768]{2,1,0:T(2,128)(2,1)S(1)}, u32[]{:S(2)}, u32[]{:S(2)}) async-start(bf16[64,2,768]{2,1,0:T(2,128)(2,1)} %reshape.364), calls=%async_computation.6 | async-start | bytes 393216 | tf_op jit(solution)/shard_map/all_to_all | solution.py:350
Sparse Core Ops, SparseCore 0:
  25.2 100.4 all-gather.1

commit v8 on v6

--- a/solution.py
+++ b/solution.py
@@ -26,6 +26,18 @@
 def sent_to_all(x, axis):
     copies = jnp.broadcast_to(x, (lax.axis_size(axis), *x.shape))
     return lax.all_to_all(copies, axis, split_axis=0, concat_axis=0, tiled=True)
+
+
+def members_in_order(x):
+    pieces = [x] + [lax.ppermute(x, "mp", [(k, k ^ step) for k in range(4)]) for step in (1, 2, 3)]
+    ordered = []
+    for member in range(4):
+        apart = lax.axis_index("mp") ^ member
+        piece = pieces[3]
+        for step in range(3):
+            piece = jnp.where(apart == step, pieces[step], piece)
+        ordered.append(piece)
+    return jnp.stack(ordered)
 
 
 def summed_on_arrival(x, axis):
@@ -125,8 +137,7 @@
         context = jnp.where(own_head, mm(shares, value_rows), 0.0)
         context = sum(context[8 * k : 8 * k + 8] for k in range(6)).astype(BF16)
         ending = ending + nt(context, att[side, :, 1152:1536])
-    for member in range(4):
-        out_ref[member] = ending.astype(BF16)
+    out_ref[...] = ending.astype(BF16)
 
 
 def trunk_rows(residual, mask_row, gains, weights):
@@ -134,7 +145,7 @@
     rows = (residual, mask_row, gains)
     return pl.pallas_call(
         trunk_rows_kernel,
-        out_shape=jax.ShapeDtypeStruct((4, 8, D), BF16),
+        out_shape=jax.ShapeDtypeStruct((8, D), BF16),
         in_specs=[vmem, vmem, vmem, pl.BlockSpec(memory_space=pl.ANY)],
         out_specs=vmem,
         scratch_shapes=[
@@ -154,8 +165,7 @@
     for side_ref in (first_ref, second_ref):
         hidden = jax.nn.gelu(mm(normed, side_ref[:, 0:384]), approximate=True).astype(BF16)
         total = total + nt(hidden, side_ref[:, 384:768])
-    for member in range(4):
-        out_ref[member] = total.astype(BF16)
+    out_ref[...] = total.astype(BF16)
 
 
 def readout_mlp(ending, gains, first_side, second_side):
@@ -163,7 +173,7 @@
     operands = (ending, gains, first_side, second_side)
     return pl.pallas_call(
         readout_mlp_kernel,
-        out_shape=jax.ShapeDtypeStruct((4, *ending.shape), BF16),
+        out_shape=jax.ShapeDtypeStruct(ending.shape, BF16),
         in_specs=[vmem] * 4,
         out_specs=vmem,
         name="readout_mlp",
@@ -239,7 +249,7 @@
         axis=1,
     )
     groups = full.shape[1] // width
-    full = sent_to_all(full, "mp").reshape(2, 2, 12, groups, width)
+    full = members_in_order(full).reshape(2, 2, 12, groups, width)
     full = full.transpose(0, 2, 3, 1, 4).reshape(2, 12, -1)
     share = jnp.stack([mlp_in[1], mlp_out[1].T], axis=1).reshape(12, 2, 2, -1)
     share = share.transpose(2, 0, 1, 3).reshape(2, 12, -1)
@@ -306,10 +316,9 @@
     residual, got, gathered_weights = lax.optimization_barrier((residual, got, gathered_weights))
     sides = [gathered_weights[D * k : D * (k + 1), 4608:5376] for k in range(2)]
     copies = trunk_rows(residual, obs_mask.reshape(1, -1), norm_gains, gathered_weights)
-    ending = lax.all_to_all(copies, "mp", split_axis=0, concat_axis=0, tiled=True)
-    ending = ending.reshape(-1, D)
+    ending = members_in_order(copies).reshape(-1, D)
     copies = readout_mlp(ending, norm_gains, *sides)
-    terms = lax.all_to_all(copies, "mp", split_axis=0, concat_axis=0, tiled=True)
+    terms = members_in_order(copies)
     ending = ending.astype(F32) + terms.astype(F32).sum(axis=0)
     readouts = normalize(ending, norm_gains[4]).astype(BF16)
 

time: 207 us -> 200 us (0.966)
  waiting for transfers between devices: 76.7 us -> 69.4 us
    ppermute x0 -> x9, starting transfers between devices: none -> 11.6 us  [members_in_order(): lax.ppermute(x, 'mp', [(k, k ^ step) for k in range(4)])]
    all_to_all x2 -> x0, waiting for transfers between devices: 7.6 us -> none  [on_device(): lax.all_to_all(copies, 'mp', split_axis=0, concat_axis=0, tiled=True)]
    all_to_all x2 -> x0, starting transfers between devices: 7.48 us -> none  [on_device(): lax.all_to_all(copies, 'mp', split_axis=0, concat_axis=0, tiled=True)]
    ppermute x0 -> x9, waiting for transfers between devices: none -> 6.85 us  [members_in_order(): lax.ppermute(x, 'mp', [(k, k ^ step) for k in range(4)])]
    all_to_all x2 -> x1, waiting for transfers between devices: 13.8 us -> 8.68 us  [sent_to_all(): return lax.all_to_all(copies, axis, split_axis=0, concat_axis=0, tiled=True)]
    all_to_all x2 -> x1, starting transfers between devices: 8.37 us -> 3.54 us  [sent_to_all(): return lax.all_to_all(copies, axis, split_axis=0, concat_axis=0, tiled=True)]
  transfers between devices with their start and end apart: 16 -> 22, of which waited for: 15 -> 17; matrix products, arithmetic and copies ran while one was open for 14% -> 16% of each run, Pallas kernels for 0% -> 0%
where the time goes in v8:
time: 200 us; the launch traced here: 199 us
  waiting for transfers between devices  69.4 us (35%)
  starting transfers between devices  61.8 us (31%)
  local copies, waits for them, and re-layouts  18.5 us (9%)
  matrix products  17.2 us (9%)
  between operations  14.8 us (7%)
  Pallas kernels  9.5 us (5%)
  other arithmetic  7.47 us (4%)
    ppermute x6, starting transfers between devices, on_device(): other = lax.ppermute(first_piece, axis, swapped)  20.5 us
    all_to_all x1, waiting for transfers between devices, summed_on_arrival(): lax.all_to_all(pieces, axis, split_axis=0, concat_axis=0, tiled=True)  12.7 us
    ppermute x9, starting transfers between devices, members_in_order(): lax.ppermute(x, 'mp', [(k, k ^ step) for k in range(4)])  11.6 us
    ppermute x6, waiting for transfers between devices, on_device(): other = lax.ppermute(first_piece, axis, swapped)  11.4 us
    all_to_all x1, waiting for transfers between devices, on_device(): features = lax.all_to_all(send, DP, split_axis=0, concat_axis=0, tiled=True)  11.3 us
    all_to_all x1, waiting for transfers between devices, on_device(): got = lax.all_to_all(sent, DP, split_axis=0, concat_axis=0, tiled=True)  9.48 us
    all_to_all x1, starting transfers between devices, on_device(): features = lax.all_to_all(send, DP, split_axis=0, concat_axis=0, tiled=True)  8.96 us
    all_to_all x1, waiting for transfers between devices, sent_to_all(): return lax.all_to_all(copies, axis, split_axis=0, concat_axis=0, tiled=True)  8.68 us
  transfers between devices with their start and end apart: 22, of which 17 were waited for; matrix products, arithmetic and copies ran while one was open for 16% of the time, Pallas kernels for 0%

profile of v8, /device:TPU:1, one launch (start us, length us, event | category | flops | bytes accessed | tf_op | source)
XLA Modules:
  0.0 198.7 jit_solution(2320040885280662398)
XLA Ops:
  8.1 0.9 fusion.113
  9.1 1.0 slice_reduce_fusion
  10.1 0.9 fusion.112
  11.1 3.6 %collective-permute-start.4 = (bf16[12,2304]{1,0:T(8,128)(2,1)S(1)}, bf16[12,2304]{1,0:T(8,128)(2,1)S(1)}, u32[]{:S(2)}, u32[]{:S(2)}) collective-permute-start(bf16[12,2304]{1,0:T(8,128)(2,1)S(1)} %concatenate.42), channel_id=1, source_target_pairs={{0,2},{1,3},{2,0},{3,1},{4,6},{5,7},{6,4},{7,5},{8,10},{9,11},{10,... | collective-permute-start | bytes 165896 | tf_op jit(solution)/shard_map/ppermute | solution.py:32
  17.0 2.0 collective-permute-done.5
  19.0 1.2 collective-permute-done.6
  21.5 1.7 collective-permute-start.7
  25.2 1.7 collective-permute-start
  28.2 3.1 %collective-permute-start.1 = (bf16[24,768]{1,0:T(8,128)(2,1)S(1)}, bf16[24,768]{1,0:T(8,128)(2,1)S(1)}, u32[]{:S(2)}, u32[]{:S(2)}) collective-permute-start(bf16[24,768]{1,0:T(8,128)(2,1)S(1)} %pad_maximum_fusion.6), channel_id=1, source_target_pairs={{0,64},{32,96},{64,0},{96,32},{128,192},{160,224},{192,128},{224,1... | collective-permute-start | bytes 110600 | tf_op jit(solution)/shard_map/ppermute | solution.py:292
  31.3 1.3 collective-permute-done.1
  32.7 6.2 %collective-permute-start.2 = (bf16[48,768]{1,0:T(8,128)(2,1)S(1)}, bf16[48,768]{1,0:T(8,128)(2,1)S(1)}, u32[]{:S(2)}, u32[]{:S(2)}) collective-permute-start(bf16[48,768]{1,0:T(8,128)(2,1)S(1)} %pad_maximum_fusion.5), channel_id=1, source_target_pairs={{0,128},{32,160},{64,192},{96,224},{128,0},{160,32},{192,64},{224,... | collective-permute-start | bytes 221192 | tf_op jit(solution)/shard_map/ppermute | solution.py:292
  39.0 1.1 broadcast_in_dim.40
  40.1 3.5 %all-to-all-start = ((bf16[4,208,768]{2,1,0:T(8,128)(2,1)}), bf16[4,208,768]{2,1,0:T(8,128)(2,1)S(1)}, u32[]{:S(2)}, u32[]{:S(2)}) async-start(bf16[4,208,768]{2,1,0:T(8,128)(2,1)} %broadcast_in_dim.40), calls=%async_computation | async-start | bytes 2555904 | tf_op jit(solution)/shard_map/all_to_all | solution.py:28
  43.7 1.4 collective-permute-start.3
  45.3 3.9 %collective-permute-done.3 = bf16[96,768]{1,0:T(8,128)(2,1)S(1)} collective-permute-done((bf16[96,768]{1,0:T(8,128)(2,1)S(1)}, bf16[96,768]{1,0:T(8,128)(2,1)S(1)}, u32[]{:S(2)}, u32[]{:S(2)}) %collective-permute-start.3) | collective-permute-done | bytes 147488 | tf_op jit(solution)/shard_map/ppermute | solution.py:292
  49.3 8.7 %all-to-all-done = bf16[4,208,768]{2,1,0:T(8,128)(2,1)S(1)} async-done(((bf16[4,208,768]{2,1,0:T(8,128)(2,1)}), bf16[4,208,768]{2,1,0:T(8,128)(2,1)S(1)}, u32[]{:S(2)}, u32[]{:S(2)}) %all-to-all-start) | async-done | bytes 1277984 | tf_op jit(solution)/shard_map/all_to_all | solution.py:28
  58.0 2.9 %collective-permute-start.8 = (bf16[192,768]{1,0:T(8,128)(2,1)S(1)}, bf16[192,768]{1,0:T(8,128)(2,1)S(1)}, u32[]{:S(2)}, u32[]{:S(2)}) collective-permute-start(bf16[192,768]{1,0:T(8,128)(2,1)S(1)} %pad_maximum_fusion.1), channel_id=1, source_target_pairs={{0,16},{8,24},{16,0},{24,8},{1,17},{9,25},{17,1},{25,9},{2,18},{10... | collective-permute-start | bytes 884744 | tf_op jit(solution)/shard_map/ppermute | solution.py:292
  61.2 3.8 %collective-permute-done.8 = bf16[192,768]{1,0:T(8,128)(2,1)S(1)} collective-permute-done((bf16[192,768]{1,0:T(8,128)(2,1)S(1)}, bf16[192,768]{1,0:T(8,128)(2,1)S(1)}, u32[]{:S(2)}, u32[]{:S(2)}) %collective-permute-start.8) | collective-permute-done | bytes 294944 | tf_op jit(solution)/shard_map/ppermute | solution.py:292
  66.0 5.3 %collective-permute-start.9 = (bf16[384,768]{1,0:T(8,128)(2,1)}, bf16[384,768]{1,0:T(8,128)(2,1)S(1)}, u32[]{:S(2)}, u32[]{:S(2)}) collective-permute-start(bf16[384,768]{1,0:T(8,128)(2,1)} %pad_maximum_fusion), channel_id=1, source_target_pairs={{0,4},{4,0},{1,5},{5,1},{2,6},{6,2},{3,7},{7,3},{8,12},{12,8},{9,1... | collective-permute-start | bytes 1769480 | tf_op jit(solution)/shard_map/ppermute | solution.py:292
  71.6 1.5 collective-permute-done.9
  73.4 1.3 fusion.1
  74.7 0.9 convolution_convert_fusion.1
  76.3 1.4 squeeze.63
  77.6 1.3 squeeze.62
  79.0 2.6 %fusion.3 = f32[12,3,64,64]{2,3,1,0:T(8,128)} fusion(bf16[12,64,3,64]{1,0,3,2:T(8,128)(2,1)S(1)} %squeeze.64, bf16[12,64,3,64]{1,0,3,2:T(8,128)(2,1)} %squeeze.63, pred[12,64,64]{1,2,0:T(8,128)(4,1)S(1)} %broadcast_or_fusion), kind=kOutput, calls=%fused_computation.8 | convolution fusion | flops 19169280 | bytes 1228800 | tf_op jit(solution)/shard_map/sqhd,skhd->shqk/dot_general | solution.py:72
  81.6 2.4 %fusion.4 = bf16[12,64,3,64]{1,3,2,0:T(8,128)(2,1)S(1)} fusion(f32[12,3,64,64]{2,3,1,0:T(8,128)} %fusion.3, bf16[12,64,3,64]{1,0,3,2:T(8,128)(2,1)} %squeeze.62), kind=kOutput, calls=%fused_computation.10 | convolution fusion | flops 19319104 | bytes 1179648 | tf_op jit(solution)/shard_map/shqk,skhd->sqhd/dot_general | solution.py:77
  84.9 2.5 %convolution_convert_fusion = bf16[768,768]{1,0:T(8,128)(2,1)} fusion(bf16[768,192]{0,1:T(8,128)(2,1)S(1)} %reshape.375, bf16[768,768]{0,1:T(8,128)(2,1)} %copy-done.4), kind=kOutput, calls=%fused_computation.4 | convolution fusion | flops 227082240 | bytes 1769472 | tf_op jit(solution)/shard_map/tk,dk->td/dot_general | solution.py:60
  87.4 3.7 %all-to-all-start.1 = ((bf16[4,192,768]{2,1,0:T(8,128)(2,1)}), bf16[4,192,768]{2,1,0:T(8,128)(2,1)S(1)}, u32[]{:S(2)}, u32[]{:S(2)}) async-start(bf16[4,192,768]{2,1,0:T(8,128)(2,1)} %bitcast.163), calls=%async_computation.1 | async-start | bytes 2359296 | tf_op jit(solution)/shard_map/all_to_all | solution.py:45
  94.7 12.7 %all-to-all-done.1 = bf16[4,192,768]{2,1,0:T(8,128)(2,1)S(1)} async-done(((bf16[4,192,768]{2,1,0:T(8,128)(2,1)}), bf16[4,192,768]{2,1,0:T(8,128)(2,1)S(1)}, u32[]{:S(2)}, u32[]{:S(2)}) %all-to-all-start.1) | async-done | bytes 1179680 | tf_op jit(solution)/shard_map/all_to_all | solution.py:45
  107.4 7.4 %all-to-all-start.2 = ((bf16[64,2,128]{2,1,0:T(2,128)(2,1)}), bf16[64,2,128]{2,1,0:T(2,128)(2,1)S(1)}, u32[]{:S(2)}, u32[]{:S(2)}) async-start(bf16[64,2,128]{2,1,0:T(2,128)(2,1)} %copy.183), calls=%async_computation.2 | async-start | bytes 65536 | tf_op jit(solution)/shard_map/all_to_all | solution.py:313
  115.0 9.5 %all-to-all-done.2 = bf16[64,2,128]{2,1,0:T(2,128)(2,1)S(1)} async-done(((bf16[64,2,128]{2,1,0:T(2,128)(2,1)}), bf16[64,2,128]{2,1,0:T(2,128)(2,1)S(1)}, u32[]{:S(2)}, u32[]{:S(2)}) %all-to-all-start.2) | async-done | bytes 32800 | tf_op jit(solution)/shard_map/all_to_all | solution.py:313
  124.5 1.2 all-gather.2.cloned.1.call-done.all_ref
  125.7 8.0 %trunk_rows.1 = bf16[8,768]{1,0:T(8,128)(2,1)S(1)} custom-call(f32[192,768]{1,0:T(8,128)S(1)} %convert_add_fusion.res_ref, s32[1,192]{1,0:T(1,128)S(1)} %reshape.372.mask_ref, f32[5,768]{1,0:T(8,128)S(1)} %copy-done.1, bf16[1536,5376]{1,0:T(8,128)(2,1)} %all-gather.2.cloned.1.call-done.all_ref), custom_call_target="tpu_custom_call" | custom-call | tf_op jit(solution)/shard_map/trunk_rows/pallas_call | solution.py:146
  133.7 3.0 %collective-permute-start.10 = (bf16[8,768]{1,0:T(8,128)(2,1)S(1)}, bf16[8,768]{1,0:T(8,128)(2,1)S(1)}, u32[]{:S(2)}, u32[]{:S(2)}) collective-permute-start(bf16[8,768]{1,0:T(8,128)(2,1)S(1)} %trunk_rows.1), channel_id=1, source_target_pairs={{0,2},{1,3},{2,0},{3,1},{4,6},{5,7},{6,4},{7,5},{8,10},{9,11},{10,... | collective-permute-start | bytes 36872 | tf_op jit(solution)/shard_map/ppermute | solution.py:32
  137.6 1.8 fusion.110
  139.4 1.4 collective-permute-done.12
  140.8 1.5 readout_mlp.1
  142.3 1.0 collective-permute-start.13
  143.7 1.9 collective-permute-start.15
  145.7 1.2 collective-permute-done.13
  147.0 1.0 collective-permute-done.15
  150.3 9.0 %all-to-all-start.3 = ((bf16[64,2,768]{2,1,0:T(2,128)(2,1)}), bf16[64,2,768]{2,1,0:T(2,128)(2,1)S(1)}, u32[]{:S(2)}, u32[]{:S(2)}) async-start(bf16[64,2,768]{2,1,0:T(2,128)(2,1)} %reshape.380), calls=%async_computation.3 | async-start | bytes 393216 | tf_op jit(solution)/shard_map/all_to_all | solution.py:326
  160.0 11.3 %all-to-all-done.3 = bf16[64,2,768]{2,1,0:T(2,128)(2,1)S(1)} async-done(((bf16[64,2,768]{2,1,0:T(2,128)(2,1)}), bf16[64,2,768]{2,1,0:T(2,128)(2,1)S(1)}, u32[]{:S(2)}, u32[]{:S(2)}) %all-to-all-start.3) | async-done | bytes 196640 | tf_op jit(solution)/shard_map/all_to_all | solution.py:326
  174.4 4.5 %all-to-all-start.4 = ((bf16[64,2,768]{2,1,0:T(2,128)(2,1)}), bf16[64,2,768]{2,1,0:T(2,128)(2,1)S(1)}, u32[]{:S(2)}, u32[]{:S(2)}) async-start(bf16[64,2,768]{2,1,0:T(2,128)(2,1)} %reshape.382), calls=%async_computation.4 | async-start | bytes 393216 | tf_op jit(solution)/shard_map/all_to_all | solution.py:349
  178.9 1.0 convolution_bitcast_fusion.2
  182.1 0.9 convolution_bitcast_fusion.1
  183.0 0.9 convolution_bitcast_fusion
  184.0 7.1 %all-to-all-done.4 = bf16[64,2,768]{2,1,0:T(2,128)(2,1)S(1)} async-done(((bf16[64,2,768]{2,1,0:T(2,128)(2,1)}), bf16[64,2,768]{2,1,0:T(2,128)(2,1)S(1)}, u32[]{:S(2)}, u32[]{:S(2)}) %all-to-all-start.4) | async-done | bytes 196640 | tf_op jit(solution)/shard_map/all_to_all | solution.py:349
  (166 shorter events, 25.7 us)
Async XLA Ops:
  7.2 164.2 %copy-start = (bf16[1,768,256]{2,1,0:T(8,128)(2,1)S(1)}, bf16[1,768,256]{2,1,0:T(8,128)(2,1)}, u32[]{:S(2)}) copy-start(bf16[1,768,256]{2,1,0:T(8,128)(2,1)} %param.30) | copy-start | bytes 1179652
  7.2 9.3 %copy-start.3 = (bf16[192,768]{1,0:T(8,128)(2,1)S(1)}, bf16[192,768]{1,0:T(8,128)(2,1)}, u32[]{:S(2)}) copy-start(bf16[192,768]{1,0:T(8,128)(2,1)} %param.18) | copy-start | bytes 884740
  7.2 118.5 %all-gather.2.cloned.1.call-start = ((), (), s32[]{:S(2)}) async-start(), calls=%async_computation.5 | async-start | bytes 16773120 | tf_op jit(solution)/shard_map/all_gather | solution.py:285
  11.1 5.9 %collective-permute-start.4 = (bf16[12,2304]{1,0:T(8,128)(2,1)S(1)}, bf16[12,2304]{1,0:T(8,128)(2,1)S(1)}, u32[]{:S(2)}, u32[]{:S(2)}) collective-permute-start(bf16[12,2304]{1,0:T(8,128)(2,1)S(1)} %concatenate.42), channel_id=1, source_target_pairs={{0,2},{1,3},{2,0},{3,1},{4,6},{5,7},{6,4},{7,5},{8,10},{9,11},{10,... | collective-permute-start | bytes 165896 | tf_op jit(solution)/shard_map/ppermute | solution.py:32
  14.7 4.3 %collective-permute-start.5 = (bf16[12,2304]{1,0:T(8,128)(2,1)S(1)}, bf16[12,2304]{1,0:T(8,128)(2,1)S(1)}, u32[]{:S(2)}, u32[]{:S(2)}) collective-permute-start(bf16[12,2304]{1,0:T(8,128)(2,1)S(1)} %concatenate.42), channel_id=1, source_target_pairs={{0,1},{1,0},{2,3},{3,2},{4,5},{5,4},{6,7},{7,6},{8,9},{9,8},{10,11... | collective-permute-start | bytes 165896 | tf_op jit(solution)/shard_map/ppermute | solution.py:32
  15.0 5.2 %collective-permute-start.6 = (bf16[12,2304]{1,0:T(8,128)(2,1)S(1)}, bf16[12,2304]{1,0:T(8,128)(2,1)S(1)}, u32[]{:S(2)}, u32[]{:S(2)}) collective-permute-start(bf16[12,2304]{1,0:T(8,128)(2,1)S(1)} %concatenate.42), channel_id=1, source_target_pairs={{0,3},{1,2},{2,1},{3,0},{4,7},{5,6},{6,5},{7,4},{8,11},{9,10},{10,... | collective-permute-start | bytes 165896 | tf_op jit(solution)/shard_map/ppermute | solution.py:32
  21.1 2.3 %copy-start.9 = (s32[3,64]{1,0:T(4,128)S(1)}, s32[3,64]{1,0:T(4,128)}, u32[]{:S(2)}) copy-start(s32[3,64]{1,0:T(4,128)} %param.19) | copy-start | bytes 2308
  21.5 2.7 %collective-permute-start.7 = (bf16[12,5376]{1,0:T(8,128)(2,1)S(1)}, bf16[12,5376]{1,0:T(8,128)(2,1)S(1)}, u32[]{:S(2)}, u32[]{:S(2)}) collective-permute-start(bf16[12,5376]{1,0:T(8,128)(2,1)S(1)} %select_bitcast_fusion), channel_id=1, source_target_pairs={{0,4},{4,0},{1,5},{5,1},{2,6},{6,2},{3,7},{7,3},{8,12},{12,8},{9,1... | collective-permute-start | bytes 387080 | tf_op jit(solution)/shard_map/ppermute | solution.py:259
  23.5 3.4 %copy-start.10 = (s32[12,2]{0,1:T(2,128)S(1)}, s32[12,2]{0,1:T(2,128)}, u32[]{:S(2)}) copy-start(s32[12,2]{0,1:T(2,128)} %param.26) | copy-start | bytes 292
  23.5 15.4 %copy-start.6 = (bf16[12,2,56]{2,1,0:T(2,128)(2,1)S(1)}, bf16[12,2,56]{2,1,0:T(2,128)(2,1)}, u32[]{:S(2)}) copy-start(bf16[12,2,56]{2,1,0:T(2,128)(2,1)} %param.28) | copy-start | bytes 8068
  23.5 15.4 %copy-start.8 = (bf16[12,2,56]{2,1,0:T(2,128)(2,1)S(1)}, bf16[12,2,56]{2,1,0:T(2,128)(2,1)}, u32[]{:S(2)}) copy-start(bf16[12,2,56]{2,1,0:T(2,128)(2,1)} %param.27) | copy-start | bytes 8068
  25.2 2.9 %collective-permute-start = (bf16[12,768]{1,0:T(8,128)(2,1)S(1)}, bf16[12,768]{1,0:T(8,128)(2,1)S(1)}, u32[]{:S(2)}, u32[]{:S(2)}) collective-permute-start(bf16[12,768]{1,0:T(8,128)(2,1)S(1)} %pad_maximum_fusion.7), channel_id=1, source_target_pairs={{0,32},{32,0},{64,96},{96,64},{128,160},{160,128},{192,224},{224,1... | collective-permute-start | bytes 55304 | tf_op jit(solution)/shard_map/ppermute | solution.py:292
  28.2 4.4 %collective-permute-start.1 = (bf16[24,768]{1,0:T(8,128)(2,1)S(1)}, bf16[24,768]{1,0:T(8,128)(2,1)S(1)}, u32[]{:S(2)}, u32[]{:S(2)}) collective-permute-start(bf16[24,768]{1,0:T(8,128)(2,1)S(1)} %pad_maximum_fusion.6), channel_id=1, source_target_pairs={{0,64},{32,96},{64,0},{96,32},{128,192},{160,224},{192,128},{224,1... | collective-permute-start | bytes 110600 | tf_op jit(solution)/shard_map/ppermute | solution.py:292
  32.7 11.0 %collective-permute-start.2 = (bf16[48,768]{1,0:T(8,128)(2,1)S(1)}, bf16[48,768]{1,0:T(8,128)(2,1)S(1)}, u32[]{:S(2)}, u32[]{:S(2)}) collective-permute-start(bf16[48,768]{1,0:T(8,128)(2,1)S(1)} %pad_maximum_fusion.5), channel_id=1, source_target_pairs={{0,128},{32,160},{64,192},{96,224},{128,0},{160,32},{192,64},{224,... | collective-permute-start | bytes 221192 | tf_op jit(solution)/shard_map/ppermute | solution.py:292
  40.1 17.9 %all-to-all-start = ((bf16[4,208,768]{2,1,0:T(8,128)(2,1)}), bf16[4,208,768]{2,1,0:T(8,128)(2,1)S(1)}, u32[]{:S(2)}, u32[]{:S(2)}) async-start(bf16[4,208,768]{2,1,0:T(8,128)(2,1)} %broadcast_in_dim.40), calls=%async_computation | async-start | bytes 2555904 | tf_op jit(solution)/shard_map/all_to_all | solution.py:28
  43.6 17.3 %copy-start.11 = (s32[12,1]{0,1:T(1,128)S(1)}, s32[12,1]{0,1:T(1,128)}, u32[]{:S(2)}) copy-start(s32[12,1]{0,1:T(1,128)} %param.25) | copy-start | bytes 148
  43.7 5.5 %collective-permute-start.3 = (bf16[96,768]{1,0:T(8,128)(2,1)S(1)}, bf16[96,768]{1,0:T(8,128)(2,1)S(1)}, u32[]{:S(2)}, u32[]{:S(2)}) collective-permute-start(bf16[96,768]{1,0:T(8,128)(2,1)S(1)} %pad_maximum_fusion.4), channel_id=1, source_target_pairs={{0,8},{8,0},{16,24},{24,16},{1,9},{9,1},{17,25},{25,17},{2,10},{10... | collective-permute-start | bytes 442376 | tf_op jit(solution)/shard_map/ppermute | solution.py:292
  58.0 13.3 %copy-start.2 = (bf16[4,208,768]{2,1,0:T(8,128)(2,1)}, bf16[4,208,768]{2,1,0:T(8,128)(2,1)S(1)}, u32[]{:S(2)}) copy-start(bf16[4,208,768]{2,1,0:T(8,128)(2,1)S(1)} %all-to-all-done) | copy-start | bytes 3833860
  58.0 7.1 %collective-permute-start.8 = (bf16[192,768]{1,0:T(8,128)(2,1)S(1)}, bf16[192,768]{1,0:T(8,128)(2,1)S(1)}, u32[]{:S(2)}, u32[]{:S(2)}) collective-permute-start(bf16[192,768]{1,0:T(8,128)(2,1)S(1)} %pad_maximum_fusion.1), channel_id=1, source_target_pairs={{0,16},{8,24},{16,0},{24,8},{1,17},{9,25},{17,1},{25,9},{2,18},{10... | collective-permute-start | bytes 884744 | tf_op jit(solution)/shard_map/ppermute | solution.py:292
  66.0 7.1 %collective-permute-start.9 = (bf16[384,768]{1,0:T(8,128)(2,1)}, bf16[384,768]{1,0:T(8,128)(2,1)S(1)}, u32[]{:S(2)}, u32[]{:S(2)}) collective-permute-start(bf16[384,768]{1,0:T(8,128)(2,1)} %pad_maximum_fusion), channel_id=1, source_target_pairs={{0,4},{4,0},{1,5},{5,1},{2,6},{6,2},{3,7},{7,3},{8,12},{12,8},{9,1... | collective-permute-start | bytes 1769480 | tf_op jit(solution)/shard_map/ppermute | solution.py:292
  73.4 1.4 slice-start
  74.7 1.0 copy-start.4
  87.4 5.2 %copy-start.15 = (s32[25]{0:T(128)S(1)}, s32[25]{0:T(128)}, u32[]{:S(2)}) copy-start(s32[25]{0:T(128)} %param.29) | copy-start | bytes 304
  87.4 20.0 %all-to-all-start.1 = ((bf16[4,192,768]{2,1,0:T(8,128)(2,1)}), bf16[4,192,768]{2,1,0:T(8,128)(2,1)S(1)}, u32[]{:S(2)}, u32[]{:S(2)}) async-start(bf16[4,192,768]{2,1,0:T(8,128)(2,1)} %bitcast.163), calls=%async_computation.1 | async-start | bytes 2359296 | tf_op jit(solution)/shard_map/all_to_all | solution.py:45
  107.4 17.1 %all-to-all-start.2 = ((bf16[64,2,128]{2,1,0:T(2,128)(2,1)}), bf16[64,2,128]{2,1,0:T(2,128)(2,1)S(1)}, u32[]{:S(2)}, u32[]{:S(2)}) async-start(bf16[64,2,128]{2,1,0:T(2,128)(2,1)} %copy.183), calls=%async_computation.2 | async-start | bytes 65536 | tf_op jit(solution)/shard_map/all_to_all | solution.py:313
  114.9 10.8 %copy-start.1 = (f32[5,768]{1,0:T(8,128)S(1)}, f32[5,768]{1,0:T(8,128)}, u32[]{:S(2)}) copy-start(f32[5,768]{1,0:T(8,128)} %gain_ref.3) | copy-start | bytes 46084
  133.7 5.7 %collective-permute-start.10 = (bf16[8,768]{1,0:T(8,128)(2,1)S(1)}, bf16[8,768]{1,0:T(8,128)(2,1)S(1)}, u32[]{:S(2)}, u32[]{:S(2)}) collective-permute-start(bf16[8,768]{1,0:T(8,128)(2,1)S(1)} %trunk_rows.1), channel_id=1, source_target_pairs={{0,2},{1,3},{2,0},{3,1},{4,6},{5,7},{6,4},{7,5},{8,10},{9,11},{10,... | collective-permute-start | bytes 36872 | tf_op jit(solution)/shard_map/ppermute | solution.py:32
  136.7 2.7 %collective-permute-start.11 = (bf16[8,768]{1,0:T(8,128)(2,1)S(1)}, bf16[8,768]{1,0:T(8,128)(2,1)S(1)}, u32[]{:S(2)}, u32[]{:S(2)}) collective-permute-start(bf16[8,768]{1,0:T(8,128)(2,1)S(1)} %trunk_rows.1), channel_id=1, source_target_pairs={{0,1},{1,0},{2,3},{3,2},{4,5},{5,4},{6,7},{7,6},{8,9},{9,8},{10,11... | collective-permute-start | bytes 36872 | tf_op jit(solution)/shard_map/ppermute | solution.py:32
  137.0 3.8 %collective-permute-start.12 = (bf16[8,768]{1,0:T(8,128)(2,1)S(1)}, bf16[8,768]{1,0:T(8,128)(2,1)S(1)}, u32[]{:S(2)}, u32[]{:S(2)}) collective-permute-start(bf16[8,768]{1,0:T(8,128)(2,1)S(1)} %trunk_rows.1), channel_id=1, source_target_pairs={{0,3},{1,2},{2,1},{3,0},{4,7},{5,6},{6,5},{7,4},{8,11},{9,10},{10,... | collective-permute-start | bytes 36872 | tf_op jit(solution)/shard_map/ppermute | solution.py:32
  140.8 4.7 %copy-start.5 = (bf16[1,56,256]{2,1,0:T(8,128)(2,1)S(1)}, bf16[1,56,256]{2,1,0:T(8,128)(2,1)}, u32[]{:S(2)}) copy-start(bf16[1,56,256]{2,1,0:T(8,128)(2,1)} %param.31) | copy-start | bytes 86020
  142.3 4.7 %collective-permute-start.13 = (bf16[32,768]{1,0:T(8,128)(2,1)}, bf16[32,768]{1,0:T(8,128)(2,1)S(1)}, u32[]{:S(2)}, u32[]{:S(2)}) collective-permute-start(bf16[32,768]{1,0:T(8,128)(2,1)} %readout_mlp.1), channel_id=1, source_target_pairs={{0,2},{1,3},{2,0},{3,1},{4,6},{5,7},{6,4},{7,5},{8,10},{9,11},{10,... | collective-permute-start | bytes 147464 | tf_op jit(solution)/shard_map/ppermute | solution.py:32
  143.3 3.6 %collective-permute-start.14 = (bf16[32,768]{1,0:T(8,128)(2,1)}, bf16[32,768]{1,0:T(8,128)(2,1)S(1)}, u32[]{:S(2)}, u32[]{:S(2)}) collective-permute-start(bf16[32,768]{1,0:T(8,128)(2,1)} %readout_mlp.1), channel_id=1, source_target_pairs={{0,1},{1,0},{2,3},{3,2},{4,5},{5,4},{6,7},{7,6},{8,9},{9,8},{10,11... | collective-permute-start | bytes 147464 | tf_op jit(solution)/shard_map/ppermute | solution.py:32
  143.7 4.4 %collective-permute-start.15 = (bf16[32,768]{1,0:T(8,128)(2,1)}, bf16[32,768]{1,0:T(8,128)(2,1)S(1)}, u32[]{:S(2)}, u32[]{:S(2)}) collective-permute-start(bf16[32,768]{1,0:T(8,128)(2,1)} %readout_mlp.1), channel_id=1, source_target_pairs={{0,3},{1,2},{2,1},{3,0},{4,7},{5,6},{6,5},{7,4},{8,11},{9,10},{10,... | collective-permute-start | bytes 147464 | tf_op jit(solution)/shard_map/ppermute | solution.py:32
  145.7 14.0 %copy-start.7 = (bf16[1,20,256]{2,1,0:T(8,128)(2,1)S(1)}, bf16[1,20,256]{2,1,0:T(8,128)(2,1)}, u32[]{:S(2)}) copy-start(bf16[1,20,256]{2,1,0:T(8,128)(2,1)} %param.32) | copy-start | bytes 30724
  149.5 22.1 %copy-start.13 = (bf16[1,256,256]{2,1,0:T(8,128)(2,1)S(1)}, bf16[1,256,256]{2,1,0:T(8,128)(2,1)}, u32[]{:S(2)}) copy-start(bf16[1,256,256]{2,1,0:T(8,128)(2,1)} %param.33) | copy-start | bytes 393220
  150.3 21.0 %all-to-all-start.3 = ((bf16[64,2,768]{2,1,0:T(2,128)(2,1)}), bf16[64,2,768]{2,1,0:T(2,128)(2,1)S(1)}, u32[]{:S(2)}, u32[]{:S(2)}) async-start(bf16[64,2,768]{2,1,0:T(2,128)(2,1)} %reshape.380), calls=%async_computation.3 | async-start | bytes 393216 | tf_op jit(solution)/shard_map/all_to_all | solution.py:326
  159.2 12.5 %copy-start.12 = (bf16[1,256,256]{2,1,0:T(8,128)(2,1)S(1)}, bf16[1,256,256]{2,1,0:T(8,128)(2,1)}, u32[]{:S(2)}) copy-start(bf16[1,256,256]{2,1,0:T(8,128)(2,1)} %param.34) | copy-start | bytes 393220
  171.6 0.8 copy-start.14
  174.4 16.6 %all-to-all-start.4 = ((bf16[64,2,768]{2,1,0:T(2,128)(2,1)}), bf16[64,2,768]{2,1,0:T(2,128)(2,1)S(1)}, u32[]{:S(2)}, u32[]{:S(2)}) async-start(bf16[64,2,768]{2,1,0:T(2,128)(2,1)} %reshape.382), calls=%async_computation.4 | async-start | bytes 393216 | tf_op jit(solution)/shard_map/all_to_all | solution.py:349
Sparse Core Ops, SparseCore 0:
  25.2 100.4 all-gather.1
